TPU v7x, 32 devices: a whole 2x2x4 slice. The times are simulated.
32 devices in a mesh: rep: 4 (over y, core), shard: 4 (over z), ctx: 2 (over x).
Axes of the slice: x: 2, y: 2, z: 4, core: 2. Of those that a mesh axis runs over, the one named last changes fastest.
Arguments:
- tokens: bfloat16 [16, 256, 1024], P(('rep', 'shard'), 'ctx'), may hold values from -6 to 6
- out_grad: bfloat16 [16, 256, 1024], P(('rep', 'shard'), 'ctx'), may hold values from -6 to 6
- positions: int32 [16, 256], P(('rep', 'shard'), 'ctx'), may hold values from 0 to 255, as said below
- stretch_order: int32 [4], replicated, may hold values from 0 to 3, as said below
- attn_gain: bfloat16 [1024], P(('shard', 'ctx')), may hold values from 0.099609375 to 1.8984375
- query_gain: bfloat16 [128], replicated, may hold values from 0.5 to 6
- key_norm_gain: bfloat16 [128], replicated, may hold values from 0.5 to 6
- query_weight: bfloat16 [1024, 2048], P(('shard', 'ctx')), may hold values from -0.1875 to 0.1875
- key_projection_matrix: bfloat16 [1024, 1024], P(('shard', 'ctx')), may hold values from -0.1875 to 0.1875
- value_projection_matrix: bfloat16 [1024, 1024], P(('shard', 'ctx')), may hold values from -0.1875 to 0.1875
- output_weight: bfloat16 [1024, 2048], P(('shard', 'ctx')), may hold values from -0.375 to 0.375
- ffn_gain: bfloat16 [1024], P(('shard', 'ctx')), may hold values from 0.099609375 to 1.8984375
- gate_weight: bfloat16 [1024, 3072], P(('shard', 'ctx')), may hold values from -0.1875 to 0.1875
- up_weight: bfloat16 [1024, 3072], P(('shard', 'ctx')), may hold values from -0.1875 to 0.1875
- down_weight: bfloat16 [1024, 3072], P(('shard', 'ctx')), may hold values from -0.109375 to 0.109375
Outputs:
- block_out: bfloat16 [16, 256, 1024], P(('rep', 'shard'), 'ctx')
- tokens_grad: float32 [16, 256, 1024], P(('rep', 'shard'), 'ctx')
- query_weight_grad: float32 [1024, 2048], P(('shard', 'ctx'))
- key_weight_grad: float32 [1024, 1024], P(('shard', 'ctx'))
- value_weight_grad: float32 [1024, 1024], P(('shard', 'ctx'))
- output_weight_grad: float32 [1024, 2048], P(('shard', 'ctx'))
- gate_weight_grad: float32 [1024, 3072], P(('shard', 'ctx'))
- up_weight_grad: float32 [1024, 3072], P(('shard', 'ctx'))
- down_weight_grad: float32 [1024, 3072], P(('shard', 'ctx'))
- attn_gain_grad: float32 [1024], P(('shard', 'ctx'))
- ffn_gain_grad: float32 [1024], P(('shard', 'ctx'))
- query_gain_grad: float32 [128], replicated
- key_gain_grad: float32 [128], replicated
Inputs may be any that keep to these rules, and one draw needn't show every extreme that they name: A permutation: stored block j of every sequence holds sequence block stretch_order[j], each block 64 tokens. In sequence order (see stretch_order) the positions of a sequence start at 0, rise by one from token to token and restart at 0 where a packed document starts; sequence 0 holds one document.
All inputs are finite; a program needn't handle non-finite values.
Results may differ from a plain program's by a relative error of at most 0.019.
The roundings to bfloat16 on the way count: a program that leaves them out, or rounds other values in their place, can miss the bound.
Values may be sent and summed in bfloat16 or wider, within the bound.
No kernel may reach another device: no remote copies, remote signals or barrier semaphores. Data moves between devices by JAX's collectives and lax.ppermute only.
A program may use at most 256 MiB of HBM per device.

v0:
```python
import math

import jax
import jax.numpy as jnp
from jax import lax
from jax.sharding import PartitionSpec as P

QUERY_HEADS = 16
KEY_VALUE_HEADS = 8
HEAD_SIZE = 128


EPSILON = 1e-06
ROPE_THETA = 1000000.0
NEGATIVE = -1e30


def plain_product(left_side, right_side):
    return jnp.dot(left_side, right_side, preferred_element_type=jnp.float32)


def dot_right(left_side, right_side):
    return lax.dot_general(
        left_side, right_side, (((1,), (1,)), ((), ())), preferred_element_type=jnp.float32
    )


def dot_left(left_side, right_side):
    return lax.dot_general(
        left_side, right_side, (((0,), (0,)), ((), ())), preferred_element_type=jnp.float32
    )


def rope_tables(positions, head_width):
    half_width = head_width // 2
    freq_steps = jnp.arange(half_width, dtype=jnp.float32)
    inverse = jnp.exp(freq_steps * (-2.0 * math.log(ROPE_THETA) / head_width))
    angles = positions.astype(jnp.float32)[..., None] * inverse
    return (jnp.cos(angles)[..., None, :], jnp.sin(angles)[..., None, :])


def apply_rotation(values, cosine_values, sine_values):
    half_width = values.shape[-1] // 2
    front_half = values[..., :half_width]
    back_half = values[..., half_width:]
    return jnp.concatenate(
        [
            front_half * cosine_values - back_half * sine_values,
            back_half * cosine_values + front_half * sine_values,
        ],
        axis=-1,
    )


def reverse_rotation(gradient, cosine_values, sine_values):
    half_width = gradient.shape[-1] // 2
    front_half = gradient[..., :half_width]
    back_half = gradient[..., half_width:]
    return jnp.concatenate(
        [
            front_half * cosine_values + back_half * sine_values,
            back_half * cosine_values - front_half * sine_values,
        ],
        axis=-1,
    )


def per_head_norm(values, gain_vector):
    inverse_rms = lax.rsqrt(jnp.mean(values * values, axis=-1, keepdims=True) + EPSILON)
    unit_vector = values * inverse_rms
    return (unit_vector * gain_vector.astype(jnp.float32), unit_vector, inverse_rms)


def per_head_norm_backward(gradient, unit_vector, inverse_rms, gain_vector):
    gain_grad = jnp.sum(gradient * unit_vector, axis=tuple(range(gradient.ndim - 1)))
    scaled = gradient * gain_vector.astype(jnp.float32)
    return (
        gain_grad,
        inverse_rms
        * (scaled - unit_vector * jnp.mean(scaled * unit_vector, axis=-1, keepdims=True)),
    )


def attention_scores(query_heads, key_heads, visible):
    scores = jnp.einsum(
        "sqgrd,skgd->sgrqk", query_heads, key_heads, preferred_element_type=jnp.float32
    ) * (1.0 / math.sqrt(HEAD_SIZE))
    return jnp.where(visible, scores, NEGATIVE)


def attend(query_rot, key_rotated, value_row_matrix, visible, group_length):
    sequence_batch, query_count = (query_rot.shape[0], query_rot.shape[1])
    key_count = key_rotated.shape[1]
    kv_heads = key_rotated.shape[2] // HEAD_SIZE
    query_heads = query_rot.reshape(sequence_batch, query_count, kv_heads, group_length, HEAD_SIZE)
    key_heads = key_rotated.reshape(sequence_batch, key_count, kv_heads, HEAD_SIZE)
    value_heads = value_row_matrix.reshape(sequence_batch, key_count, kv_heads, HEAD_SIZE)
    scores = attention_scores(query_heads, key_heads, visible)
    row_max = jnp.max(scores, axis=-1, keepdims=True)
    log_total = row_max + jnp.log(jnp.sum(jnp.exp(scores - row_max), axis=-1, keepdims=True))
    attention_probs = jnp.exp(scores - log_total).astype(jnp.bfloat16)
    attended = jnp.einsum(
        "sgrqk,skgd->sqgrd", attention_probs, value_heads, preferred_element_type=jnp.float32
    )
    return (
        attended.astype(jnp.bfloat16).reshape(
            sequence_batch, query_count, kv_heads * group_length * HEAD_SIZE
        ),
        log_total,
    )


def attend_back(
    query_rot,
    key_rotated,
    value_row_matrix,
    attended,
    attended_grad,
    log_total,
    visible,
    group_length,
):
    sequence_batch, query_count = (query_rot.shape[0], query_rot.shape[1])
    key_count = key_rotated.shape[1]
    kv_heads = key_rotated.shape[2] // HEAD_SIZE
    query_heads = query_rot.reshape(sequence_batch, query_count, kv_heads, group_length, HEAD_SIZE)
    key_heads = key_rotated.reshape(sequence_batch, key_count, kv_heads, HEAD_SIZE)
    value_heads = value_row_matrix.reshape(sequence_batch, key_count, kv_heads, HEAD_SIZE)
    scores = attention_scores(query_heads, key_heads, visible)
    prob_float = jnp.exp(scores - log_total)
    attention_probs = prob_float.astype(jnp.bfloat16)
    grad_heads = attended_grad.reshape(
        sequence_batch, query_count, kv_heads, group_length, HEAD_SIZE
    )
    output_heads = attended.reshape(sequence_batch, query_count, kv_heads, group_length, HEAD_SIZE)
    row_delta = jnp.einsum(
        "sqgrd,sqgrd->sgrq", grad_heads, output_heads, preferred_element_type=jnp.float32
    )
    value_gradient = jnp.einsum(
        "sgrqk,sqgrd->skgd", attention_probs, grad_heads, preferred_element_type=jnp.float32
    )
    prob_grad = jnp.einsum(
        "sqgrd,skgd->sgrqk", grad_heads, value_heads, preferred_element_type=jnp.float32
    )
    score_grad = (prob_float * (prob_grad - row_delta[..., None])).astype(jnp.bfloat16)
    scale_factor = 1.0 / math.sqrt(HEAD_SIZE)
    query_grad = (
        jnp.einsum("sgrqk,skgd->sqgrd", score_grad, key_heads, preferred_element_type=jnp.float32)
        * scale_factor
    )
    key_gradient = (
        jnp.einsum("sgrqk,sqgrd->skgd", score_grad, query_heads, preferred_element_type=jnp.float32)
        * scale_factor
    )
    return (
        query_grad.reshape(sequence_batch, query_count, kv_heads * group_length * HEAD_SIZE),
        key_gradient.reshape(sequence_batch, key_count, kv_heads * HEAD_SIZE),
        value_gradient.reshape(sequence_batch, key_count, kv_heads * HEAD_SIZE),
    )


def replica_total(gradient_rows):
    return lax.psum(gradient_rows.astype(jnp.bfloat16), "rep").astype(jnp.float32)


def per_device(
    tokens,
    out_grad,
    positions,
    stretch_order,
    attn_gain,
    query_gain,
    key_norm_gain,
    query_weight,
    key_projection_matrix,
    value_projection_matrix,
    output_weight,
    ffn_gain,
    gate_weight,
    up_weight,
    down_weight,
):
    sequence_batch, count_of_rows, model_width = (tokens.shape[0], tokens.shape[1], tokens.shape[2])
    total_rows = sequence_batch * count_of_rows
    block_rows = count_of_rows // 2
    grouped_heads = QUERY_HEADS // KEY_VALUE_HEADS
    query_width = QUERY_HEADS * HEAD_SIZE
    key_value_width = KEY_VALUE_HEADS * HEAD_SIZE
    hidden_width = gate_weight.shape[1]
    own_rows = model_width // lax.axis_size(("shard", "ctx"))
    context_place = lax.axis_index("ctx")
    own_blocks = lax.dynamic_slice_in_dim(stretch_order, 2 * context_place, 2)
    local_places = jnp.arange(count_of_rows, dtype=jnp.int32)
    query_index = (
        jnp.where(local_places < block_rows, own_blocks[0], own_blocks[1]) * block_rows
        + local_places % block_rows
    )
    key_places = jnp.arange(count_of_rows * lax.axis_size("ctx"), dtype=jnp.int32)
    block_match = (key_places // block_rows)[:, None] == jnp.arange(
        stretch_order.shape[0], dtype=jnp.int32
    )[None, :]
    key_index = (
        jnp.sum(jnp.where(block_match, stretch_order[None, :], 0), axis=1) * block_rows
        + key_places % block_rows
    )
    visible = key_index[None, :] <= query_index[:, None]
    flat_tokens = tokens.reshape(total_rows, model_width).astype(jnp.float32)
    inv_first = lax.rsqrt(jnp.mean(flat_tokens * flat_tokens, axis=1, keepdims=True) + EPSILON)
    unit_first = flat_tokens * inv_first
    full_gain, full_query, full_key, full_value = (
        lax.all_gather(attn_gain, ("shard", "ctx"), axis=0, tiled=True),
        lax.all_gather(query_weight, ("shard", "ctx"), axis=0, tiled=True),
        lax.all_gather(key_projection_matrix, ("shard", "ctx"), axis=0, tiled=True),
        lax.all_gather(value_projection_matrix, ("shard", "ctx"), axis=0, tiled=True),
    )
    first_normalized = (unit_first * full_gain.astype(jnp.float32)).astype(jnp.bfloat16)
    query = plain_product(first_normalized, full_query)
    key = plain_product(first_normalized, full_key)
    value_row_matrix = (
        plain_product(first_normalized, full_value)
        .astype(jnp.bfloat16)
        .reshape(sequence_batch, count_of_rows, key_value_width)
    )
    cosine_values, sine_values = rope_tables(positions, HEAD_SIZE)
    query_scaled, query_unit, query_inv = per_head_norm(
        query.reshape(sequence_batch, count_of_rows, QUERY_HEADS, HEAD_SIZE), query_gain
    )
    key_gain_scaled, key_normalized, key_inverse_norm = per_head_norm(
        key.reshape(sequence_batch, count_of_rows, KEY_VALUE_HEADS, HEAD_SIZE), key_norm_gain
    )
    query_rot = (
        apply_rotation(query_scaled, cosine_values, sine_values)
        .astype(jnp.bfloat16)
        .reshape(sequence_batch, count_of_rows, query_width)
    )
    key_rotated = (
        apply_rotation(key_gain_scaled, cosine_values, sine_values)
        .astype(jnp.bfloat16)
        .reshape(sequence_batch, count_of_rows, key_value_width)
    )
    all_keys, all_values = (
        lax.all_gather(key_rotated, "ctx", axis=1, tiled=True),
        lax.all_gather(value_row_matrix, "ctx", axis=1, tiled=True),
    )
    attended, log_total = attend(query_rot, all_keys, all_values, visible, grouped_heads)
    attended_flat = attended.reshape(total_rows, query_width)
    middle = flat_tokens + dot_right(
        attended_flat, lax.all_gather(output_weight, ("shard", "ctx"), axis=0, tiled=True)
    )
    inv_second = lax.rsqrt(jnp.mean(middle * middle, axis=1, keepdims=True) + EPSILON)
    unit_second = middle * inv_second
    full_ffn_gain, full_gate, full_up = (
        lax.all_gather(ffn_gain, ("shard", "ctx"), axis=0, tiled=True),
        lax.all_gather(gate_weight, ("shard", "ctx"), axis=0, tiled=True),
        lax.all_gather(up_weight, ("shard", "ctx"), axis=0, tiled=True),
    )
    normed_second = (unit_second * full_ffn_gain.astype(jnp.float32)).astype(jnp.bfloat16)
    gate_value = plain_product(normed_second, full_gate)
    up_value = plain_product(normed_second, full_up)
    sigmoid_gate = jax.nn.sigmoid(gate_value)
    activated = gate_value * sigmoid_gate
    hidden = (activated * up_value).astype(jnp.bfloat16)
    block_sum = middle + dot_right(
        hidden, lax.all_gather(down_weight, ("shard", "ctx"), axis=0, tiled=True)
    )
    block_out = block_sum.astype(jnp.bfloat16).reshape(sequence_batch, count_of_rows, model_width)
    grad_rows = out_grad.reshape(total_rows, model_width)
    full_down = lax.all_gather(down_weight, ("shard", "ctx"), axis=0, tiled=True)
    hidden_grad = plain_product(grad_rows, full_down)
    gate_grad = (
        hidden_grad * up_value * sigmoid_gate * (1.0 + gate_value * (1.0 - sigmoid_gate))
    ).astype(jnp.bfloat16)
    up_grad = (hidden_grad * activated).astype(jnp.bfloat16)
    back_ffn_gain, back_gate, back_up = (
        lax.all_gather(ffn_gain, ("shard", "ctx"), axis=0, tiled=True),
        lax.all_gather(gate_weight, ("shard", "ctx"), axis=0, tiled=True),
        lax.all_gather(up_weight, ("shard", "ctx"), axis=0, tiled=True),
    )
    normed_grad_second = dot_right(gate_grad, back_gate) + dot_right(up_grad, back_up)
    ffn_gain_part = jnp.sum(normed_grad_second * unit_second, axis=0)
    unit_grad_second = normed_grad_second * back_ffn_gain.astype(jnp.float32)
    middle_grad = grad_rows.astype(jnp.float32) + inv_second * (
        unit_grad_second
        - unit_second * jnp.mean(unit_grad_second * unit_second, axis=1, keepdims=True)
    )
    middle_grad_b = middle_grad.astype(jnp.bfloat16)
    full_output = lax.all_gather(output_weight, ("shard", "ctx"), axis=0, tiled=True)
    attended_grad = plain_product(middle_grad_b, full_output).astype(jnp.bfloat16)
    query_grad, key_grad_terms, value_grad_terms = attend_back(
        query_rot,
        all_keys,
        all_values,
        attended,
        attended_grad.reshape(sequence_batch, count_of_rows, query_width),
        log_total,
        visible,
        grouped_heads,
    )
    key_gradient, value_gradient = (
        lax.psum_scatter(
            key_grad_terms.astype(jnp.bfloat16), "ctx", scatter_dimension=1, tiled=True
        ).astype(jnp.float32),
        lax.psum_scatter(
            value_grad_terms.astype(jnp.bfloat16), "ctx", scatter_dimension=1, tiled=True
        ).astype(jnp.float32),
    )
    query_gain_part, query_pre = per_head_norm_backward(
        reverse_rotation(
            query_grad.reshape(sequence_batch, count_of_rows, QUERY_HEADS, HEAD_SIZE),
            cosine_values,
            sine_values,
        ),
        query_unit,
        query_inv,
        query_gain,
    )
    key_gain_part, key_projected = per_head_norm_backward(
        reverse_rotation(
            key_gradient.reshape(sequence_batch, count_of_rows, KEY_VALUE_HEADS, HEAD_SIZE),
            cosine_values,
            sine_values,
        ),
        key_normalized,
        key_inverse_norm,
        key_norm_gain,
    )
    query_grad_b = query_pre.reshape(total_rows, query_width).astype(jnp.bfloat16)
    key_gradient_second = key_projected.reshape(total_rows, key_value_width).astype(jnp.bfloat16)
    value_gradient_second = value_gradient.reshape(total_rows, key_value_width).astype(jnp.bfloat16)
    back_gain, back_query, back_key, back_value = (
        lax.all_gather(attn_gain, ("shard", "ctx"), axis=0, tiled=True),
        lax.all_gather(query_weight, ("shard", "ctx"), axis=0, tiled=True),
        lax.all_gather(key_projection_matrix, ("shard", "ctx"), axis=0, tiled=True),
        lax.all_gather(value_projection_matrix, ("shard", "ctx"), axis=0, tiled=True),
    )
    normed_grad_first = (
        dot_right(query_grad_b, back_query)
        + dot_right(key_gradient_second, back_key)
        + dot_right(value_gradient_second, back_value)
    )
    attn_gain_part = jnp.sum(normed_grad_first * unit_first, axis=0)
    unit_grad_first = normed_grad_first * back_gain.astype(jnp.float32)
    tokens_grad = middle_grad + inv_first * (
        unit_grad_first - unit_first * jnp.mean(unit_grad_first * unit_first, axis=1, keepdims=True)
    )
    normed_part = normed_second
    grad_part = grad_rows
    ffn_local = lax.psum_scatter(
        jnp.concatenate(
            [
                dot_left(normed_part, gate_grad),
                dot_left(normed_part, up_grad),
                dot_left(grad_part, hidden),
            ],
            axis=1,
        ),
        ("shard", "ctx"),
        scatter_dimension=0,
        tiled=True,
    )
    normed_part = first_normalized
    grad_part = middle_grad_b
    attn_local = lax.psum_scatter(
        jnp.concatenate(
            [
                dot_left(normed_part, query_grad_b),
                dot_left(normed_part, key_gradient_second),
                dot_left(normed_part, value_gradient_second),
                dot_left(grad_part, attended_flat),
            ],
            axis=1,
        ),
        ("shard", "ctx"),
        scatter_dimension=0,
        tiled=True,
    )
    joined = replica_total(jnp.concatenate([ffn_local, attn_local], axis=1))
    ffn_total = joined[:, : 3 * hidden_width]
    attn_total = joined[:, 3 * hidden_width :]
    gain_totals = lax.psum(
        (attn_gain_part, ffn_gain_part, query_gain_part, key_gain_part), ("rep", "shard", "ctx")
    )
    own_start = lax.axis_index(("shard", "ctx")) * own_rows
    attn_gain_grad = lax.dynamic_slice_in_dim(gain_totals[0], own_start, own_rows)
    ffn_gain_grad = lax.dynamic_slice_in_dim(gain_totals[1], own_start, own_rows)
    query_weight_grad = attn_total[:, :query_width]
    key_weight_grad = attn_total[:, query_width : query_width + key_value_width]
    value_weight_grad = attn_total[
        :, query_width + key_value_width : query_width + 2 * key_value_width
    ]
    output_weight_grad = attn_total[:, query_width + 2 * key_value_width :]
    gate_weight_grad = ffn_total[:, :hidden_width]
    up_weight_grad = ffn_total[:, hidden_width : 2 * hidden_width]
    down_weight_grad = ffn_total[:, 2 * hidden_width :]
    return (
        block_out,
        tokens_grad.reshape(sequence_batch, count_of_rows, model_width),
        query_weight_grad,
        key_weight_grad,
        value_weight_grad,
        output_weight_grad,
        gate_weight_grad,
        up_weight_grad,
        down_weight_grad,
        attn_gain_grad,
        ffn_gain_grad,
        gain_totals[2],
        gain_totals[3],
    )


def solution(mesh):
    in_specs = (
        P(("rep", "shard"), "ctx", None),
        P(("rep", "shard"), "ctx", None),
        P(("rep", "shard"), "ctx"),
        P(),
        P(("shard", "ctx")),
        P(),
        P(),
        P(("shard", "ctx"), None),
        P(("shard", "ctx"), None),
        P(("shard", "ctx"), None),
        P(("shard", "ctx"), None),
        P(("shard", "ctx")),
        P(("shard", "ctx"), None),
        P(("shard", "ctx"), None),
        P(("shard", "ctx"), None),
    )
    out_specs = (
        P(("rep", "shard"), "ctx", None),
        P(("rep", "shard"), "ctx", None),
        P(("shard", "ctx"), None),
        P(("shard", "ctx"), None),
        P(("shard", "ctx"), None),
        P(("shard", "ctx"), None),
        P(("shard", "ctx"), None),
        P(("shard", "ctx"), None),
        P(("shard", "ctx"), None),
        P(("shard", "ctx")),
        P(("shard", "ctx")),
        P(),
        P(),
    )
    return jax.shard_map(
        per_device, mesh=mesh, in_specs=in_specs, out_specs=out_specs, check_vma=False
    )
```

profile of v0, /device:TPU:0, one launch (start us, length us, event | category | flops | bytes accessed | tf_op | source)
XLA Modules:
  0.0 1761.2 jit_solution(3105430753535905351)
XLA Ops:
  12.1 22.4 %all-gather.1 = bf16[8,1,128]{2,1,0:T(2,128)(2,1)S(1)} all-gather(bf16[1,1,128]{2,1,0:T(2,128)(2,1)S(1)} %bitcast.337), channel_id=1, replica_groups=mesh['rep'=4,'shard'=4,'ctx'=2] {'shard','ctx'}, dimensions={0}, use_global_device_ids=true | all-gather | bytes 2304 | tf_op jit(solution)/shard_map/all_gather | solution.py:211
  34.5 16.6 all-gather.2
  55.6 6.8 all-gather.11.cloned.1.call-done
  64.4 7.2 all-gather
  72.5 39.7 %all-gather.13.cloned.1.call-done = bf16[1024,1024]{1,0:T(8,128)(2,1)} async-done(((bf16[128,1024]{1,0:T(8,128)(2,1)}), bf16[1024,1024]{1,0:T(8,128)(2,1)}) %all-gather.13.cloned.1.call-update) | async-done | bytes 2097168 | tf_op jit(solution)/shard_map/all_gather | solution.py:213
  116.1 7.3 all_gather.46
  123.5 62.2 %all-gather.15.cloned.1.call-done = bf16[1024,2048]{1,0:T(8,128)(2,1)} async-done(((bf16[128,2048]{1,0:T(8,128)(2,1)}), bf16[1024,2048]{1,0:T(8,128)(2,1)}) %all-gather.15.cloned.1.call-update) | async-done | bytes 4194320 | tf_op jit(solution)/shard_map/all_gather | solution.py:212
  194.4 64.5 %all-gather.17.cloned.1.call-done = bf16[1024,2048]{1,0:T(8,128)(2,1)} async-done(((bf16[128,2048]{1,0:T(8,128)(2,1)}), bf16[1024,2048]{1,0:T(8,128)(2,1)}) %all-gather.17.cloned.1.call-update) | async-done | bytes 4194320 | tf_op jit(solution)/shard_map/all_gather | solution.py:248
  264.5 93.7 %all-gather.21.cloned.1.call-done = bf16[1024,3072]{1,0:T(8,128)(2,1)} async-done(((bf16[128,3072]{1,0:T(8,128)(2,1)}), bf16[1024,3072]{1,0:T(8,128)(2,1)}) %all-gather.21.cloned.1.call-update) | async-done | bytes 6291472 | tf_op jit(solution)/shard_map/all_gather | solution.py:255
  358.3 5.0 fusion.82
  363.3 93.9 %all-gather.19.cloned.1.call-done = bf16[1024,3072]{1,0:T(8,128)(2,1)} async-done(((bf16[128,3072]{1,0:T(8,128)(2,1)}), bf16[1024,3072]{1,0:T(8,128)(2,1)}) %all-gather.19.cloned.1.call-update) | async-done | bytes 6291472 | tf_op jit(solution)/shard_map/all_gather | solution.py:254
  462.2 94.1 %all-gather.23.cloned.1.call-done = bf16[1024,3072]{1,0:T(8,128)(2,1)} async-done(((bf16[128,3072]{1,0:T(8,128)(2,1)}), bf16[1024,3072]{1,0:T(8,128)(2,1)}) %all-gather.23.cloned.1.call-update) | async-done | bytes 6291472 | tf_op jit(solution)/shard_map/all_gather | solution.py:264
  556.3 6.5 multiply_convert_fusion
  565.1 5.9 multiply_reduce_fusion.2
  639.8 13.1 pad_maximum_fusion.1
  654.2 6.8 fusion.86
  661.0 6.3 fusion.85
  667.3 6.4 convolution_bitcast_fusion
  673.8 26.1 %pad_maximum_fusion = f32[1024,9216]{1,0:T(8,128)} fusion(f32[1024,3072]{1,0:T(8,128)} %convolution_bitcast_fusion, f32[1024,3072]{1,0:T(8,128)} %fusion.86, f32[1024,3072]{1,0:T(8,128)} %fusion.85), kind=kLoop, calls=%fused_computation | loop fusion | flops 18874368 | bytes 75497472 | tf_op jit(solution)/shard_map/concatenate | solution.py:349
  700.6 355.8 %reduce-scatter.11.cloned.1.call-done = f32[128,6144]{1,0:T(8,128)} async-done(((f32[1024,6144]{1,0:T(8,128)}), f32[128,6144]{1,0:T(8,128)}) %reduce-scatter.11.cloned.1.call-update) | async-done | bytes 3145744 | tf_op jit(solution)/shard_map/reduce_scatter | solution.py:363
  1059.5 600.7 %reduce-scatter.9.cloned.1.call-done = f32[128,9216]{1,0:T(8,128)} async-done(((f32[1024,9216]{1,0:T(8,128)}), f32[128,9216]{1,0:T(8,128)}) %reduce-scatter.9.cloned.1.call-update) | async-done | bytes 4718608 | tf_op jit(solution)/shard_map/reduce_scatter | solution.py:348
  1666.3 5.8 fusion.10
  1676.0 40.2 %all-reduce = (f32[1024]{0:T(1024)S(1)}, f32[1024]{0:T(1024)S(1)}, f32[128]{0:T(128)}, f32[128]{0:T(128)}) all-reduce(f32[1024]{0:T(1024)S(1)} %get-tuple-element.15, f32[1024]{0:T(1024)S(1)} %copy-done.50, f32[128]{0:T(128)S(1)} %bitcast_reduce_fusion, ...), channel_id=1, replica_groups=mesh['rep'=4,'shard'=4,'ctx'=2] {'rep','shard','ctx'}, use_global_device_ids=true, to_apply=%region_17.18 | all-reduce | flops 2304 | bytes 18432 | tf_op jit(solution)/shard_map/psum | solution.py:380
  1718.5 28.3 %all-reduce.3.cloned.1.call-done = bf16[128,15360]{1,0:T(8,128)(2,1)} async-done(((bf16[128,15360]{1,0:T(8,128)(2,1)}), bf16[128,15360]{1,0:T(8,128)(2,1)}) %all-reduce.3.cloned.1.call-update) | async-done | bytes 3932176 | tf_op jit(solution)/shard_map/psum | solution.py:163
  (261 shorter events, 130.4 us)
Async XLA Ops:
  7.2 27.3 %copy-start.59 = (bf16[128]{0:T(256)(128)(2,1)S(1)}, bf16[128]{0:T(256)(128)(2,1)}, u32[]{:S(2)}) copy-start(bf16[128]{0:T(256)(128)(2,1)} %param.26) | copy-start | bytes 772
  7.2 43.9 %copy-start.60 = (s32[4]{0:T(128)S(1)}, s32[4]{0:T(128)}, u32[]{:S(2)}) copy-start(s32[4]{0:T(128)} %param.18) | copy-start | bytes 52
  7.2 45.9 %copy-start.2 = (bf16[1,128,1024]{2,1,0:T(8,128)(2,1)S(1)}, bf16[1,128,1024]{2,1,0:T(8,128)(2,1)}, u32[]{:S(2)}) copy-start(bf16[1,128,1024]{2,1,0:T(8,128)(2,1)} %param.15) | copy-start | bytes 786436
  7.2 46.1 %copy-start.63 = (s32[1,128]{1,0:T(1,128)S(1)}, s32[1,128]{1,0:T(1,128)}, u32[]{:S(2)}) copy-start(s32[1,128]{1,0:T(1,128)} %param.17) | copy-start | bytes 1540
  7.3 55.1 %all-gather.11.cloned.1.call-start = ((), (), s32[]{:S(2)}) async-start(), calls=%async_computation.4 | async-start | bytes 2359296 | tf_op jit(solution)/shard_map/all_gather | solution.py:214
  8.0 104.2 %all-gather.13.cloned.1.call-start = ((), (), s32[]{:S(2)}) async-start(), calls=%async_computation.5 | async-start | bytes 2359296 | tf_op jit(solution)/shard_map/all_gather | solution.py:213
  8.7 176.9 %all-gather.15.cloned.1.call-start = ((), (), s32[]{:S(2)}) async-start(), calls=%async_computation.6 | async-start | bytes 4718592 | tf_op jit(solution)/shard_map/all_gather | solution.py:212
  9.5 249.5 %all-gather.17.cloned.1.call-start = ((), (), s32[]{:S(2)}) async-start(), calls=%async_computation.7 | async-start | bytes 4718592 | tf_op jit(solution)/shard_map/all_gather | solution.py:248
  10.0 348.2 %all-gather.21.cloned.1.call-start = ((), (), s32[]{:S(2)}) async-start(), calls=%async_computation.9 | async-start | bytes 7077888 | tf_op jit(solution)/shard_map/all_gather | solution.py:255
  10.6 446.6 %all-gather.19.cloned.1.call-start = ((), (), s32[]{:S(2)}) async-start(), calls=%async_computation.8 | async-start | bytes 7077888 | tf_op jit(solution)/shard_map/all_gather | solution.py:254
  11.2 545.1 %all-gather.23.cloned.1.call-start = ((), (), s32[]{:S(2)}) async-start(), calls=%async_computation.10 | async-start | bytes 7077888 | tf_op jit(solution)/shard_map/all_gather | solution.py:264
  12.0 610.8 %reduce-scatter.15.cloned.1.call-start = ((), (), s32[]{:S(2)}) async-start(), calls=%async_computation.15 | async-start | bytes 786432
  12.0 177.5 %copy-start.54 = (f32[128]{0:T(128)}, f32[128]{0:T(128)S(1)}, u32[]{:S(2)}) copy-start(f32[128]{0:T(128)S(1)} %convert_element_type.163) | copy-start | bytes 1540
  12.1 102.5 %copy-start.52 = (f32[128]{0:T(128)}, f32[128]{0:T(128)S(1)}, u32[]{:S(2)}) copy-start(f32[128]{0:T(128)S(1)} %convert_element_type.160) | copy-start | bytes 1540
  53.3 132.3 %copy-start.46 = (f32[128]{0:T(128)}, f32[128]{0:T(128)S(1)}, u32[]{:S(2)}) copy-start(f32[128]{0:T(128)S(1)} %add_rsqrt_fusion.3) | copy-start | bytes 1540
  114.6 74.0 %copy-start.43 = (f32[128,8]{1,0:T(8,128)}, f32[128,8]{1,0:T(8,128)S(1)}, u32[]{:S(2)}) copy-start(f32[128,8]{1,0:T(8,128)S(1)} %add_rsqrt_fusion.1) | copy-start | bytes 12292
  588.5 9.3 copy-start.15
  597.7 30.4 %reduce-scatter.13.cloned.1.call-start = ((), (), s32[]{:S(2)}) async-start(), calls=%async_computation.14 | async-start | bytes 786432
  608.3 448.0 %reduce-scatter.11.cloned.1.call-start = ((), (), s32[]{:S(2)}) async-start(), calls=%async_computation.12 | async-start | bytes 28311552 | tf_op jit(solution)/shard_map/reduce_scatter | solution.py:363
  622.8 10.7 copy-start.17
  622.8 10.7 copy-start.44
  622.8 10.7 copy-start.53
  653.0 1007.3 %reduce-scatter.9.cloned.1.call-start = ((), (), s32[]{:S(2)}) async-start(), calls=%async_computation.11 | async-start | bytes 42467328 | tf_op jit(solution)/shard_map/reduce_scatter | solution.py:348
  699.9 1047.0 %all-reduce.3.cloned.1.call-start = ((), (), s32[]{:S(2)}) async-start(), calls=%async_computation.13 | async-start | bytes 7864320 | tf_op jit(solution)/shard_map/psum | solution.py:163
  (54 other events, 214.4 us)
Sparse Core Ops, SparseCore 0:
  10.2 52.1 all-gather.10
  64.5 47.6 all-gather.12
  114.3 71.3 all-gather.14
  187.6 71.3 all-gather.16
  261.0 97.2 all-gather.20
  360.3 96.8 all-gather.18
  459.4 96.8 all-gather.22
  597.9 12.8 reduce-scatter.14
  613.5 14.6 reduce-scatter.12
  653.1 403.1 reduce-scatter.10
  1060.2 600.0 reduce-scatter.8
  1665.4 81.3 all-reduce.2
where the time goes:
time: 1770 us; the launch traced here: 1760 us
  waiting for transfers between devices  1450 us (82%)
  blocking collectives  93.8 us (5%)
  matrix products  85.8 us (5%)
  other arithmetic  68.1 us (4%)
  local copies, waits for them, and re-layouts  49.5 us (3%)
    reduce_scatter x1, waiting for transfers between devices, per_device(): lax.psum_scatter(jnp.concatenate([dot_left(normed_part, gate_grad), dot_l...  601 us
    reduce_scatter x1, waiting for transfers between devices, per_device(): lax.psum_scatter(jnp.concatenate([dot_left(normed_part, query_grad_b), do...  356 us
    all_gather x1, waiting for transfers between devices, per_device(): lax.all_gather(down_weight, ('shard', 'ctx'), axis=0, tiled=True)  94.1 us
    all_gather x1, waiting for transfers between devices, per_device(): lax.all_gather(gate_weight, ('shard', 'ctx'), axis=0, tiled=True)  93.9 us
    all_gather x1, waiting for transfers between devices, per_device(): lax.all_gather(up_weight, ('shard', 'ctx'), axis=0, tiled=True)  93.7 us
    all_gather x1, waiting for transfers between devices, per_device(): lax.all_gather(output_weight, ('shard', 'ctx'), axis=0, tiled=True)  64.5 us
    all_gather x1, waiting for transfers between devices, per_device(): lax.all_gather(query_weight, ('shard', 'ctx'), axis=0, tiled=True)  62.2 us
    psum x1, blocking collectives, per_device(): lax.psum((attn_gain_part, ffn_gain_part, query_gain_part, key_gain_part),...  40.2 us
  transfers between devices with their start and end apart: 12, of which 11 were waited for; matrix products, arithmetic and copies ran while one was open for 7% of the time, Pallas kernels for 0%

commit v1 on v0

v1 whole, which is shorter than its diff:
```python
import math

import jax
import jax.numpy as jnp
from jax import lax
from jax.sharding import PartitionSpec as P

QUERY_HEADS = 16
KEY_VALUE_HEADS = 8
HEAD_SIZE = 128


EPSILON = 1e-06
ROPE_THETA = 1000000.0
NEGATIVE = -1e30


def plain_product(left_side, right_side):
    return jnp.dot(left_side, right_side, preferred_element_type=jnp.float32)


def dot_right(left_side, right_side):
    return lax.dot_general(
        left_side, right_side, (((1,), (1,)), ((), ())), preferred_element_type=jnp.float32
    )


def dot_left(left_side, right_side):
    return lax.dot_general(
        left_side, right_side, (((0,), (0,)), ((), ())), preferred_element_type=jnp.float32
    )


def rope_tables(positions, head_width):
    half_width = head_width // 2
    freq_steps = jnp.arange(half_width, dtype=jnp.float32)
    inverse = jnp.exp(freq_steps * (-2.0 * math.log(ROPE_THETA) / head_width))
    angles = positions.astype(jnp.float32)[..., None] * inverse
    return (jnp.cos(angles)[..., None, :], jnp.sin(angles)[..., None, :])


def apply_rotation(values, cosine_values, sine_values):
    half_width = values.shape[-1] // 2
    front_half = values[..., :half_width]
    back_half = values[..., half_width:]
    return jnp.concatenate(
        [
            front_half * cosine_values - back_half * sine_values,
            back_half * cosine_values + front_half * sine_values,
        ],
        axis=-1,
    )


def reverse_rotation(gradient, cosine_values, sine_values):
    half_width = gradient.shape[-1] // 2
    front_half = gradient[..., :half_width]
    back_half = gradient[..., half_width:]
    return jnp.concatenate(
        [
            front_half * cosine_values + back_half * sine_values,
            back_half * cosine_values - front_half * sine_values,
        ],
        axis=-1,
    )


def per_head_norm(values, gain_vector):
    inverse_rms = lax.rsqrt(jnp.mean(values * values, axis=-1, keepdims=True) + EPSILON)
    unit_vector = values * inverse_rms
    return (unit_vector * gain_vector.astype(jnp.float32), unit_vector, inverse_rms)


def per_head_norm_backward(gradient, unit_vector, inverse_rms, gain_vector):
    gain_grad = jnp.sum(gradient * unit_vector, axis=tuple(range(gradient.ndim - 1)))
    scaled = gradient * gain_vector.astype(jnp.float32)
    return (
        gain_grad,
        inverse_rms
        * (scaled - unit_vector * jnp.mean(scaled * unit_vector, axis=-1, keepdims=True)),
    )


def peer_of(index, step, size):
    if size & (size - 1) == 0:
        return index ^ step
    return (index + step) % size


def gather_blocks(value, axis_name):
    size = lax.axis_size(axis_name)
    blocks = [value]
    for step in range(1, size):
        pairs = [(peer_of(index, step, size), index) for index in range(size)]
        blocks.append(lax.ppermute(value, axis_name, pairs))
    return blocks


def scatter_sum(parts, axis_name):
    size = lax.axis_size(axis_name)
    total = parts[0]
    for step in range(1, size):
        pairs = [(index, peer_of(index, step, size)) for index in range(size)]
        moved = lax.ppermute(parts[step].astype(jnp.bfloat16), axis_name, pairs)
        total = total + moved.astype(jnp.float32)
    return total


def block_source(axis_name, step):
    return peer_of(lax.axis_index(axis_name), step, lax.axis_size(axis_name))


def split_rows(value, count):
    rows = value.shape[0] // count
    return [value[place * rows : (place + 1) * rows] for place in range(count)]


def column_slice(matrix, place, count):
    width = matrix.shape[1] // count
    return lax.dynamic_slice_in_dim(matrix, place * width, width, axis=1)


def masked_scores(query_heads, key_heads, visible):
    scores = jnp.einsum(
        "sqgrd,skgd->sgrqk", query_heads, key_heads, preferred_element_type=jnp.float32
    ) * (1.0 / math.sqrt(HEAD_SIZE))
    return jnp.where(visible, scores, NEGATIVE)


def attend(query_heads, key_heads, value_heads, visible):
    scores = masked_scores(query_heads, key_heads, visible)
    row_max = jnp.max(scores, axis=-1, keepdims=True)
    log_total = row_max + jnp.log(jnp.sum(jnp.exp(scores - row_max), axis=-1, keepdims=True))
    attention_probs = jnp.exp(scores - log_total).astype(jnp.bfloat16)
    attended = jnp.einsum(
        "sgrqk,skgd->sqgrd", attention_probs, value_heads, preferred_element_type=jnp.float32
    ).astype(jnp.bfloat16)
    return (attended, log_total)


def attend_back(query_heads, key_heads, value_heads, attended, attended_grad, log_total, visible):
    scores = masked_scores(query_heads, key_heads, visible)
    prob_float = jnp.exp(scores - log_total)
    attention_probs = prob_float.astype(jnp.bfloat16)
    row_delta = jnp.einsum(
        "sqgrd,sqgrd->sgrq", attended_grad, attended, preferred_element_type=jnp.float32
    )
    value_gradient = jnp.einsum(
        "sgrqk,sqgrd->skgd", attention_probs, attended_grad, preferred_element_type=jnp.float32
    )
    prob_grad = jnp.einsum(
        "sqgrd,skgd->sgrqk", attended_grad, value_heads, preferred_element_type=jnp.float32
    )
    score_grad = (prob_float * (prob_grad - row_delta[..., None])).astype(jnp.bfloat16)
    scale_factor = 1.0 / math.sqrt(HEAD_SIZE)
    query_grad = (
        jnp.einsum("sgrqk,skgd->sqgrd", score_grad, key_heads, preferred_element_type=jnp.float32)
        * scale_factor
    )
    key_gradient = (
        jnp.einsum("sgrqk,sqgrd->skgd", score_grad, query_heads, preferred_element_type=jnp.float32)
        * scale_factor
    )
    return (query_grad, key_gradient, value_gradient)


def per_device(
    tokens,
    out_grad,
    positions,
    stretch_order,
    attn_gain,
    query_gain,
    key_norm_gain,
    query_weight,
    key_projection_matrix,
    value_projection_matrix,
    output_weight,
    ffn_gain,
    gate_weight,
    up_weight,
    down_weight,
):
    owners = ("shard", "ctx")
    sequence_batch, count_of_rows, model_width = tokens.shape
    local_rows = sequence_batch * count_of_rows
    members = lax.axis_size("rep")
    own_member = lax.axis_index("rep")
    ctx_size = lax.axis_size("ctx")
    sequences = members * sequence_batch
    total_rows = members * local_rows
    query_heads_here = QUERY_HEADS // members
    kv_heads_here = KEY_VALUE_HEADS // members
    grouped_heads = QUERY_HEADS // KEY_VALUE_HEADS
    query_width = query_heads_here * HEAD_SIZE
    kv_width = kv_heads_here * HEAD_SIZE
    hidden_width = gate_weight.shape[1] // members
    own_rows = model_width // lax.axis_size(owners)
    own_start = lax.axis_index(owners) * own_rows

    def part(matrix):
        return column_slice(matrix, own_member, members)

    full_qkv = lax.all_gather(
        jnp.concatenate(
            [part(query_weight), part(key_projection_matrix), part(value_projection_matrix)],
            axis=1,
        ),
        owners,
        axis=0,
        tiled=True,
    )
    full_output = lax.all_gather(part(output_weight), owners, axis=0, tiled=True)
    full_gate_up = lax.all_gather(
        jnp.concatenate([part(gate_weight), part(up_weight)], axis=1), owners, axis=0, tiled=True
    )
    full_down = lax.all_gather(part(down_weight), owners, axis=0, tiled=True)
    gains = lax.all_gather(jnp.stack([attn_gain, ffn_gain]), owners, axis=1, tiled=True).astype(
        jnp.float32
    )
    full_gain = gains[0][None, :]
    full_ffn_gain = gains[1][None, :]

    own_tokens = tokens.reshape(local_rows, model_width)
    own_grads = out_grad.reshape(local_rows, model_width)
    all_tokens = jnp.concatenate(gather_blocks(own_tokens, "rep"), axis=0)
    all_grads = jnp.concatenate(gather_blocks(own_grads, "rep"), axis=0)
    all_positions = jnp.concatenate(gather_blocks(positions, "rep"), axis=0)
    cosine_values, sine_values = rope_tables(all_positions, HEAD_SIZE)

    block_count = stretch_order.shape[0]
    stretches_here = block_count // ctx_size
    block_rows = count_of_rows // stretches_here

    def stored_index(place):
        blocks = lax.dynamic_slice_in_dim(stretch_order, place * stretches_here, stretches_here)
        local = jnp.arange(count_of_rows, dtype=jnp.int32)
        match = (local // block_rows)[:, None] == jnp.arange(stretches_here, dtype=jnp.int32)[None]
        return (
            jnp.sum(jnp.where(match, blocks[None, :], 0), axis=1) * block_rows + local % block_rows
        )

    key_index = jnp.concatenate([stored_index(block_source("ctx", step)) for step in range(ctx_size)])
    query_index = key_index[:count_of_rows]
    visible = key_index[None, :] <= query_index[:, None]

    float_tokens = all_tokens.astype(jnp.float32)
    inv_first_all = lax.rsqrt(
        jnp.mean(float_tokens * float_tokens, axis=1, keepdims=True) + EPSILON
    )
    first_normalized = (float_tokens * inv_first_all * full_gain).astype(jnp.bfloat16)
    flat_tokens = own_tokens.astype(jnp.float32)
    inv_first = inv_first_all[:local_rows]
    unit_first = flat_tokens * inv_first
    projected = plain_product(first_normalized, full_qkv)
    query = projected[:, :query_width]
    key = projected[:, query_width : query_width + kv_width]
    value_rows = projected[:, query_width + kv_width :].astype(jnp.bfloat16)
    query_scaled, query_unit, query_inv = per_head_norm(
        query.reshape(sequences, count_of_rows, query_heads_here, HEAD_SIZE), query_gain
    )
    key_scaled, key_unit, key_inv = per_head_norm(
        key.reshape(sequences, count_of_rows, kv_heads_here, HEAD_SIZE), key_norm_gain
    )
    query_heads = (
        apply_rotation(query_scaled, cosine_values, sine_values)
        .astype(jnp.bfloat16)
        .reshape(sequences, count_of_rows, kv_heads_here, grouped_heads, HEAD_SIZE)
    )
    key_rot = (
        apply_rotation(key_scaled, cosine_values, sine_values)
        .astype(jnp.bfloat16)
        .reshape(sequences, count_of_rows, kv_heads_here, HEAD_SIZE)
    )
    key_value = jnp.stack(
        [key_rot, value_rows.reshape(sequences, count_of_rows, kv_heads_here, HEAD_SIZE)]
    )
    all_key_value = jnp.concatenate(gather_blocks(key_value, "ctx"), axis=2)
    key_heads = all_key_value[0]
    value_heads = all_key_value[1]
    attended, log_total = attend(query_heads, key_heads, value_heads, visible)
    attended_flat = attended.reshape(total_rows, query_width)
    middle = flat_tokens + scatter_sum(
        split_rows(dot_right(attended_flat, full_output), members), "rep"
    )
    inv_second = lax.rsqrt(jnp.mean(middle * middle, axis=1, keepdims=True) + EPSILON)
    unit_second = middle * inv_second
    normed_own = (unit_second * full_ffn_gain).astype(jnp.bfloat16)
    normed_second = jnp.concatenate(gather_blocks(normed_own, "rep"), axis=0)
    gate_up = plain_product(normed_second, full_gate_up)
    gate_value = gate_up[:, :hidden_width]
    up_value = gate_up[:, hidden_width:]
    sigmoid_gate = jax.nn.sigmoid(gate_value)
    activated = gate_value * sigmoid_gate
    hidden = (activated * up_value).astype(jnp.bfloat16)
    hidden_grad = plain_product(all_grads, full_down)
    gate_grad = (
        hidden_grad * up_value * sigmoid_gate * (1.0 + gate_value * (1.0 - sigmoid_gate))
    ).astype(jnp.bfloat16)
    up_grad = (hidden_grad * activated).astype(jnp.bfloat16)
    gate_up_grad = jnp.concatenate([gate_grad, up_grad], axis=1)
    normed_grad_second = scatter_sum(
        split_rows(dot_right(gate_up_grad, full_gate_up), members), "rep"
    )
    block_sum = middle + scatter_sum(split_rows(dot_right(hidden, full_down), members), "rep")
    block_out = block_sum.astype(jnp.bfloat16).reshape(sequence_batch, count_of_rows, model_width)

    def owner_rows(left_sides, right_sides):
        columns = [
            dot_left(left_side, right_side).astype(jnp.bfloat16)
            for left_side, right_side in zip(left_sides, right_sides)
        ]
        return lax.psum_scatter(
            jnp.concatenate(columns, axis=1), owners, scatter_dimension=0, tiled=True
        )

    ffn_rows = owner_rows([normed_second, all_grads], [gate_up_grad, hidden])
    ffn_gain_part = jnp.sum(normed_grad_second * unit_second, axis=0)
    unit_grad_second = normed_grad_second * full_ffn_gain
    middle_grad = own_grads.astype(jnp.float32) + inv_second * (
        unit_grad_second
        - unit_second * jnp.mean(unit_grad_second * unit_second, axis=1, keepdims=True)
    )
    middle_grad_b = jnp.concatenate(
        gather_blocks(middle_grad.astype(jnp.bfloat16), "rep"), axis=0
    )
    attended_grad = (
        plain_product(middle_grad_b, full_output).astype(jnp.bfloat16).reshape(attended.shape)
    )
    query_rot_grad, key_terms, value_terms = attend_back(
        query_heads, key_heads, value_heads, attended, attended_grad, log_total, visible
    )
    own_terms = jnp.stack([key_terms, value_terms])
    key_value_grad = scatter_sum(
        [
            own_terms[:, :, place * count_of_rows : (place + 1) * count_of_rows]
            for place in range(ctx_size)
        ],
        "ctx",
    )
    query_gain_part, query_pre = per_head_norm_backward(
        reverse_rotation(
            query_rot_grad.reshape(sequences, count_of_rows, query_heads_here, HEAD_SIZE),
            cosine_values,
            sine_values,
        ),
        query_unit,
        query_inv,
        query_gain,
    )
    key_gain_part, key_pre = per_head_norm_backward(
        reverse_rotation(key_value_grad[0], cosine_values, sine_values),
        key_unit,
        key_inv,
        key_norm_gain,
    )
    projected_grad = jnp.concatenate(
        [
            query_pre.reshape(total_rows, query_width).astype(jnp.bfloat16),
            key_pre.reshape(total_rows, kv_width).astype(jnp.bfloat16),
            key_value_grad[1].reshape(total_rows, kv_width).astype(jnp.bfloat16),
        ],
        axis=1,
    )
    attn_rows = owner_rows([first_normalized, middle_grad_b], [projected_grad, attended_flat])
    normed_grad_first = scatter_sum(
        split_rows(dot_right(projected_grad, full_qkv), members), "rep"
    )
    attn_gain_part = jnp.sum(normed_grad_first * unit_first, axis=0)
    unit_grad_first = normed_grad_first * full_gain
    tokens_grad = middle_grad + inv_first * (
        unit_grad_first - unit_first * jnp.mean(unit_grad_first * unit_first, axis=1, keepdims=True)
    )
    gain_totals = lax.psum(
        (attn_gain_part, ffn_gain_part, query_gain_part, key_gain_part), ("rep",) + owners
    )
    attn_gain_grad = lax.dynamic_slice_in_dim(gain_totals[0], own_start, own_rows)
    ffn_gain_grad = lax.dynamic_slice_in_dim(gain_totals[1], own_start, own_rows)

    ffn_all = lax.all_gather(ffn_rows, "rep", axis=0)
    attn_all = lax.all_gather(attn_rows, "rep", axis=0)

    def whole(pieces, start, width):
        return jnp.concatenate(
            [pieces[place, :, start : start + width] for place in range(members)], axis=1
        ).astype(jnp.float32)

    return (
        block_out,
        tokens_grad.reshape(sequence_batch, count_of_rows, model_width),
        whole(attn_all, 0, query_width),
        whole(attn_all, query_width, kv_width),
        whole(attn_all, query_width + kv_width, kv_width),
        whole(attn_all, query_width + 2 * kv_width, query_width),
        whole(ffn_all, 0, hidden_width),
        whole(ffn_all, hidden_width, hidden_width),
        whole(ffn_all, 2 * hidden_width, hidden_width),
        attn_gain_grad,
        ffn_gain_grad,
        gain_totals[2],
        gain_totals[3],
    )


def solution(mesh):
    in_specs = (
        P(("rep", "shard"), "ctx", None),
        P(("rep", "shard"), "ctx", None),
        P(("rep", "shard"), "ctx"),
        P(),
        P(("shard", "ctx")),
        P(),
        P(),
        P(("shard", "ctx"), None),
        P(("shard", "ctx"), None),
        P(("shard", "ctx"), None),
        P(("shard", "ctx"), None),
        P(("shard", "ctx")),
        P(("shard", "ctx"), None),
        P(("shard", "ctx"), None),
        P(("shard", "ctx"), None),
    )
    out_specs = (
        P(("rep", "shard"), "ctx", None),
        P(("rep", "shard"), "ctx", None),
        P(("shard", "ctx"), None),
        P(("shard", "ctx"), None),
        P(("shard", "ctx"), None),
        P(("shard", "ctx"), None),
        P(("shard", "ctx"), None),
        P(("shard", "ctx"), None),
        P(("shard", "ctx"), None),
        P(("shard", "ctx")),
        P(("shard", "ctx")),
        P(),
        P(),
    )
    return jax.shard_map(
        per_device, mesh=mesh, in_specs=in_specs, out_specs=out_specs, check_vma=False
    )
```

time: 1770 us -> 567 us (0.32)
  waiting for transfers between devices: 1450 us -> 341 us
  matrix products: 85.8 us -> 37.2 us
  other arithmetic: 68.1 us -> 33.4 us
  blocking collectives: 93.8 us -> 64.8 us
  starting transfers between devices: 1.05 us -> 20.9 us
    reduce_scatter x2 -> x1, waiting for transfers between devices: 956 us -> 96.3 us  [owner_rows(): lax.psum_scatter(jnp.concatenate(columns, axis=1), owners, scatter_dimens...]
    all_gather x7 -> x6, waiting for transfers between devices: 455 us -> 95.9 us  [the longest x1 39.8 us: per_device(): full_down = lax.all_gather(part(down_weight), owners, axis=0, tiled=True)]
    ppermute x0 -> x29, waiting for transfers between devices: none -> 84.7 us  [the longest x13 47.3 us: scatter_sum(): moved = lax.ppermute(parts[step].astype(jnp.bfloat16), axis_name, pairs)]
    unnamed x14 -> x9, waiting for transfers between devices: 8.11 us -> 63.8 us
    concatenate x3 -> x6, other arithmetic: 41.3 us -> 5.56 us  [the longest x2 2.81 us: owner_rows(): jnp.concatenate(columns, axis=1)]
    all_gather x4 -> x1, blocking collectives: 53.5 us -> 20.8 us  [per_device(): lax.all_gather(jnp.stack([attn_gain, ffn_gain]), owners, axis=1, tiled=True)]
    psum x1 -> x0, waiting for transfers between devices: 28.3 us -> none  [replica_total(): lax.psum(gradient_rows.astype(jnp.bfloat16), 'rep').astype(jnp.float32)]
    dot_general x7 -> x4, matrix products: 32.6 us -> 8.15 us  [dot_left(): lax.dot_general(left_side, right_side, (((0,), (0,)), ((), ())), preferre...]
  transfers between devices with their start and end apart: 12 -> 37, of which waited for: 11 -> 19; matrix products, arithmetic and copies ran while one was open for 7% -> 11% of each run, Pallas kernels for 0% -> 0%
where the time goes in v1:
time: 567 us; the launch traced here: 561 us
  waiting for transfers between devices  341 us (60%)
  blocking collectives  64.8 us (11%)
  local copies, waits for them, and re-layouts  48.3 us (9%)
  matrix products  37.2 us (7%)
  other arithmetic  33.4 us (6%)
  starting transfers between devices  20.9 us (4%)
  between operations  16.1 us (3%)
    reduce_scatter x1, waiting for transfers between devices, owner_rows(): lax.psum_scatter(jnp.concatenate(columns, axis=1), owners, scatter_dimens...  96.3 us
    unnamed x9, waiting for transfers between devices  63.8 us
    ppermute x13, waiting for transfers between devices, scatter_sum(): moved = lax.ppermute(parts[step].astype(jnp.bfloat16), axis_name, pairs)  47.3 us
    psum x1, blocking collectives, per_device(): lax.psum((attn_gain_part, ffn_gain_part, query_gain_part, key_gain_part),...  44 us
    all_gather x1, waiting for transfers between devices, per_device(): full_down = lax.all_gather(part(down_weight), owners, axis=0, tiled=True)  39.8 us
    ppermute x16, waiting for transfers between devices, gather_blocks(): blocks.append(lax.ppermute(value, axis_name, pairs))  37.4 us
    all_gather x1, waiting for transfers between devices, per_device(): lax.all_gather(jnp.concatenate([part(gate_weight), part(up_weight)], axis...  29.6 us
    all_gather x1, blocking collectives, per_device(): lax.all_gather(jnp.stack([attn_gain, ffn_gain]), owners, axis=1, tiled=True)  20.8 us
  transfers between devices with their start and end apart: 37, of which 19 were waited for; matrix products, arithmetic and copies ran while one was open for 11% of the time, Pallas kernels for 0%

profile of v1, /device:TPU:0, one launch (start us, length us, event | category | flops | bytes accessed | tf_op | source)
XLA Modules:
  0.0 561.3 jit_solution(4459717981588676727)
XLA Ops:
  19.4 20.8 %all_gather.27 = bf16[2,1024]{1,0:T(2,128)(2,1)S(1)} all-gather(bf16[2,128]{1,0:T(2,128)(2,1)S(1)} %pad_maximum_fusion.28), channel_id=1, replica_groups=mesh['rep'=4,'shard'=4,'ctx'=2] {'shard','ctx'}, dimensions={1}, use_global_device_ids=true | all-gather | bytes 4608 | tf_op jit(solution)/shard_map/all_gather | solution.py:218
  41.8 6.7 %collective-permute-done.2 = bf16[128,1024]{1,0:T(8,128)(2,1)S(1)} collective-permute-done((bf16[128,1024]{1,0:T(8,128)(2,1)S(1)}, bf16[128,1024]{1,0:T(8,128)(2,1)S(1)}, u32[]{:S(2)}, u32[]{:S(2)}) %collective-permute-start.2) | collective-permute-done | bytes 262176 | tf_op jit(solution)/shard_map/ppermute | solution.py:95
  48.8 13.8 %all-gather.9.cloned.1.call-done = bf16[1024,1024]{1,0:T(8,128)(2,1)} async-done(((bf16[128,1024]{1,0:T(8,128)(2,1)}), bf16[1024,1024]{1,0:T(8,128)(2,1)}) %all-gather.9.cloned.1.call-update) | async-done | bytes 2097168 | tf_op jit(solution)/shard_map/all_gather | solution.py:204
  62.6 3.1 fusion.43
  75.5 9.6 %collective-permute-done.6 = bf16[2,4,128,2,128]{4,2,3,1,0:T(8,128)(2,1)} collective-permute-done((bf16[2,4,128,2,128]{4,2,3,1,0:T(8,128)(2,1)S(1)}, bf16[2,4,128,2,128]{4,2,3,1,0:T(8,128)(2,1)}, u32[]{:S(2)}, u32[]{:S(2)}) %collective-permute-start.6) | collective-permute-done | bytes 524320 | tf_op jit(solution)/shard_map/ppermute | solution.py:95
  92.8 12.6 %all-gather.11.cloned.1.call-done = bf16[1024,512]{1,0:T(8,128)(2,1)} async-done(((bf16[128,512]{1,0:T(8,128)(2,1)}), bf16[1024,512]{1,0:T(8,128)(2,1)}) %all-gather.11.cloned.1.call-update) | async-done | bytes 1048592 | tf_op jit(solution)/shard_map/all_gather | solution.py:213
  109.6 7.4 %collective-permute-done.8 = bf16[128,1024]{1,0:T(8,128)(2,1)S(1)} collective-permute-done((bf16[128,1024]{1,0:T(8,128)(2,1)S(1)}, bf16[128,1024]{1,0:T(8,128)(2,1)S(1)}, u32[]{:S(2)}, u32[]{:S(2)}) %collective-permute-start.8) | collective-permute-done | bytes 262176 | tf_op jit(solution)/shard_map/ppermute | solution.py:104
  117.0 4.5 collective-permute-done.9
  127.2 5.5 collective-permute-done.11
  133.4 3.9 collective-permute-done.12
  137.3 29.6 %all-gather.13.cloned.1.call-done = bf16[1024,1536]{1,0:T(8,128)(2,1)} async-done(((bf16[128,1536]{1,0:T(8,128)(2,1)}), bf16[1024,1536]{1,0:T(8,128)(2,1)}) %all-gather.13.cloned.1.call-update) | async-done | bytes 3145744 | tf_op jit(solution)/shard_map/all_gather | solution.py:214
  166.9 5.7 %fusion.51 = f32[512,1536]{1,0:T(8,128)} fusion(bf16[1024,1536]{1,0:T(8,128)(2,1)} %all-gather.13.cloned.1.call-done, bf16[128,1024]{1,0:T(8,128)(2,1)} %collective-permute-done.12, bf16[128,1024]{1,0:T(8,128)(2,1)} %copy-done.64, bf16[128,1024]{1,0:T(8,128)(2,1)} %copy-done.62, bf16[128,1024]{1,0:T(8,128)(2,1)} %copy-done.52), kind=kOutput, calls=%fused_computation.148 | convolution fusion | flops 1614807040 | bytes 7340032 | tf_op jit(solution)/shard_map/dot_general | solution.py:19
  172.6 39.8 %all-gather.15.cloned.1.call-done = bf16[1024,768]{1,0:T(8,128)(2,1)} async-done(((bf16[128,768]{1,0:T(8,128)(2,1)}), bf16[1024,768]{1,0:T(8,128)(2,1)}) %all-gather.15.cloned.1.call-update) | async-done | bytes 1572880 | tf_op jit(solution)/shard_map/all_gather | solution.py:217
  212.4 5.1 multiply_convert_fusion.1
  221.4 7.4 %collective-permute-done.20 = bf16[128,1024]{1,0:T(8,128)(2,1)S(1)} collective-permute-done((bf16[128,1024]{1,0:T(8,128)(2,1)S(1)}, bf16[128,1024]{1,0:T(8,128)(2,1)S(1)}, u32[]{:S(2)}, u32[]{:S(2)}) %collective-permute-start.20) | collective-permute-done | bytes 262176 | tf_op jit(solution)/shard_map/ppermute | solution.py:104
  228.8 4.5 collective-permute-done.21
  236.9 7.7 %collective-permute-done.23 = bf16[128,1024]{1,0:T(8,128)(2,1)S(1)} collective-permute-done((bf16[128,1024]{1,0:T(8,128)(2,1)S(1)}, bf16[128,1024]{1,0:T(8,128)(2,1)S(1)}, u32[]{:S(2)}, u32[]{:S(2)}) %collective-permute-start.23) | collective-permute-done | bytes 262176 | tf_op jit(solution)/shard_map/ppermute | solution.py:95
  244.6 4.0 collective-permute-done.24
  280.6 5.8 %collective-permute-done.25 = bf16[2,4,128,2,128]{4,2,3,1,0:T(8,128)(2,1)S(1)} collective-permute-done((bf16[2,4,128,2,128]{4,2,3,1,0:T(8,128)(2,1)S(1)}, bf16[2,4,128,2,128]{4,2,3,1,0:T(8,128)(2,1)S(1)}, u32[]{:S(2)}, u32[]{:S(2)}) %collective-permute-start.25) | collective-permute-done | bytes 524320 | tf_op jit(solution)/shard_map/ppermute | solution.py:104
  305.4 63.7 %reduce-scatter.7.cloned.1.call-done = bf16[128,1536]{1,0:T(8,128)(2,1)} async-done(((bf16[1024,1536]{1,0:T(8,128)(2,1)}), bf16[128,1536]{1,0:T(8,128)(2,1)}) %reduce-scatter.7.cloned.1.call-update) | async-done | bytes 393232
  371.0 96.3 %reduce-scatter.5.cloned.1.call-done = bf16[128,2304]{1,0:T(8,128)(2,1)} async-done(((bf16[1024,2304]{1,0:T(8,128)(2,1)}), bf16[128,2304]{1,0:T(8,128)(2,1)}) %reduce-scatter.5.cloned.1.call-update) | async-done | bytes 589840 | tf_op jit(solution)/shard_map/reduce_scatter | solution.py:313
  476.2 6.6 %collective-permute-done.27 = bf16[128,1024]{1,0:T(8,128)(2,1)S(1)} collective-permute-done((bf16[128,1024]{1,0:T(8,128)(2,1)S(1)}, bf16[128,1024]{1,0:T(8,128)(2,1)S(1)}, u32[]{:S(2)}, u32[]{:S(2)}) %collective-permute-start.27) | collective-permute-done | bytes 262176 | tf_op jit(solution)/shard_map/ppermute | solution.py:104
  482.8 11.0 %collective-permute-done.28 = bf16[128,1024]{1,0:T(8,128)(2,1)S(1)} collective-permute-done((bf16[128,1024]{1,0:T(8,128)(2,1)S(1)}, bf16[128,1024]{1,0:T(8,128)(2,1)S(1)}, u32[]{:S(2)}, u32[]{:S(2)}) %collective-permute-start.28) | collective-permute-done | bytes 262176 | tf_op jit(solution)/shard_map/ppermute | solution.py:104
  494.8 44.0 %all-reduce = (f32[1024]{0:T(1024)S(1)}, f32[1024]{0:T(1024)S(1)}, f32[128]{0:T(128)}, f32[128]{0:T(128)}) all-reduce(f32[1024]{0:T(1024)S(1)} %get-tuple-element.15, f32[1024]{0:T(1024)S(1)} %get-tuple-element.13, f32[128]{0:T(128)S(1)} %bitcast_reduce_fusion, ...), channel_id=1, replica_groups=mesh['rep'=4,'shard'=4,'ctx'=2] {'rep','shard','ctx'}, use_global_device_ids=true, to_apply=%region_15.16 | all-reduce | flops 2304 | bytes 18432 | tf_op jit(solution)/shard_map/psum | solution.py:374
  (349 shorter events, 126.2 us)
Async XLA Ops:
  7.2 55.4 %all-gather.9.cloned.1.call-start = ((), (), s32[]{:S(2)}) async-start(), calls=%async_computation.2 | async-start | bytes 2359296 | tf_op jit(solution)/shard_map/all_gather | solution.py:204
  10.0 95.4 %all-gather.11.cloned.1.call-start = ((), (), s32[]{:S(2)}) async-start(), calls=%async_computation.3 | async-start | bytes 1179648 | tf_op jit(solution)/shard_map/all_gather | solution.py:213
  11.6 155.3 %all-gather.13.cloned.1.call-start = ((), (), s32[]{:S(2)}) async-start(), calls=%async_computation.4 | async-start | bytes 3538944 | tf_op jit(solution)/shard_map/all_gather | solution.py:214
  13.5 198.9 %all-gather.15.cloned.1.call-start = ((), (), s32[]{:S(2)}) async-start(), calls=%async_computation.5 | async-start | bytes 1769472 | tf_op jit(solution)/shard_map/all_gather | solution.py:217
  13.6 28.2 %collective-permute-start = (bf16[128,1024]{1,0:T(8,128)(2,1)S(1)}, bf16[128,1024]{1,0:T(8,128)(2,1)S(1)}, u32[]{:S(2)}, u32[]{:S(2)}) collective-permute-start(bf16[128,1024]{1,0:T(8,128)(2,1)S(1)} %bitcast.240), channel_id=1, source_target_pairs={{8,0},{0,8},{24,16},{16,24},{9,1},{1,9},{25,17},{17,25},{10,2},{2,... | collective-permute-start | bytes 786440 | tf_op jit(solution)/shard_map/ppermute | solution.py:95
  14.2 27.6 %collective-permute-start.1 = (bf16[128,1024]{1,0:T(8,128)(2,1)S(1)}, bf16[128,1024]{1,0:T(8,128)(2,1)S(1)}, u32[]{:S(2)}, u32[]{:S(2)}) collective-permute-start(bf16[128,1024]{1,0:T(8,128)(2,1)S(1)} %bitcast.241), channel_id=1, source_target_pairs={{16,0},{24,8},{0,16},{8,24},{17,1},{25,9},{1,17},{9,25},{18,2},{26... | collective-permute-start | bytes 786440 | tf_op jit(solution)/shard_map/ppermute | solution.py:95
  16.7 23.9 %collective-permute-start.3 = (s32[1,128]{1,0:T(1,128)S(1)}, s32[1,128]{1,0:T(1,128)S(1)}, u32[]{:S(2)}, u32[]{:S(2)}) collective-permute-start(s32[1,128]{1,0:T(1,128)S(1)} %copy-done.59), channel_id=1, source_target_pairs={{8,0},{0,8},{24,16},{16,24},{9,1},{1,9},{25,17},{17,25},{10,2},{2,... | collective-permute-start | bytes 1544 | tf_op jit(solution)/shard_map/ppermute | solution.py:95
  16.9 23.8 %collective-permute-start.4 = (s32[1,128]{1,0:T(1,128)S(1)}, s32[1,128]{1,0:T(1,128)S(1)}, u32[]{:S(2)}, u32[]{:S(2)}) collective-permute-start(s32[1,128]{1,0:T(1,128)S(1)} %copy-done.59), channel_id=1, source_target_pairs={{16,0},{24,8},{0,16},{8,24},{17,1},{25,9},{1,17},{9,25},{18,2},{26... | collective-permute-start | bytes 1544 | tf_op jit(solution)/shard_map/ppermute | solution.py:95
  17.2 23.6 %collective-permute-start.5 = (s32[1,128]{1,0:T(1,128)S(1)}, s32[1,128]{1,0:T(1,128)S(1)}, u32[]{:S(2)}, u32[]{:S(2)}) collective-permute-start(s32[1,128]{1,0:T(1,128)S(1)} %copy-done.59), channel_id=1, source_target_pairs={{24,0},{16,8},{8,16},{0,24},{25,1},{17,9},{9,17},{1,25},{26,2},{18... | collective-permute-start | bytes 1544 | tf_op jit(solution)/shard_map/ppermute | solution.py:95
  19.3 349.7 %reduce-scatter.7.cloned.1.call-start = ((), (), s32[]{:S(2)}) async-start(), calls=%async_computation.9 | async-start | bytes 3538944
  71.9 13.3 %collective-permute-start.6 = (bf16[2,4,128,2,128]{4,2,3,1,0:T(8,128)(2,1)S(1)}, bf16[2,4,128,2,128]{4,2,3,1,0:T(8,128)(2,1)}, u32[]{:S(2)}, u32[]{:S(2)}) collective-permute-start(bf16[2,4,128,2,128]{4,2,3,1,0:T(8,128)(2,1)S(1)} %pad_maximum_fusion.13), channel_id=1, source_target_pairs={{1,0},{0,1},{3,2},{2,3},{5,4},{4,5},{7,6},{6,7},{9,8},{8,9},{11,10... | collective-permute-start | bytes 1572872 | tf_op jit(solution)/shard_map/ppermute | solution.py:95
  125.0 12.3 %collective-permute-start.12 = (bf16[128,1024]{1,0:T(8,128)(2,1)S(1)}, bf16[128,1024]{1,0:T(8,128)(2,1)}, u32[]{:S(2)}, u32[]{:S(2)}) collective-permute-start(bf16[128,1024]{1,0:T(8,128)(2,1)S(1)} %multiply_convert_fusion.3), channel_id=1, source_target_pairs={{24,0},{16,8},{8,16},{0,24},{25,1},{17,9},{9,17},{1,25},{26,2},{18... | collective-permute-start | bytes 786440 | tf_op jit(solution)/shard_map/ppermute | solution.py:95
  125.3 47.3 %collective-permute-start.16 = (bf16[128,1024]{1,0:T(8,128)(2,1)}, bf16[128,1024]{1,0:T(8,128)(2,1)}, u32[]{:S(2)}, u32[]{:S(2)}) collective-permute-start(bf16[128,1024]{1,0:T(8,128)(2,1)} %bitcast.19), channel_id=1, source_target_pairs={{8,0},{0,8},{24,16},{16,24},{9,1},{1,9},{25,17},{17,25},{10,2},{2,... | collective-permute-start | bytes 786440 | tf_op jit(solution)/shard_map/ppermute | solution.py:95
  125.7 46.9 %collective-permute-start.17 = (bf16[128,1024]{1,0:T(8,128)(2,1)}, bf16[128,1024]{1,0:T(8,128)(2,1)}, u32[]{:S(2)}, u32[]{:S(2)}) collective-permute-start(bf16[128,1024]{1,0:T(8,128)(2,1)} %bitcast.19), channel_id=1, source_target_pairs={{16,0},{24,8},{0,16},{8,24},{17,1},{25,9},{1,17},{9,25},{18,2},{26... | collective-permute-start | bytes 786440 | tf_op jit(solution)/shard_map/ppermute | solution.py:95
  127.2 45.4 %collective-permute-start.18 = (bf16[128,1024]{1,0:T(8,128)(2,1)}, bf16[128,1024]{1,0:T(8,128)(2,1)}, u32[]{:S(2)}, u32[]{:S(2)}) collective-permute-start(bf16[128,1024]{1,0:T(8,128)(2,1)} %bitcast.19), channel_id=1, source_target_pairs={{24,0},{16,8},{8,16},{0,24},{25,1},{17,9},{9,17},{1,25},{26,2},{18... | collective-permute-start | bytes 786440 | tf_op jit(solution)/shard_map/ppermute | solution.py:95
  221.0 12.2 %collective-permute-start.21 = (bf16[128,1024]{1,0:T(8,128)(2,1)S(1)}, bf16[128,1024]{1,0:T(8,128)(2,1)S(1)}, u32[]{:S(2)}, u32[]{:S(2)}) collective-permute-start(bf16[128,1024]{1,0:T(8,128)(2,1)S(1)} %get-tuple-element.78), channel_id=1, source_target_pairs={{0,24},{8,16},{16,8},{24,0},{1,25},{9,17},{17,9},{25,1},{2,26},{10... | collective-permute-start | bytes 786440 | tf_op jit(solution)/shard_map/ppermute | solution.py:104
  271.9 14.5 %collective-permute-start.25 = (bf16[2,4,128,2,128]{4,2,3,1,0:T(8,128)(2,1)S(1)}, bf16[2,4,128,2,128]{4,2,3,1,0:T(8,128)(2,1)S(1)}, u32[]{:S(2)}, u32[]{:S(2)}) collective-permute-start(bf16[2,4,128,2,128]{4,2,3,1,0:T(8,128)(2,1)S(1)} %fusion.15), channel_id=1, source_target_pairs={{0,1},{1,0},{2,3},{3,2},{4,5},{5,4},{6,7},{7,6},{8,9},{9,8},{10,11... | collective-permute-start | bytes 1572872 | tf_op jit(solution)/shard_map/ppermute | solution.py:104
  296.2 171.1 %reduce-scatter.5.cloned.1.call-start = ((), (), s32[]{:S(2)}) async-start(), calls=%async_computation.6 | async-start | bytes 5308416 | tf_op jit(solution)/shard_map/reduce_scatter | solution.py:313
  305.3 237.2 %all-gather.17.cloned.1.call-start = ((), (), s32[]{:S(2)}) async-start(), calls=%async_computation.7 | async-start | bytes 1966080 | tf_op jit(solution)/shard_map/all_gather | solution.py:381
  371.0 177.3 %all-gather.19.cloned.1.call-start = ((), (), s32[]{:S(2)}) async-start(), calls=%async_computation.8 | async-start | bytes 2949120 | tf_op jit(solution)/shard_map/all_gather | solution.py:380
  473.0 20.7 %collective-permute-start.28 = (bf16[128,1024]{1,0:T(8,128)(2,1)S(1)}, bf16[128,1024]{1,0:T(8,128)(2,1)S(1)}, u32[]{:S(2)}, u32[]{:S(2)}) collective-permute-start(bf16[128,1024]{1,0:T(8,128)(2,1)S(1)} %get-tuple-element.71), channel_id=1, source_target_pairs={{0,24},{8,16},{16,8},{24,0},{1,25},{9,17},{17,9},{25,1},{2,26},{10... | collective-permute-start | bytes 786440 | tf_op jit(solution)/shard_map/ppermute | solution.py:104
  474.2 65.8 %collective-permute-start.13 = (bf16[128,1024]{1,0:T(8,128)(2,1)}, bf16[128,1024]{1,0:T(8,128)(2,1)}, u32[]{:S(2)}, u32[]{:S(2)}) collective-permute-start(bf16[128,1024]{1,0:T(8,128)(2,1)} %get-tuple-element.80), channel_id=1, source_target_pairs={{0,8},{8,0},{16,24},{24,16},{1,9},{9,1},{17,25},{25,17},{2,10},{10... | collective-permute-start | bytes 786440 | tf_op jit(solution)/shard_map/ppermute | solution.py:104
  474.6 65.4 %collective-permute-start.14 = (bf16[128,1024]{1,0:T(8,128)(2,1)}, bf16[128,1024]{1,0:T(8,128)(2,1)}, u32[]{:S(2)}, u32[]{:S(2)}) collective-permute-start(bf16[128,1024]{1,0:T(8,128)(2,1)} %get-tuple-element.82), channel_id=1, source_target_pairs={{0,16},{8,24},{16,0},{24,8},{1,17},{9,25},{17,1},{25,9},{2,18},{10... | collective-permute-start | bytes 786440 | tf_op jit(solution)/shard_map/ppermute | solution.py:104
  476.1 63.9 %collective-permute-start.15 = (bf16[128,1024]{1,0:T(8,128)(2,1)}, bf16[128,1024]{1,0:T(8,128)(2,1)}, u32[]{:S(2)}, u32[]{:S(2)}) collective-permute-start(bf16[128,1024]{1,0:T(8,128)(2,1)} %get-tuple-element.81), channel_id=1, source_target_pairs={{0,24},{8,16},{16,8},{24,0},{1,25},{9,17},{17,9},{25,1},{2,26},{10... | collective-permute-start | bytes 786440 | tf_op jit(solution)/shard_map/ppermute | solution.py:104
  (94 other events, 725.3 us)
Sparse Core Ops, SparseCore 0:
  10.7 51.8 all-gather.8
  65.3 40.0 all-gather.10
  108.2 58.7 all-gather.12
  169.5 42.8 all-gather.14
  296.3 72.6 reduce-scatter.6
  372.5 94.7 reduce-scatter.4
  469.4 27.9 all-gather.16
  499.0 24.2 all-gather.18

commit v2 on v1

v2 whole, which is shorter than its diff:
```python
import math

import jax
import jax.numpy as jnp
from jax import lax
from jax.experimental import pallas as pl
from jax.experimental.pallas import tpu as pltpu
from jax.sharding import PartitionSpec as P

QUERY_HEADS = 16
KEY_VALUE_HEADS = 8
HEAD_SIZE = 128


EPSILON = 1e-06
ROPE_THETA = 1000000.0
NEGATIVE = -1e30
TEAM = ("rep", "ctx")
OWNERS = ("shard", "ctx")


def plain_product(left_side, right_side):
    return jnp.dot(left_side, right_side, preferred_element_type=jnp.float32)


def dot_right(left_side, right_side):
    return lax.dot_general(
        left_side, right_side, (((1,), (1,)), ((), ())), preferred_element_type=jnp.float32
    )


def dot_left(left_side, right_side):
    return lax.dot_general(
        left_side, right_side, (((0,), (0,)), ((), ())), preferred_element_type=jnp.float32
    )


def axis_bits(axis_name):
    size = lax.axis_size(axis_name)
    assert size & (size - 1) == 0
    return [(axis_name, 1 << place) for place in range(size.bit_length() - 1)]


def swap(value, step):
    axis_name, bit = step
    pairs = [(index, index ^ bit) for index in range(lax.axis_size(axis_name))]
    return lax.ppermute(value, axis_name, pairs)


def team_steps():
    return axis_bits("ctx") + axis_bits("rep")[::-1]


def gather_plain(value, steps):
    blocks = value[None]
    for step in steps:
        blocks = jnp.concatenate([blocks, swap(blocks, step)], axis=0)
    return blocks


def crossed(steps):
    return [steps[1], steps[0]] if len(steps) > 1 else list(steps)


def gather_rows(value):
    steps = team_steps()
    first, rest = steps[:2], steps[2:]
    front, back = jnp.split(value, 2, axis=0)
    front_blocks = gather_plain(front, crossed(first))
    back_blocks = gather_plain(back, first)
    if len(first) == 2:
        front_list = [front_blocks[place] for place in (0, 2, 1, 3)]
    else:
        front_list = list(front_blocks)
    back_list = list(back_blocks)
    for step in rest:
        near = [jnp.stack(front_list), jnp.stack(back_list)]
        far = [swap(blocks, step) for blocks in (front_blocks, back_blocks)]
        far_front = (
            [far[0][place] for place in (0, 2, 1, 3)] if len(front_list) == 4 else list(far[0])
        )
        front_list = front_list + far_front
        back_list = back_list + list(far[1])
        front_blocks, back_blocks = near
    pieces = []
    for front_piece, back_piece in zip(front_list, back_list):
        pieces += [front_piece, back_piece]
    return jnp.concatenate(pieces, axis=0)


def scatter_rows(value):
    steps = team_steps()
    first, rest = steps[:2], steps[2:]
    members = 1 << len(steps)
    rows = value.shape[0] // members
    halves = value.reshape(members, 2, rows // 2, value.shape[1])

    def shed(part, step):
        count = part.shape[0] // 2
        moved = swap(part[count:].astype(jnp.bfloat16), step)
        return part[:count] + moved.astype(jnp.float32)

    totals = []
    for half in range(2):
        part = halves[:, half]
        for step in rest[::-1]:
            part = shed(part, step)
        if half == 0 and len(first) == 2:
            moved = swap(part[1::2].astype(jnp.bfloat16), first[0])
            part = part[0::2] + moved.astype(jnp.float32)
            part = shed(part, first[1])
        else:
            for step in first[::-1]:
                part = shed(part, step)
        totals.append(part[0])
    return jnp.concatenate(totals, axis=0)


def everyone_sum(value):
    for axis_name in ("rep", "ctx", "shard"):
        for step in axis_bits(axis_name):
            value = value + swap(value, step)
    return value


def turned(values, cosine, sine):
    return values * cosine + pltpu.roll(values, HEAD_SIZE // 2, 1) * sine


def unit_rows(values):
    inverse = lax.rsqrt(jnp.mean(values * values, axis=-1, keepdims=True) + EPSILON)
    return (values * inverse, inverse)


def heads_of(projected_ref, cosine, sine, query_gain, key_gain, query_count):
    key_start = query_count * HEAD_SIZE
    queries = []
    for head in range(query_count):
        unit, inverse = unit_rows(projected_ref[:, head * HEAD_SIZE : (head + 1) * HEAD_SIZE])
        queries.append(
            (turned(unit * query_gain, cosine, sine).astype(jnp.bfloat16), unit, inverse)
        )
    key_unit, key_inverse = unit_rows(projected_ref[:, key_start : key_start + HEAD_SIZE])
    key_rot = turned(key_unit * key_gain, cosine, sine).astype(jnp.bfloat16)
    value_rows = projected_ref[:, key_start + HEAD_SIZE : key_start + 2 * HEAD_SIZE].astype(
        jnp.bfloat16
    )
    return queries, (key_rot, key_unit, key_inverse), value_rows


def probabilities(query_rot, key_rot, visible):
    scores = dot_right(query_rot, key_rot) * (1.0 / math.sqrt(HEAD_SIZE))
    scores = jnp.where(visible, scores, NEGATIVE)
    row_max = jnp.max(scores, axis=-1, keepdims=True)
    log_total = row_max + jnp.log(jnp.sum(jnp.exp(scores - row_max), axis=-1, keepdims=True))
    return jnp.exp(scores - log_total)


def attend_kernel(
    projected_ref, cosine_ref, sine_ref, row_ref, column_ref, query_gain_ref, key_gain_ref, out_ref
):
    query_count = out_ref.shape[1] // HEAD_SIZE
    visible = column_ref[...] <= row_ref[...]
    queries, (key_rot, _, _), value_rows = heads_of(
        projected_ref,
        cosine_ref[...],
        sine_ref[...],
        query_gain_ref[...],
        key_gain_ref[...],
        query_count,
    )
    for head in range(query_count):
        probs = probabilities(queries[head][0], key_rot, visible).astype(jnp.bfloat16)
        out_ref[:, head * HEAD_SIZE : (head + 1) * HEAD_SIZE] = plain_product(
            probs, value_rows
        ).astype(jnp.bfloat16)


def norm_back(gradient, unit, inverse, gain):
    gain_part = jnp.sum(gradient * unit, axis=0, keepdims=True)
    scaled = gradient * gain
    return (
        gain_part,
        inverse * (scaled - unit * jnp.mean(scaled * unit, axis=-1, keepdims=True)),
    )


def attend_back_kernel(
    projected_ref,
    attended_ref,
    attended_grad_ref,
    cosine_ref,
    sine_ref,
    row_ref,
    column_ref,
    query_gain_ref,
    key_gain_ref,
    out_ref,
    gain_ref,
):
    query_count = attended_ref.shape[1] // HEAD_SIZE
    key_start = query_count * HEAD_SIZE
    visible = column_ref[...] <= row_ref[...]
    cosine = cosine_ref[...]
    sine = sine_ref[...]
    scale = 1.0 / math.sqrt(HEAD_SIZE)
    queries, (key_rot, key_unit, key_inverse), value_rows = heads_of(
        projected_ref, cosine, sine, query_gain_ref[...], key_gain_ref[...], query_count
    )
    query_gain_part = jnp.zeros((1, HEAD_SIZE), jnp.float32)
    key_grad = jnp.zeros(key_unit.shape, jnp.float32)
    value_grad = jnp.zeros(key_unit.shape, jnp.float32)
    for head in range(query_count):
        columns = slice(head * HEAD_SIZE, (head + 1) * HEAD_SIZE)
        query_rot, query_unit, query_inverse = queries[head]
        grads = attended_grad_ref[:, columns]
        row_delta = jnp.sum(
            grads.astype(jnp.float32) * attended_ref[:, columns].astype(jnp.float32),
            axis=-1,
            keepdims=True,
        )
        prob_float = probabilities(query_rot, key_rot, visible)
        value_grad = value_grad + dot_left(prob_float.astype(jnp.bfloat16), grads)
        score_grad = (prob_float * (dot_right(grads, value_rows) - row_delta)).astype(jnp.bfloat16)
        query_grad = plain_product(score_grad, key_rot) * scale
        key_grad = key_grad + dot_left(score_grad, query_rot)
        part, query_pre = norm_back(
            turned(query_grad, cosine, -sine), query_unit, query_inverse, query_gain_ref[...]
        )
        query_gain_part = query_gain_part + part
        out_ref[:, columns] = query_pre.astype(jnp.bfloat16)
    key_gain_part, key_pre = norm_back(
        turned(key_grad * scale, cosine, -sine), key_unit, key_inverse, key_gain_ref[...]
    )
    out_ref[:, key_start : key_start + HEAD_SIZE] = key_pre.astype(jnp.bfloat16)
    out_ref[:, key_start + HEAD_SIZE : key_start + 2 * HEAD_SIZE] = value_grad.astype(jnp.bfloat16)

    @pl.when(pl.program_id(0) == 0)
    def _():
        gain_ref[...] = jnp.zeros_like(gain_ref)

    gain_ref[0:1, :] += query_gain_part
    gain_ref[1:2, :] += key_gain_part


def sequence_spec(rows, width):
    return pl.BlockSpec((rows, width), lambda place: (place, 0))


def fixed_spec(shape):
    return pl.BlockSpec(shape, lambda place: (0, 0))


def attention_call(kernel, out_specs, out_shape, wide, tables, small, rows):
    cosine, sine = tables
    return pl.pallas_call(
        kernel,
        grid=(wide[0].shape[0] // rows,),
        in_specs=[sequence_spec(rows, array.shape[1]) for array in wide]
        + [sequence_spec(rows, HEAD_SIZE)] * 2
        + [fixed_spec(array.shape) for array in small],
        out_specs=out_specs,
        out_shape=out_shape,
        compiler_params=pltpu.CompilerParams(dimension_semantics=("arbitrary",)),
    )(*wide, cosine, sine, *small)


def spread_kernel(place_ref, blocks_ref, *out_refs):
    start = 0
    for out_ref in out_refs:
        width = out_ref.shape[1]
        out_ref[...] = blocks_ref[0, :, start : start + width].astype(jnp.float32)
        start += width


def spread_columns(blocks, member, widths, order):
    count, rows, width = blocks.shape

    def source(place, member_ref):
        return (order(place ^ member_ref[0]), 0, 0)

    return pl.pallas_call(
        spread_kernel,
        grid_spec=pltpu.PrefetchScalarGridSpec(
            num_scalar_prefetch=1,
            grid=(count,),
            in_specs=[pl.BlockSpec((1, rows, width), source)],
            out_specs=[
                pl.BlockSpec((rows, size), lambda place, member_ref: (0, place)) for size in widths
            ],
        ),
        out_shape=[jax.ShapeDtypeStruct((rows, size * count), jnp.float32) for size in widths],
        compiler_params=pltpu.CompilerParams(dimension_semantics=("arbitrary",)),
    )(member.reshape(1), blocks)


def per_device(
    tokens,
    out_grad,
    positions,
    stretch_order,
    attn_gain,
    query_gain,
    key_norm_gain,
    query_weight,
    key_projection_matrix,
    value_projection_matrix,
    output_weight,
    ffn_gain,
    gate_weight,
    up_weight,
    down_weight,
):
    sequence_batch, count_of_rows, model_width = tokens.shape
    local_rows = sequence_batch * count_of_rows
    team = lax.axis_size(TEAM)
    ctx_size = lax.axis_size("ctx")
    ctx_place = lax.axis_index("ctx")
    member = lax.axis_index(TEAM)
    steps = team_steps()
    query_width = QUERY_HEADS // team * HEAD_SIZE
    kv_width = KEY_VALUE_HEADS // team * HEAD_SIZE
    hidden_width = gate_weight.shape[1] // team
    own_rows = model_width // lax.axis_size(OWNERS)
    own_start = lax.axis_index(OWNERS) * own_rows

    def ctx_columns(matrices, place):
        start_member = lax.axis_index("rep") * ctx_size + place
        pieces = []
        for matrix in matrices:
            width = matrix.shape[1] // team
            pieces.append(
                lax.dynamic_slice_in_dim(matrix, start_member * width, width, axis=1)
            )
        return jnp.concatenate(pieces, axis=1)

    def ctx_exchange(pick, axis):
        received = [pick(ctx_place)]
        for offset in range(1, ctx_size):
            pairs = [(index, index ^ offset) for index in range(ctx_size)]
            received.append(lax.ppermute(pick(ctx_place ^ offset), "ctx", pairs))
        if ctx_size == 1:
            return received[0]
        if ctx_size == 2:
            return jnp.where(
                ctx_place == 0,
                jnp.concatenate(received, axis=axis),
                jnp.concatenate(received[::-1], axis=axis),
            )
        stacked = jnp.stack(received)
        return jnp.concatenate(
            [
                lax.dynamic_index_in_dim(stacked, ctx_place ^ place, 0, keepdims=False)
                for place in range(ctx_size)
            ],
            axis=axis,
        )

    def team_weights(matrices):
        rows = ctx_exchange(lambda place: ctx_columns(matrices, place), 0)
        return lax.all_gather(rows, "shard", axis=0, tiled=True)

    attn_weights = team_weights(
        [query_weight, key_projection_matrix, value_projection_matrix, output_weight]
    )
    ffn_weights = team_weights([gate_weight, up_weight, down_weight])
    qkv_width = query_width + 2 * kv_width
    full_qkv = attn_weights[:, :qkv_width]
    full_output = attn_weights[:, qkv_width:]
    full_gate_up = ffn_weights[:, : 2 * hidden_width]
    full_down = ffn_weights[:, 2 * hidden_width :]
    gains = lax.all_gather(jnp.stack([attn_gain, ffn_gain]), OWNERS, axis=1, tiled=True).astype(
        jnp.float32
    )
    full_gain = gains[0][None, :]
    full_ffn_gain = gains[1][None, :]

    own_tokens = tokens.reshape(local_rows, model_width)
    own_grads = out_grad.reshape(local_rows, model_width)
    all_tokens = gather_rows(own_tokens)
    all_grads = gather_rows(own_grads)
    total_rows = all_tokens.shape[0]
    sequence_rows = count_of_rows * ctx_size
    assert sequence_batch == 1

    half_size = HEAD_SIZE // 2
    freq_steps = jnp.arange(HEAD_SIZE, dtype=jnp.int32)
    inverse = jnp.exp(
        (freq_steps % half_size).astype(jnp.float32) * (-2.0 * math.log(ROPE_THETA) / HEAD_SIZE)
    )
    all_positions = gather_plain(positions, steps).reshape(total_rows)
    angles = all_positions.astype(jnp.float32)[:, None] * inverse[None, :]
    tables = (
        jnp.cos(angles),
        jnp.sin(angles) * jnp.where(freq_steps < half_size, -1.0, 1.0)[None, :],
    )

    stretches_here = stretch_order.shape[0] // ctx_size
    block_rows = count_of_rows // stretches_here
    local = jnp.arange(count_of_rows, dtype=jnp.int32)
    match = (local // block_rows)[:, None] == jnp.arange(stretches_here, dtype=jnp.int32)[None]

    def stored_index(place):
        blocks = lax.dynamic_slice_in_dim(stretch_order, place * stretches_here, stretches_here)
        return (
            jnp.sum(jnp.where(match, blocks[None, :], 0), axis=1) * block_rows + local % block_rows
        )

    seq_index = jnp.concatenate([stored_index(ctx_place ^ offset) for offset in range(ctx_size)])
    small = (
        seq_index[:, None],
        seq_index[None, :],
        query_gain.astype(jnp.float32)[None, :],
        key_norm_gain.astype(jnp.float32)[None, :],
    )

    float_tokens = all_tokens.astype(jnp.float32)
    inv_first_all = lax.rsqrt(
        jnp.mean(float_tokens * float_tokens, axis=1, keepdims=True) + EPSILON
    )
    first_normalized = (float_tokens * inv_first_all * full_gain).astype(jnp.bfloat16)
    flat_tokens = own_tokens.astype(jnp.float32)
    inv_first = inv_first_all[:local_rows]
    unit_first = flat_tokens * inv_first
    projected = plain_product(first_normalized, full_qkv)
    attended = attention_call(
        attend_kernel,
        sequence_spec(sequence_rows, query_width),
        jax.ShapeDtypeStruct((total_rows, query_width), jnp.bfloat16),
        [projected],
        tables,
        small,
        sequence_rows,
    )
    middle = flat_tokens + scatter_rows(dot_right(attended, full_output))
    inv_second = lax.rsqrt(jnp.mean(middle * middle, axis=1, keepdims=True) + EPSILON)
    unit_second = middle * inv_second
    normed_second = gather_rows((unit_second * full_ffn_gain).astype(jnp.bfloat16))
    gate_up = plain_product(normed_second, full_gate_up)
    gate_value = gate_up[:, :hidden_width]
    up_value = gate_up[:, hidden_width:]
    sigmoid_gate = jax.nn.sigmoid(gate_value)
    activated = gate_value * sigmoid_gate
    hidden = (activated * up_value).astype(jnp.bfloat16)
    hidden_grad = plain_product(all_grads, full_down)
    gate_grad = (
        hidden_grad * up_value * sigmoid_gate * (1.0 + gate_value * (1.0 - sigmoid_gate))
    ).astype(jnp.bfloat16)
    up_grad = (hidden_grad * activated).astype(jnp.bfloat16)
    gate_up_grad = jnp.concatenate([gate_grad, up_grad], axis=1)

    def joined_products(pairs):
        return jnp.concatenate(
            [dot_left(left, right).astype(jnp.bfloat16) for left, right in pairs], axis=1
        )

    def shard_sum(rows):
        return lax.psum_scatter(rows, "shard", scatter_dimension=0, tiled=True)

    ffn_terms = joined_products([(normed_second, gate_up_grad), (all_grads, hidden)])
    ffn_terms, gate_up_grad = lax.optimization_barrier((ffn_terms, gate_up_grad))
    ffn_rows = shard_sum(ffn_terms)
    normed_grad_second = scatter_rows(dot_right(gate_up_grad, full_gate_up))
    ffn_gain_part = jnp.sum(normed_grad_second * unit_second, axis=0)
    unit_grad_second = normed_grad_second * full_ffn_gain
    middle_grad = own_grads.astype(jnp.float32) + inv_second * (
        unit_grad_second
        - unit_second * jnp.mean(unit_grad_second * unit_second, axis=1, keepdims=True)
    )
    middle_grad_b = gather_rows(middle_grad.astype(jnp.bfloat16))
    attended_grad = plain_product(middle_grad_b, full_output).astype(jnp.bfloat16)
    projected_grad, norm_gain_parts = attention_call(
        attend_back_kernel,
        [sequence_spec(sequence_rows, qkv_width), fixed_spec((8, HEAD_SIZE))],
        [
            jax.ShapeDtypeStruct((total_rows, qkv_width), jnp.bfloat16),
            jax.ShapeDtypeStruct((8, HEAD_SIZE), jnp.float32),
        ],
        [projected, attended, attended_grad],
        tables,
        small,
        sequence_rows,
    )
    attn_terms = joined_products([(first_normalized, projected_grad), (middle_grad_b, attended)])
    attn_terms, projected_grad = lax.optimization_barrier((attn_terms, projected_grad))
    attn_rows = shard_sum(attn_terms)
    block_sum = middle + scatter_rows(dot_right(hidden, full_down))
    block_out = block_sum.astype(jnp.bfloat16).reshape(sequence_batch, count_of_rows, model_width)
    normed_grad_first = scatter_rows(dot_right(projected_grad, full_qkv))
    attn_gain_part = jnp.sum(normed_grad_first * unit_first, axis=0)
    unit_grad_first = normed_grad_first * full_gain
    tokens_grad = middle_grad + inv_first * (
        unit_grad_first - unit_first * jnp.mean(unit_grad_first * unit_first, axis=1, keepdims=True)
    )
    gain_totals = everyone_sum(
        jnp.concatenate(
            [
                attn_gain_part.reshape(-1, HEAD_SIZE),
                ffn_gain_part.reshape(-1, HEAD_SIZE),
                norm_gain_parts,
            ],
            axis=0,
        )
    )
    gain_rows = model_width // HEAD_SIZE
    attn_gain_grad = lax.dynamic_slice_in_dim(
        gain_totals[:gain_rows].reshape(model_width), own_start, own_rows
    )
    ffn_gain_grad = lax.dynamic_slice_in_dim(
        gain_totals[gain_rows : 2 * gain_rows].reshape(model_width), own_start, own_rows
    )

    def block_order(offset):
        place = 0
        for position, (axis_name, bit) in enumerate(steps):
            weight = bit if axis_name == "ctx" else bit * ctx_size
            place = place + ((offset // weight) % 2) * (1 << position)
        return place

    def whole_columns(rows, widths):
        own = lax.dynamic_slice_in_dim(rows, ctx_place * own_rows, own_rows)
        blocks = [own]
        for offset in range(1, ctx_size):
            pairs = [(index, index ^ offset) for index in range(ctx_size)]
            sent = lax.dynamic_slice_in_dim(rows, (ctx_place ^ offset) * own_rows, own_rows)
            blocks.append(lax.ppermute(sent, "ctx", pairs))
        blocks = jnp.stack(blocks)
        for step in steps[len(axis_bits("ctx")) :]:
            blocks = jnp.concatenate([blocks, swap(blocks, step)], axis=0)
        return spread_columns(blocks, member, widths, block_order)

    gate_weight_grad, up_weight_grad, down_weight_grad = whole_columns(
        ffn_rows, [hidden_width] * 3
    )
    query_weight_grad, key_weight_grad, value_weight_grad, output_weight_grad = whole_columns(
        attn_rows, [query_width, kv_width, kv_width, query_width]
    )
    return (
        block_out,
        tokens_grad.reshape(sequence_batch, count_of_rows, model_width),
        query_weight_grad,
        key_weight_grad,
        value_weight_grad,
        output_weight_grad,
        gate_weight_grad,
        up_weight_grad,
        down_weight_grad,
        attn_gain_grad,
        ffn_gain_grad,
        gain_totals[2 * gain_rows],
        gain_totals[2 * gain_rows + 1],
    )


def solution(mesh):
    in_specs = (
        P(("rep", "shard"), "ctx", None),
        P(("rep", "shard"), "ctx", None),
        P(("rep", "shard"), "ctx"),
        P(),
        P(("shard", "ctx")),
        P(),
        P(),
        P(("shard", "ctx"), None),
        P(("shard", "ctx"), None),
        P(("shard", "ctx"), None),
        P(("shard", "ctx"), None),
        P(("shard", "ctx")),
        P(("shard", "ctx"), None),
        P(("shard", "ctx"), None),
        P(("shard", "ctx"), None),
    )
    out_specs = (
        P(("rep", "shard"), "ctx", None),
        P(("rep", "shard"), "ctx", None),
        P(("shard", "ctx"), None),
        P(("shard", "ctx"), None),
        P(("shard", "ctx"), None),
        P(("shard", "ctx"), None),
        P(("shard", "ctx"), None),
        P(("shard", "ctx"), None),
        P(("shard", "ctx"), None),
        P(("shard", "ctx")),
        P(("shard", "ctx")),
        P(),
        P(),
    )
    return jax.shard_map(
        per_device, mesh=mesh, in_specs=in_specs, out_specs=out_specs, check_vma=False
    )
```

time: 567 us -> 322 us (0.57)
  waiting for transfers between devices: 341 us -> 79.2 us
  blocking collectives: 64.8 us -> 20.8 us
  starting transfers between devices: 20.9 us -> 50.8 us
  Pallas kernels: 0 us -> 29.8 us
  other arithmetic: 33.4 us -> 44.7 us
    reduce_scatter x1 -> x2, waiting for transfers between devices: 96.3 us -> 0.02 us  [shard_sum(): return lax.psum_scatter(rows, 'shard', scatter_dimension=0, tiled=True)]
    all_gather x6 -> x2, waiting for transfers between devices: 95.9 us -> 0.02 us  [team_weights(): return lax.all_gather(rows, 'shard', axis=0, tiled=True)]
    unnamed x9 -> x4, waiting for transfers between devices: 63.8 us -> 0.07 us
    psum x1 -> x0, blocking collectives: 44 us -> none  [per_device(): lax.psum((attn_gain_part, ffn_gain_part, query_gain_part, key_gain_part),...]
    ppermute x29 -> x64, starting transfers between devices: 20.3 us -> 50.6 us  [the longest x60 45 us: swap(): return lax.ppermute(value, axis_name, pairs)]
    pallas_call x0 -> x4, Pallas kernels: none -> 29.8 us  [the longest x2 18 us: attention_call(): pl.pallas_call(kernel, grid=(wide[0].shape[0] // rows,), in_specs=[sequen...]
    concatenate x7 -> x29, other arithmetic: 5.83 us -> 20 us  [the longest x18 8.98 us: gather_plain(): blocks = jnp.concatenate([blocks, swap(blocks, step)], axis=0)]
    convert_element_type x12 -> x1, other arithmetic: 9.21 us -> 0.7 us  [per_device(): angles = all_positions.astype(jnp.float32)[:, None] * inverse[None, :]]
  transfers between devices with their start and end apart: 37 -> 68, of which waited for: 19 -> 30; matrix products, arithmetic and copies ran while one was open for 11% -> 28% of each run, Pallas kernels for 0% -> 7%
where the time goes in v2:
time: 322 us; the launch traced here: 320 us
  waiting for transfers between devices  79.2 us (25%)
  starting transfers between devices  50.8 us (16%)
  local copies, waits for them, and re-layouts  46.8 us (15%)
  other arithmetic  44.7 us (14%)
  matrix products  32.8 us (10%)
  Pallas kernels  29.8 us (9%)
  blocking collectives  20.8 us (6%)
  between operations  15.2 us (5%)
    ppermute x60, waiting for transfers between devices, swap(): return lax.ppermute(value, axis_name, pairs)  72.4 us
    ppermute x60, starting transfers between devices, swap(): return lax.ppermute(value, axis_name, pairs)  45 us
    unnamed x120, local copies, waits for them, and re-layouts  27.6 us
    all_gather x1, blocking collectives, per_device(): lax.all_gather(jnp.stack([attn_gain, ffn_gain]), OWNERS, axis=1, tiled=True)  20.8 us
    pallas_call x2, Pallas kernels, attention_call(): pl.pallas_call(kernel, grid=(wide[0].shape[0] // rows,), in_specs=[sequen...  18 us
    dot_general x4, matrix products, plain_product(): return jnp.dot(left_side, right_side, preferred_element_type=jnp.float32)  13.2 us
    pallas_call x2, Pallas kernels, spread_columns(): pl.pallas_call(spread_kernel, grid_spec=pltpu.PrefetchScalarGridSpec(num_...  11.8 us
    dot_general x4, matrix products, dot_right(): lax.dot_general(left_side, right_side, (((1,), (1,)), ((), ())), preferre...  10.9 us
  transfers between devices with their start and end apart: 68, of which 30 were waited for; matrix products, arithmetic and copies ran while one was open for 28% of the time, Pallas kernels for 7%

profile of v2, /device:TPU:0, one launch (start us, length us, event | category | flops | bytes accessed | tf_op | source)
XLA Modules:
  0.0 320.2 jit_solution(14256270211083828462)
XLA Ops:
  11.1 3.0 collective-permute-start.6
  25.3 20.8 %all_gather.9 = bf16[2,1024]{1,0:T(2,128)(2,1)S(1)} all-gather(bf16[2,128]{1,0:T(2,128)(2,1)S(1)} %pad_maximum_fusion.30), channel_id=1, replica_groups=mesh['rep'=4,'shard'=4,'ctx'=2] {'shard','ctx'}, dimensions={1}, use_global_device_ids=true | all-gather | bytes 4608 | tf_op jit(solution)/shard_map/all_gather | solution.py:372
  56.9 3.7 %fusion.35 = (f32[1024,128]{1,0:T(8,128)}, f32[1024,128]{1,0:T(8,128)}) fusion(f32[128]{0:T(128)} %get-tuple-element.116, f32[128]{0:T(128)} %get-tuple-element.117, f32[1024]{0:T(1024)S(1)} %bitcast.403), kind=kLoop, calls=%fused_computation.68 | loop fusion | flops 262144 | bytes 1053696 | tf_op jit(solution)/shard_map/mul | solution.py:395
  93.3 3.9 %fusion.18.projected_ref = f32[1024,512]{1,0:T(8,128)} fusion(bf16[1024,768]{1,0:T(8,128)(2,1)} %all-gather.3.cloned.1.call-done, bf16[1024,1024]{1,0:T(8,128)(2,1)S(1)} %fusion.81, f32[1024]{0:T(1024)S(1)} %bitcast.395, f32[1024]{0:T(1024)S(1)} %add_rsqrt_fusion), kind=kOutput, calls=%fused_computation.43 | convolution fusion | flops 1077936128 | bytes 5251072 | tf_op jit(solution)/shard_map/dot_general | solution.py:23
  97.3 8.2 %shard_map.246.attended_ref = bf16[1024,256]{1,0:T(8,128)(2,1)} custom-call(f32[1024,512]{1,0:T(8,128)} %fusion.18.projected_ref, f32[1024,128]{1,0:T(8,128)} %get-tuple-element.105.cosine_ref, f32[1024,128]{1,0:T(8,128)} %get-tuple-element.104.sine_ref, s32[256,1]{1,0:T(8,128)} %copy.62.row_ref, s32[1,256]{1,0:T(1,128)} %bitcast.405, ...), custom_call_target="tpu_custom_call" | custom-call | tf_op jit(solution)/shard_map/pallas_call | solution.py:256
  117.7 3.6 %collective-permute-done.11 = bf16[2,64,1024]{2,1,0:T(8,128)(2,1)S(1)} collective-permute-done((bf16[2,64,1024]{2,1,0:T(8,128)(2,1)S(1)}, bf16[2,64,1024]{2,1,0:T(8,128)(2,1)S(1)}, u32[]{:S(2)}, u32[]{:S(2)}) %collective-permute-start.11) | collective-permute-done | bytes 262176 | tf_op jit(solution)/shard_map/ppermute | solution.py:47
  144.8 3.3 %fusion.6 = f32[1024,768]{0,1:T(8,128)S(1)} fusion(bf16[1024,1024]{1,0:T(8,128)(2,1)S(1)} %fusion.69, bf16[1024,1152]{1,0:T(8,128)(2,1)} %all-gather.5.cloned.1.call-done), kind=kOutput, calls=%fused_computation.20 | convolution fusion | flops 1610612736 | bytes 6815744 | tf_op jit(solution)/shard_map/dot_general | solution.py:23
  148.1 3.4 %multiply_convert_fusion.1 = (bf16[1024,384]{0,1:T(8,128)(2,1)S(1)}, bf16[1024,384]{0,1:T(8,128)(2,1)S(1)}, bf16[1024,384]{0,1:T(8,128)(2,1)S(1)}) fusion(f32[1024,768]{0,1:T(8,128)S(1)} %fusion.6, bf16[1024,1024]{1,0:T(8,128)(2,1)} %fusion.57, bf16[1024,1152]{1,0:T(8,128)(2,1)} %all-gather.5.cloned.1.call-done), kind=kOutput, calls=%fused_computation.12 | convolution fusion | flops 811204608 | bytes 8388608 | tf_op jit(solution)/shard_map/dot_general | solution.py:23
  155.6 2.9 convolution_convert_fusion.2
  160.0 3.7 %fusion.4 = f32[1024,1024]{1,0:T(8,128)S(1)} fusion(bf16[1024,768]{0,1:T(8,128)(2,1)} %pad_maximum_fusion.2, bf16[1024,1152]{1,0:T(8,128)(2,1)} %all-gather.5.cloned.1.call-done), kind=kOutput, calls=%fused_computation.18 | convolution fusion | flops 1610612736 | bytes 7340032 | tf_op jit(solution)/shard_map/dot_general | solution.py:27
  171.9 5.6 %collective-permute-done.36 = bf16[2,64,1024]{2,1,0:T(8,128)(2,1)S(1)} collective-permute-done((bf16[2,64,1024]{2,1,0:T(8,128)(2,1)}, bf16[2,64,1024]{2,1,0:T(8,128)(2,1)S(1)}, u32[]{:S(2)}, u32[]{:S(2)}) %collective-permute-start.36) | collective-permute-done | bytes 262176 | tf_op jit(solution)/shard_map/ppermute | solution.py:47
  191.9 3.0 collective-permute-start.42
  205.3 9.8 %shard_map.247 = (bf16[1024,512]{1,0:T(8,128)(2,1)}, f32[8,128]{1,0:T(8,128)}) custom-call(f32[1024,512]{1,0:T(8,128)} %fusion.18.projected_ref, bf16[1024,256]{1,0:T(8,128)(2,1)} %shard_map.246.attended_ref, bf16[1024,256]{1,0:T(8,128)(2,1)} %convolution_convert_fusion.4.attended_grad_ref, f32[1024,128]{1,0:T(8,128)} %get-tuple-element.105.cosine_ref, ...), custom_call_target="tpu_custom_call" | custom-call | tf_op jit(solution)/shard_map/pallas_call | solution.py:256
  220.4 2.8 fusion.16
  234.1 4.3 %collective-permute-done.24 = bf16[2,64,1024]{2,1,0:T(8,128)(2,1)S(1)} collective-permute-done((bf16[2,64,1024]{2,1,0:T(8,128)(2,1)S(1)}, bf16[2,64,1024]{2,1,0:T(8,128)(2,1)S(1)}, u32[]{:S(2)}, u32[]{:S(2)}) %collective-permute-start.24) | collective-permute-done | bytes 262176 | tf_op jit(solution)/shard_map/ppermute | solution.py:47
  244.4 6.6 %collective-permute-done.51 = bf16[2,64,1024]{2,1,0:T(8,128)(2,1)S(1)} collective-permute-done((bf16[2,64,1024]{2,1,0:T(8,128)(2,1)S(1)}, bf16[2,64,1024]{2,1,0:T(8,128)(2,1)S(1)}, u32[]{:S(2)}, u32[]{:S(2)}) %collective-permute-start.51) | collective-permute-done | bytes 262176 | tf_op jit(solution)/shard_map/ppermute | solution.py:47
  252.7 3.5 %collective-permute-done.52 = bf16[1,64,1024]{2,1,0:T(8,128)(2,1)S(1)} collective-permute-done((bf16[1,64,1024]{2,1,0:T(8,128)(2,1)S(1)}, bf16[1,64,1024]{2,1,0:T(8,128)(2,1)S(1)}, u32[]{:S(2)}, u32[]{:S(2)}) %collective-permute-start.52) | collective-permute-done | bytes 131104 | tf_op jit(solution)/shard_map/ppermute | solution.py:47
  261.7 6.4 %collective-permute-done.56 = bf16[128,1152]{1,0:T(8,128)(2,1)S(1)} collective-permute-done((bf16[128,1152]{1,0:T(8,128)(2,1)S(1)}, bf16[128,1152]{1,0:T(8,128)(2,1)S(1)}, u32[]{:S(2)}, u32[]{:S(2)}) %collective-permute-start.56) | collective-permute-done | bytes 294944 | tf_op jit(solution)/shard_map/ppermute | solution.py:526
  274.6 9.8 %collective-permute-done.57 = bf16[2,128,1152]{2,1,0:T(8,128)(2,1)S(1)} collective-permute-done((bf16[2,128,1152]{2,1,0:T(8,128)(2,1)S(1)}, bf16[2,128,1152]{2,1,0:T(8,128)(2,1)S(1)}, u32[]{:S(2)}, u32[]{:S(2)}) %collective-permute-start.57) | collective-permute-done | bytes 589856 | tf_op jit(solution)/shard_map/ppermute | solution.py:47
  285.5 5.4 %collective-permute-done.54 = bf16[2,128,768]{2,1,0:T(8,128)(2,1)S(1)} collective-permute-done((bf16[2,128,768]{2,1,0:T(8,128)(2,1)S(1)}, bf16[2,128,768]{2,1,0:T(8,128)(2,1)S(1)}, u32[]{:S(2)}, u32[]{:S(2)}) %collective-permute-start.54) | collective-permute-done | bytes 393248 | tf_op jit(solution)/shard_map/ppermute | solution.py:47
  292.5 3.3 %collective-permute-done.63 = f32[24,128]{1,0:T(8,128)S(1)} collective-permute-done((f32[24,128]{1,0:T(8,128)S(1)}, f32[24,128]{1,0:T(8,128)S(1)}, u32[]{:S(2)}, u32[]{:S(2)}) %collective-permute-start.63) | collective-permute-done | bytes 12320 | tf_op jit(solution)/shard_map/ppermute | solution.py:47
  298.8 5.7 %shard_map.248 = (f32[128,2048]{1,0:T(8,128)}, f32[128,1024]{1,0:T(8,128)}, f32[128,1024]{1,0:T(8,128)}, f32[128,2048]{1,0:T(8,128)}) custom-call(s32[1]{0:T(128)} %bitcast.104.place_ref, bf16[8,128,768]{2,1,0:T(8,128)(2,1)} %pad_maximum_fusion.4.blocks_ref), custom_call_target="tpu_custom_call" | custom-call | tf_op jit(solution)/shard_map/pallas_call | solution.py:282
  304.6 2.9 pad_maximum_fusion.1.blocks_ref
  307.5 6.1 %shard_map.249 = (f32[128,3072]{1,0:T(8,128)}, f32[128,3072]{1,0:T(8,128)}, f32[128,3072]{1,0:T(8,128)}) custom-call(s32[1]{0:T(128)} %bitcast.104.place_ref, bf16[8,128,1152]{2,1,0:T(8,128)(2,1)} %pad_maximum_fusion.1.blocks_ref), custom_call_target="tpu_custom_call" | custom-call | tf_op jit(solution)/shard_map/pallas_call | solution.py:282
  (372 shorter events, 173.2 us)
Async XLA Ops:
  7.2 86.1 %all-gather.3.cloned.1.call-start = ((), (), s32[]{:S(2)}) async-start(), calls=%async_computation.2 | async-start | bytes 1966080 | tf_op jit(solution)/shard_map/all_gather | solution.py:361
  11.1 35.2 %collective-permute-start.6 = (bf16[128,768]{1,0:T(8,128)(2,1)}, bf16[128,768]{1,0:T(8,128)(2,1)}, u32[]{:S(2)}, u32[]{:S(2)}) collective-permute-start(bf16[128,768]{1,0:T(8,128)(2,1)} %pad_maximum_fusion.28), channel_id=1, source_target_pairs={{0,1},{1,0},{2,3},{3,2},{4,5},{5,4},{6,7},{7,6},{8,9},{9,8},{10,11... | collective-permute-start | bytes 589832 | tf_op jit(solution)/shard_map/ppermute | solution.py:341
  15.0 45.6 %collective-permute-start = (bf16[1,64,1024]{2,1,0:T(8,128)(2,1)S(1)}, bf16[1,64,1024]{2,1,0:T(8,128)(2,1)S(1)}, u32[]{:S(2)}, u32[]{:S(2)}) collective-permute-start(bf16[1,64,1024]{2,1,0:T(8,128)(2,1)S(1)} %get-tuple-element.95), channel_id=1, source_target_pairs={{0,16},{8,24},{16,0},{24,8},{1,17},{9,25},{17,1},{25,9},{2,18},{10... | collective-permute-start | bytes 393224 | tf_op jit(solution)/shard_map/ppermute | solution.py:47
  16.6 46.8 %collective-permute-start.2 = (bf16[1,64,1024]{2,1,0:T(8,128)(2,1)S(1)}, bf16[1,64,1024]{2,1,0:T(8,128)(2,1)S(1)}, u32[]{:S(2)}, u32[]{:S(2)}) collective-permute-start(bf16[1,64,1024]{2,1,0:T(8,128)(2,1)S(1)} %get-tuple-element.94), channel_id=1, source_target_pairs={{0,1},{1,0},{2,3},{3,2},{4,5},{5,4},{6,7},{7,6},{8,9},{9,8},{10,11... | collective-permute-start | bytes 393224 | tf_op jit(solution)/shard_map/ppermute | solution.py:47
  17.1 33.7 %collective-permute-start.7 = (s32[1,1,128]{2,1,0:T(1,128)}, s32[1,1,128]{2,1,0:T(1,128)S(1)}, u32[]{:S(2)}, u32[]{:S(2)}) collective-permute-start(s32[1,1,128]{2,1,0:T(1,128)} %bitcast.407), channel_id=1, source_target_pairs={{0,1},{1,0},{2,3},{3,2},{4,5},{5,4},{6,7},{7,6},{8,9},{9,8},{10,11... | collective-permute-start | bytes 1544 | tf_op jit(solution)/shard_map/ppermute | solution.py:47
  22.7 45.8 %collective-permute-start.22 = (bf16[128,1152]{1,0:T(8,128)(2,1)}, bf16[128,1152]{1,0:T(8,128)(2,1)}, u32[]{:S(2)}, u32[]{:S(2)}) collective-permute-start(bf16[128,1152]{1,0:T(8,128)(2,1)} %pad_maximum_fusion.19), channel_id=1, source_target_pairs={{0,1},{1,0},{2,3},{3,2},{4,5},{5,4},{6,7},{7,6},{8,9},{9,8},{10,11... | collective-permute-start | bytes 884744 | tf_op jit(solution)/shard_map/ppermute | solution.py:341
  46.3 19.3 %collective-permute-start.29 = (bf16[1,64,1024]{2,1,0:T(8,128)(2,1)}, bf16[1,64,1024]{2,1,0:T(8,128)(2,1)S(1)}, u32[]{:S(2)}, u32[]{:S(2)}) collective-permute-start(bf16[1,64,1024]{2,1,0:T(8,128)(2,1)} %get-tuple-element.91), channel_id=1, source_target_pairs={{0,16},{8,24},{16,0},{24,8},{1,17},{9,25},{17,1},{25,9},{2,18},{10... | collective-permute-start | bytes 393224 | tf_op jit(solution)/shard_map/ppermute | solution.py:47
  48.9 94.6 %all-gather.5.cloned.1.call-start = ((), (), s32[]{:S(2)}) async-start(), calls=%async_computation.3 | async-start | bytes 2949120 | tf_op jit(solution)/shard_map/all_gather | solution.py:361
  56.2 11.1 %collective-permute-start.31 = (bf16[1,64,1024]{2,1,0:T(8,128)(2,1)S(1)}, bf16[1,64,1024]{2,1,0:T(8,128)(2,1)S(1)}, u32[]{:S(2)}, u32[]{:S(2)}) collective-permute-start(bf16[1,64,1024]{2,1,0:T(8,128)(2,1)S(1)} %get-tuple-element.90), channel_id=1, source_target_pairs={{0,1},{1,0},{2,3},{3,2},{4,5},{5,4},{6,7},{7,6},{8,9},{9,8},{10,11... | collective-permute-start | bytes 393224 | tf_op jit(solution)/shard_map/ppermute | solution.py:47
  70.7 186.3 %reduce-scatter.5.cloned.1.call-start = ((), (), s32[]{:S(2)}) async-start(), calls=%async_computation.5 | async-start | bytes 2949120 | tf_op jit(solution)/shard_map/reduce_scatter | solution.py:458
  71.8 19.2 %collective-permute-start.4 = (bf16[4,64,1024]{2,1,0:T(8,128)(2,1)S(1)}, bf16[4,64,1024]{2,1,0:T(8,128)(2,1)S(1)}, u32[]{:S(2)}, u32[]{:S(2)}) collective-permute-start(bf16[4,64,1024]{2,1,0:T(8,128)(2,1)S(1)} %pad_maximum_fusion.8), channel_id=1, source_target_pairs={{0,8},{8,0},{16,24},{24,16},{1,9},{9,1},{17,25},{25,17},{2,10},{10... | collective-permute-start | bytes 1572872 | tf_op jit(solution)/shard_map/ppermute | solution.py:47
  74.6 16.4 %collective-permute-start.5 = (bf16[4,64,1024]{2,1,0:T(8,128)(2,1)S(1)}, bf16[4,64,1024]{2,1,0:T(8,128)(2,1)S(1)}, u32[]{:S(2)}, u32[]{:S(2)}) collective-permute-start(bf16[4,64,1024]{2,1,0:T(8,128)(2,1)S(1)} %pad_maximum_fusion.9), channel_id=1, source_target_pairs={{0,8},{8,0},{16,24},{24,16},{1,9},{9,1},{17,25},{25,17},{2,10},{10... | collective-permute-start | bytes 1572872 | tf_op jit(solution)/shard_map/ppermute | solution.py:47
  76.7 15.0 %collective-permute-start.33 = (bf16[4,64,1024]{2,1,0:T(8,128)(2,1)S(1)}, bf16[4,64,1024]{2,1,0:T(8,128)(2,1)S(1)}, u32[]{:S(2)}, u32[]{:S(2)}) collective-permute-start(bf16[4,64,1024]{2,1,0:T(8,128)(2,1)S(1)} %pad_maximum_fusion.12), channel_id=1, source_target_pairs={{0,8},{8,0},{16,24},{24,16},{1,9},{9,1},{17,25},{25,17},{2,10},{10... | collective-permute-start | bytes 1572872 | tf_op jit(solution)/shard_map/ppermute | solution.py:47
  79.7 28.6 %collective-permute-start.34 = (bf16[4,64,1024]{2,1,0:T(8,128)(2,1)}, bf16[4,64,1024]{2,1,0:T(8,128)(2,1)}, u32[]{:S(2)}, u32[]{:S(2)}) collective-permute-start(bf16[4,64,1024]{2,1,0:T(8,128)(2,1)} %pad_maximum_fusion.13), channel_id=1, source_target_pairs={{0,8},{8,0},{16,24},{24,16},{1,9},{9,1},{17,25},{25,17},{2,10},{10... | collective-permute-start | bytes 1572872 | tf_op jit(solution)/shard_map/ppermute | solution.py:47
  171.8 88.2 %reduce-scatter.3.cloned.1.call-start = ((), (), s32[]{:S(2)}) async-start(), calls=%async_computation.4 | async-start | bytes 1966080 | tf_op jit(solution)/shard_map/reduce_scatter | solution.py:458
  195.1 31.7 %collective-permute-start.23 = (bf16[4,64,1024]{2,1,0:T(8,128)(2,1)S(1)}, bf16[4,64,1024]{2,1,0:T(8,128)(2,1)}, u32[]{:S(2)}, u32[]{:S(2)}) collective-permute-start(bf16[4,64,1024]{2,1,0:T(8,128)(2,1)S(1)} %get-tuple-element.68), channel_id=1, source_target_pairs={{0,8},{8,0},{16,24},{24,16},{1,9},{9,1},{17,25},{25,17},{2,10},{10... | collective-permute-start | bytes 1572872 | tf_op jit(solution)/shard_map/ppermute | solution.py:47
  195.2 31.6 %collective-permute-start.26 = (bf16[4,64,1024]{2,1,0:T(8,128)(2,1)S(1)}, bf16[4,64,1024]{2,1,0:T(8,128)(2,1)}, u32[]{:S(2)}, u32[]{:S(2)}) collective-permute-start(bf16[4,64,1024]{2,1,0:T(8,128)(2,1)S(1)} %get-tuple-element.69), channel_id=1, source_target_pairs={{0,8},{8,0},{16,24},{24,16},{1,9},{9,1},{17,25},{25,17},{2,10},{10... | collective-permute-start | bytes 1572872 | tf_op jit(solution)/shard_map/ppermute | solution.py:47
  233.2 11.0 %collective-permute-start.48 = (bf16[2,64,1024]{2,1,0:T(8,128)(2,1)S(1)}, bf16[2,64,1024]{2,1,0:T(8,128)(2,1)S(1)}, u32[]{:S(2)}, u32[]{:S(2)}) collective-permute-start(bf16[2,64,1024]{2,1,0:T(8,128)(2,1)S(1)} %slice.421), channel_id=1, source_target_pairs={{0,1},{1,0},{2,3},{3,2},{4,5},{5,4},{6,7},{7,6},{8,9},{9,8},{10,11... | collective-permute-start | bytes 786440 | tf_op jit(solution)/shard_map/ppermute | solution.py:47
  239.2 29.3 %collective-permute-start.25 = (bf16[1,64,1024]{2,1,0:T(8,128)(2,1)}, bf16[1,64,1024]{2,1,0:T(8,128)(2,1)S(1)}, u32[]{:S(2)}, u32[]{:S(2)}) collective-permute-start(bf16[1,64,1024]{2,1,0:T(8,128)(2,1)} %slice.680), channel_id=1, source_target_pairs={{0,16},{8,24},{16,0},{24,8},{1,17},{9,25},{17,1},{25,9},{2,18},{10... | collective-permute-start | bytes 393224 | tf_op jit(solution)/shard_map/ppermute | solution.py:47
  242.1 31.4 %collective-permute-start.28 = (bf16[1,64,1024]{2,1,0:T(8,128)(2,1)}, bf16[1,64,1024]{2,1,0:T(8,128)(2,1)S(1)}, u32[]{:S(2)}, u32[]{:S(2)}) collective-permute-start(bf16[1,64,1024]{2,1,0:T(8,128)(2,1)} %slice.679), channel_id=1, source_target_pairs={{0,1},{1,0},{2,3},{3,2},{4,5},{5,4},{6,7},{7,6},{8,9},{9,8},{10,11... | collective-permute-start | bytes 393224 | tf_op jit(solution)/shard_map/ppermute | solution.py:47
  268.1 16.3 %collective-permute-start.57 = (bf16[2,128,1152]{2,1,0:T(8,128)(2,1)S(1)}, bf16[2,128,1152]{2,1,0:T(8,128)(2,1)S(1)}, u32[]{:S(2)}, u32[]{:S(2)}) collective-permute-start(bf16[2,128,1152]{2,1,0:T(8,128)(2,1)S(1)} %pad_maximum_fusion.7), channel_id=1, source_target_pairs={{0,16},{8,24},{16,0},{24,8},{1,17},{9,25},{17,1},{25,9},{2,18},{10... | collective-permute-start | bytes 1769480 | tf_op jit(solution)/shard_map/ppermute | solution.py:47
  271.9 19.0 %collective-permute-start.54 = (bf16[2,128,768]{2,1,0:T(8,128)(2,1)S(1)}, bf16[2,128,768]{2,1,0:T(8,128)(2,1)S(1)}, u32[]{:S(2)}, u32[]{:S(2)}) collective-permute-start(bf16[2,128,768]{2,1,0:T(8,128)(2,1)S(1)} %pad_maximum_fusion.18), channel_id=1, source_target_pairs={{0,16},{8,24},{16,0},{24,8},{1,17},{9,25},{17,1},{25,9},{2,18},{10... | collective-permute-start | bytes 1179656 | tf_op jit(solution)/shard_map/ppermute | solution.py:47
  274.6 16.6 %collective-permute-start.62 = (f32[24,128]{1,0:T(8,128)S(1)}, f32[24,128]{1,0:T(8,128)S(1)}, u32[]{:S(2)}, u32[]{:S(2)}) collective-permute-start(f32[24,128]{1,0:T(8,128)S(1)} %add.283), channel_id=1, source_target_pairs={{0,2},{2,0},{4,6},{6,4},{1,3},{3,1},{5,7},{7,5},{8,10},{10,8},{12,... | collective-permute-start | bytes 36872 | tf_op jit(solution)/shard_map/ppermute | solution.py:47
  285.5 19.0 %collective-permute-start.58 = (bf16[4,128,1152]{2,1,0:T(8,128)(2,1)}, bf16[4,128,1152]{2,1,0:T(8,128)(2,1)}, u32[]{:S(2)}, u32[]{:S(2)}) collective-permute-start(bf16[4,128,1152]{2,1,0:T(8,128)(2,1)} %pad_maximum_fusion.5), channel_id=1, source_target_pairs={{0,8},{8,0},{16,24},{24,16},{1,9},{9,1},{17,25},{25,17},{2,10},{10... | collective-permute-start | bytes 3538952 | tf_op jit(solution)/shard_map/ppermute | solution.py:47
  (76 other events, 851.3 us)
Sparse Core Ops, SparseCore 0:
  49.0 34.2 all-gather.2
  85.5 48.8 all-gather.4
  171.9 45.4 reduce-scatter.4
  220.5 34.4 reduce-scatter.2

commit v3 on v2

v3 whole, which is shorter than its diff:
```python
import functools
import math

import jax
import jax.numpy as jnp
from jax import lax
from jax.experimental import pallas as pl
from jax.experimental.pallas import tpu as pltpu
from jax.sharding import PartitionSpec as P

QUERY_HEADS = 16
KEY_VALUE_HEADS = 8
HEAD_SIZE = 128


EPSILON = 1e-06
ROPE_THETA = 1000000.0
NEGATIVE = -1e30
TEAM = ("rep", "ctx")
OWNERS = ("shard", "ctx")
FLOPS_HINT = 8_000_000_000


def plain_product(left_side, right_side):
    return jnp.dot(left_side, right_side, preferred_element_type=jnp.float32)


def dot_right(left_side, right_side):
    return lax.dot_general(
        left_side, right_side, (((1,), (1,)), ((), ())), preferred_element_type=jnp.float32
    )


def dot_left(left_side, right_side):
    return lax.dot_general(
        left_side, right_side, (((0,), (0,)), ((), ())), preferred_element_type=jnp.float32
    )


def axis_bits(axis_name):
    size = lax.axis_size(axis_name)
    assert size & (size - 1) == 0
    return [1 << place for place in range(size.bit_length() - 1)]


def swap(value, axes, offset):
    pairs = [(index, index ^ offset) for index in range(lax.axis_size(axes))]
    return lax.ppermute(value, axes, pairs)


def after(value, *others):
    return lax.optimization_barrier((value,) + others)[0]


def gather_plain(value, axes, offsets):
    blocks = value[None]
    for offset in offsets:
        blocks = jnp.concatenate([blocks, swap(blocks, axes, offset)], axis=0)
    return blocks


def team_layout():
    near = lax.axis_size("ctx")
    members = lax.axis_size(TEAM)
    direct = [offset for offset in range(members) if not offset & near]
    return near, direct, direct + [offset | near for offset in direct]


def gather_pieces(piece_for, *others):
    near, direct, _ = team_layout()
    pieces = [piece_for(0)]
    for offset in direct[:0:-1]:
        pieces.insert(1, swap(piece_for(offset), TEAM, offset))
    if others:
        pieces = [after(piece, *others) for piece in pieces]
    return pieces + [swap(piece, TEAM, near) for piece in pieces]


def near_sums(parts):
    keep, send_last, send_rest = parts
    near = team_layout()[0]
    last = swap(send_last, TEAM, near)
    rest = swap(send_rest, TEAM, near)
    split = send_rest.shape[0]
    return (
        keep[:split] + rest.astype(jnp.float32),
        keep[split:] + last.astype(jnp.float32),
    )


def direct_sums(sums):
    rest, last = sums
    _, direct, _ = team_layout()
    rows = last.shape[0]
    bands = [rest[place * rows : (place + 1) * rows] for place in range(len(direct) - 1)] + [last]
    total = bands[0]
    moved = [
        swap(part.astype(jnp.bfloat16), TEAM, offset)
        for offset, part in list(zip(direct, bands))[:0:-1]
    ]
    for part in moved:
        total = total + part.astype(jnp.float32)
    return total


def scatter_parts(value):
    rows = value.shape[0] // lax.axis_size(TEAM)
    half = value.shape[0] // 2
    sent = value[half:].astype(jnp.bfloat16)
    return value[:half], sent[half - rows :], sent[: half - rows]


def everyone_sum(value):
    for axis_name in ("rep", "ctx", "shard"):
        for bit in axis_bits(axis_name):
            value = value + swap(value, axis_name, bit)
    return value


def turned(values, cosine, sine):
    return values * cosine + pltpu.roll(values, HEAD_SIZE // 2, 1) * sine


def unit_rows(values):
    inverse = lax.rsqrt(jnp.mean(values * values, axis=-1, keepdims=True) + EPSILON)
    return (values * inverse, inverse)


def heads_of(projected_ref, cosine, sine, query_gain, key_gain, query_count):
    key_start = query_count * HEAD_SIZE
    queries = []
    for head in range(query_count):
        unit, inverse = unit_rows(projected_ref[:, head * HEAD_SIZE : (head + 1) * HEAD_SIZE])
        queries.append(
            (turned(unit * query_gain, cosine, sine).astype(jnp.bfloat16), unit, inverse)
        )
    key_unit, key_inverse = unit_rows(projected_ref[:, key_start : key_start + HEAD_SIZE])
    key_rot = turned(key_unit * key_gain, cosine, sine).astype(jnp.bfloat16)
    value_rows = projected_ref[:, key_start + HEAD_SIZE : key_start + 2 * HEAD_SIZE].astype(
        jnp.bfloat16
    )
    return queries, (key_rot, key_unit, key_inverse), value_rows


def probabilities(query_rot, key_rot, visible):
    scores = dot_right(query_rot, key_rot) * (1.0 / math.sqrt(HEAD_SIZE))
    scores = jnp.where(visible, scores, NEGATIVE)
    weights = jnp.exp(scores - jnp.max(scores, axis=-1, keepdims=True))
    return weights * (1.0 / jnp.sum(weights, axis=-1, keepdims=True))


def put_partial(value, first, keep_ref, last_ref, rest_ref):
    kept_rows, rest_rows = keep_ref.shape[0], rest_ref.shape[0]
    count = value.shape[0]
    if first < kept_rows:
        keep_ref[first : first + count, :] = value
        return
    start = first - kept_rows
    sent = value.astype(jnp.bfloat16)
    inside = max(0, min(count, rest_rows - start))
    if inside:
        rest_ref[start : start + inside, :] = sent[:inside]
    if inside < count:
        last_start = max(0, start - rest_rows)
        last_ref[last_start : last_start + count - inside, :] = sent[inside:]


def attend_kernel(
    normed_ref,
    cosine_ref,
    sine_ref,
    weights_ref,
    row_ref,
    column_ref,
    query_gain_ref,
    key_gain_ref,
    projected_ref,
    out_ref,
    keep_ref,
    last_ref,
    rest_ref,
):
    query_count = out_ref.shape[1] // HEAD_SIZE
    qkv_width = projected_ref.shape[1]
    length = row_ref.shape[0]
    visible = column_ref[...] <= row_ref[...]
    projected_ref[...] = plain_product(normed_ref[...], weights_ref[:, :qkv_width])
    for first in range(0, normed_ref.shape[0], length):
        rows = slice(first, first + length)
        queries, (key_rot, _, _), value_rows = heads_of(
            projected_ref.at[rows, :],
            cosine_ref[rows, :],
            sine_ref[rows, :],
            query_gain_ref[...],
            key_gain_ref[...],
            query_count,
        )
        for head in range(query_count):
            probs = probabilities(queries[head][0], key_rot, visible).astype(jnp.bfloat16)
            out_ref[rows, head * HEAD_SIZE : (head + 1) * HEAD_SIZE] = plain_product(
                probs, value_rows
            ).astype(jnp.bfloat16)
        put_partial(
            dot_right(out_ref[rows, :], weights_ref[:, qkv_width:]),
            first,
            keep_ref,
            last_ref,
            rest_ref,
        )


def feed_kernel(*refs):
    pieces = refs[:-8]
    (
        grads_ref,
        weights_ref,
        normed_ref,
        gate_up_grad_ref,
        hidden_ref,
        keep_ref,
        last_ref,
        rest_ref,
    ) = refs[-8:]
    hidden_width = hidden_ref.shape[1]
    height = pieces[0].shape[0]
    for place, piece in enumerate(pieces):
        normed_ref[place * height : (place + 1) * height, :] = piece[...]
    count = 2 * height
    for first in range(0, normed_ref.shape[0], count):
        rows = slice(first, first + count)
        gate_up = plain_product(normed_ref[rows, :], weights_ref[:, : 2 * hidden_width])
        gate_value = gate_up[:, :hidden_width]
        up_value = gate_up[:, hidden_width:]
        hidden_grad = plain_product(grads_ref[rows, :], weights_ref[:, 2 * hidden_width :])
        sigmoid_gate = jax.nn.sigmoid(gate_value)
        activated = gate_value * sigmoid_gate
        hidden_ref[rows, :] = (activated * up_value).astype(jnp.bfloat16)
        gate_up_grad_ref[rows, :hidden_width] = (
            hidden_grad * up_value * sigmoid_gate * (1.0 + gate_value * (1.0 - sigmoid_gate))
        ).astype(jnp.bfloat16)
        gate_up_grad_ref[rows, hidden_width:] = (hidden_grad * activated).astype(jnp.bfloat16)
        put_partial(
            dot_right(gate_up_grad_ref[rows, :], weights_ref[:, : 2 * hidden_width]),
            first,
            keep_ref,
            last_ref,
            rest_ref,
        )


def norm_back(gradient, unit, inverse, gain):
    gain_part = jnp.sum(gradient * unit, axis=0, keepdims=True)
    scaled = gradient * gain
    return (
        gain_part,
        inverse * (scaled - unit * jnp.mean(scaled * unit, axis=-1, keepdims=True)),
    )


def attend_back_kernel(*refs):
    pieces = refs[:-13]
    (
        projected_ref,
        attended_ref,
        cosine_ref,
        sine_ref,
        weights_ref,
        row_ref,
        column_ref,
        query_gain_ref,
        key_gain_ref,
        middle_grad_ref,
        out_ref,
        gain_ref,
        grads_ref,
    ) = refs[-13:]
    height = pieces[0].shape[0]
    qkv_width = projected_ref.shape[1]
    length = row_ref.shape[0]
    query_count = attended_ref.shape[1] // HEAD_SIZE
    key_start = query_count * HEAD_SIZE
    visible = column_ref[...] <= row_ref[...]
    scale = 1.0 / math.sqrt(HEAD_SIZE)
    for place, piece in enumerate(pieces):
        middle_grad_ref[place * height : (place + 1) * height, :] = piece[...]
    grads_ref[...] = plain_product(middle_grad_ref[...], weights_ref[:, qkv_width:]).astype(
        jnp.bfloat16
    )
    query_gain_part = jnp.zeros((1, HEAD_SIZE), jnp.float32)
    key_gain_part = jnp.zeros((1, HEAD_SIZE), jnp.float32)
    for first in range(0, projected_ref.shape[0], length):
        rows = slice(first, first + length)
        cosine = cosine_ref[rows, :]
        sine = sine_ref[rows, :]
        queries, (key_rot, key_unit, key_inverse), value_rows = heads_of(
            projected_ref.at[rows, :],
            cosine,
            sine,
            query_gain_ref[...],
            key_gain_ref[...],
            query_count,
        )
        key_grad = jnp.zeros(key_unit.shape, jnp.float32)
        value_grad = jnp.zeros(key_unit.shape, jnp.float32)
        for head in range(query_count):
            columns = slice(head * HEAD_SIZE, (head + 1) * HEAD_SIZE)
            query_rot, query_unit, query_inverse = queries[head]
            grads = grads_ref[rows, columns]
            row_delta = jnp.sum(
                grads.astype(jnp.float32) * attended_ref[rows, columns].astype(jnp.float32),
                axis=-1,
                keepdims=True,
            )
            prob_float = probabilities(query_rot, key_rot, visible)
            value_grad = value_grad + dot_left(prob_float.astype(jnp.bfloat16), grads)
            score_grad = (prob_float * (dot_right(grads, value_rows) - row_delta)).astype(
                jnp.bfloat16
            )
            query_grad = plain_product(score_grad, key_rot) * scale
            key_grad = key_grad + dot_left(score_grad, query_rot)
            part, query_pre = norm_back(
                turned(query_grad, cosine, -sine), query_unit, query_inverse, query_gain_ref[...]
            )
            query_gain_part = query_gain_part + part
            out_ref[rows, columns] = query_pre.astype(jnp.bfloat16)
        part, key_pre = norm_back(
            turned(key_grad * scale, cosine, -sine), key_unit, key_inverse, key_gain_ref[...]
        )
        key_gain_part = key_gain_part + part
        out_ref[rows, key_start : key_start + HEAD_SIZE] = key_pre.astype(jnp.bfloat16)
        out_ref[rows, key_start + HEAD_SIZE : key_start + 2 * HEAD_SIZE] = value_grad.astype(
            jnp.bfloat16
        )
    gain_ref[...] = jnp.zeros_like(gain_ref)
    gain_ref[0:1, :] = query_gain_part
    gain_ref[1:2, :] = key_gain_part


def whole_call(kernel, out_shapes, operands, scratch=(), flops=0):
    moved = sum(math.prod(shape) * jnp.dtype(kind).itemsize for shape, kind in out_shapes)
    moved += sum(array.size * array.dtype.itemsize for array in operands)
    return pl.pallas_call(
        kernel,
        in_specs=[pl.BlockSpec(memory_space=pltpu.VMEM)] * len(operands),
        out_specs=[pl.BlockSpec(memory_space=pltpu.VMEM)] * len(out_shapes),
        out_shape=[jax.ShapeDtypeStruct(shape, kind) for shape, kind in out_shapes],
        scratch_shapes=list(scratch),
        cost_estimate=pl.CostEstimate(flops=flops, transcendentals=0, bytes_accessed=moved),
    )(*operands)


def partial_shapes(rows, width, members):
    own = rows // members
    return [
        ((rows // 2, width), jnp.float32),
        ((own, width), jnp.bfloat16),
        ((rows // 2 - own, width), jnp.bfloat16),
    ]


def spread_kernel(member_ref, *refs, widths, offsets):
    blocks, out_refs = refs[: len(offsets)], refs[len(offsets) :]
    for block, offset in zip(blocks, offsets):
        place = member_ref[0] ^ offset
        start = 0
        for out_ref, width in zip(out_refs, widths):
            first = pl.multiple_of(place * width, width)
            out_ref[:, pl.ds(first, width)] = block[:, start : start + width].astype(jnp.float32)
            start += width


def spread_columns(blocks, member, widths):
    offsets = team_layout()[2]
    rows = blocks[0].shape[0]
    return pl.pallas_call(
        functools.partial(spread_kernel, widths=widths, offsets=offsets),
        in_specs=[pl.BlockSpec(memory_space=pltpu.SMEM)]
        + [pl.BlockSpec(memory_space=pltpu.VMEM)] * len(blocks),
        out_specs=[pl.BlockSpec(memory_space=pltpu.VMEM)] * len(widths),
        out_shape=[
            jax.ShapeDtypeStruct((rows, size * len(blocks)), jnp.float32) for size in widths
        ],
    )(member.reshape(1), *blocks)


def per_device(
    tokens,
    out_grad,
    positions,
    stretch_order,
    attn_gain,
    query_gain,
    key_norm_gain,
    query_weight,
    key_projection_matrix,
    value_projection_matrix,
    output_weight,
    ffn_gain,
    gate_weight,
    up_weight,
    down_weight,
):
    sequence_batch, count_of_rows, model_width = tokens.shape
    local_rows = sequence_batch * count_of_rows
    team = lax.axis_size(TEAM)
    ctx_size = lax.axis_size("ctx")
    ctx_place = lax.axis_index("ctx")
    member = lax.axis_index(TEAM)
    axis_offsets = [1 << bit for bit in range(team.bit_length() - 1)]
    query_width = QUERY_HEADS // team * HEAD_SIZE
    kv_width = KEY_VALUE_HEADS // team * HEAD_SIZE
    hidden_width = gate_weight.shape[1] // team
    own_rows = model_width // lax.axis_size(OWNERS)
    own_start = lax.axis_index(OWNERS) * own_rows

    def ctx_columns(matrices, place):
        start_member = lax.axis_index("rep") * ctx_size + place
        pieces = []
        for matrix in matrices:
            width = matrix.shape[1] // team
            pieces.append(
                lax.dynamic_slice_in_dim(matrix, start_member * width, width, axis=1)
            )
        return jnp.concatenate(pieces, axis=1)

    def ctx_exchange(pick, axis, *others):
        received = [pick(ctx_place)]
        for offset in range(1, ctx_size):
            received.append(swap(after(pick(ctx_place ^ offset), *others), "ctx", offset))
        if ctx_size == 1:
            return received[0]
        if ctx_size == 2:
            return jnp.where(
                ctx_place == 0,
                jnp.concatenate(received, axis=axis),
                jnp.concatenate(received[::-1], axis=axis),
            )
        stacked = jnp.stack(received)
        return jnp.concatenate(
            [
                lax.dynamic_index_in_dim(stacked, ctx_place ^ place, 0, keepdims=False)
                for place in range(ctx_size)
            ],
            axis=axis,
        )

    def team_rows(matrices, *others):
        return ctx_exchange(lambda place: ctx_columns(matrices, place), 0, *others)

    def all_rows(rows):
        return lax.all_gather(rows, "shard", axis=0, tiled=True)

    attn_part = team_rows(
        [query_weight, key_projection_matrix, value_projection_matrix, output_weight]
    )
    ffn_part = team_rows([gate_weight, up_weight, down_weight], attn_part)
    attn_weights = all_rows(attn_part)
    ffn_weights = all_rows(ffn_part)
    qkv_width = query_width + 2 * kv_width
    full_qkv = attn_weights[:, :qkv_width]
    full_down = ffn_weights[:, 2 * hidden_width :]
    owners = lax.axis_size(OWNERS)
    gain_blocks = gather_plain(
        jnp.stack([attn_gain, ffn_gain]),
        OWNERS, [1 << bit for bit in range(owners.bit_length() - 1)]
    )
    owner_places = jnp.arange(owners, dtype=jnp.int32)
    from_block = (owner_places[:, None] ^ lax.axis_index(OWNERS)) == owner_places[None, :]
    gains = jnp.einsum(
        "jk,kgf->gjf",
        from_block.astype(jnp.bfloat16),
        gain_blocks,
        preferred_element_type=jnp.float32,
    ).reshape(2, 1, model_width)
    full_gain = gains[0]
    full_ffn_gain = gains[1]

    own_tokens = tokens.reshape(local_rows, model_width)
    own_grads = out_grad.reshape(local_rows, model_width)
    token_source = after(own_tokens, attn_part)
    token_pieces = gather_pieces(lambda offset: token_source)
    all_tokens = jnp.concatenate(token_pieces, axis=0)
    grad_source = after(own_grads, *token_pieces)
    total_rows = all_tokens.shape[0]
    assert sequence_batch == 1

    half_size = HEAD_SIZE // 2
    freq_steps = jnp.arange(HEAD_SIZE, dtype=jnp.int32)
    inverse = jnp.exp(
        (freq_steps % half_size).astype(jnp.float32) * (-2.0 * math.log(ROPE_THETA) / HEAD_SIZE)
    )
    all_positions = gather_plain(
        after(positions, token_pieces[1]),
        TEAM,
        [bit for bit in axis_offsets if bit != ctx_size] + [ctx_size],
    ).reshape(total_rows)
    angles = all_positions.astype(jnp.float32)[:, None] * inverse[None, :]
    tables = (
        jnp.cos(angles),
        jnp.sin(angles) * jnp.where(freq_steps < half_size, -1.0, 1.0)[None, :],
    )

    stretches_here = stretch_order.shape[0] // ctx_size
    block_rows = count_of_rows // stretches_here
    local = jnp.arange(count_of_rows, dtype=jnp.int32)
    match = (local // block_rows)[:, None] == jnp.arange(stretches_here, dtype=jnp.int32)[None]

    def stored_index(place):
        blocks = lax.dynamic_slice_in_dim(stretch_order, place * stretches_here, stretches_here)
        return (
            jnp.sum(jnp.where(match, blocks[None, :], 0), axis=1) * block_rows + local % block_rows
        )

    seq_index = jnp.concatenate([stored_index(ctx_place ^ offset) for offset in range(ctx_size)])
    small = (
        seq_index[:, None],
        seq_index[None, :],
        query_gain.astype(jnp.float32)[None, :],
        key_norm_gain.astype(jnp.float32)[None, :],
    )

    float_tokens = all_tokens.astype(jnp.float32)
    inv_first_all = lax.rsqrt(
        jnp.mean(float_tokens * float_tokens, axis=1, keepdims=True) + EPSILON
    )
    unit_first_all = float_tokens * inv_first_all
    first_normalized = (unit_first_all * full_gain).astype(jnp.bfloat16)
    flat_tokens = own_tokens.astype(jnp.float32)
    inv_first = inv_first_all[:local_rows]
    unit_first = flat_tokens * inv_first
    bfloat = jnp.bfloat16
    projected, attended, *output_parts = whole_call(
        attend_kernel,
        [((total_rows, qkv_width), jnp.float32), ((total_rows, query_width), bfloat)]
        + partial_shapes(total_rows, model_width, team),
        [after(first_normalized, ffn_part), *tables, attn_weights, *small],
        flops=FLOPS_HINT,
    )
    grad_pieces = gather_pieces(lambda offset: grad_source, attended)
    all_grads = jnp.concatenate(grad_pieces, axis=0)
    middle = flat_tokens + direct_sums(near_sums(output_parts))
    inv_second = lax.rsqrt(jnp.mean(middle * middle, axis=1, keepdims=True) + EPSILON)
    unit_second = middle * inv_second
    normed_own = (unit_second * full_ffn_gain).astype(bfloat)
    normed_pieces = gather_pieces(lambda offset: normed_own)
    normed_second, gate_up_grad, hidden, *second_parts = whole_call(
        feed_kernel,
        [
            ((total_rows, model_width), bfloat),
            ((total_rows, 2 * hidden_width), bfloat),
            ((total_rows, hidden_width), bfloat),
        ]
        + partial_shapes(total_rows, model_width, team),
        [*normed_pieces, all_grads, ffn_weights],
        flops=FLOPS_HINT,
    )

    def joined_products(pairs):
        return jnp.concatenate(
            [dot_left(left, right).astype(jnp.bfloat16) for left, right in pairs], axis=1
        )

    def shard_sum(rows):
        return lax.psum_scatter(rows, "shard", scatter_dimension=0, tiled=True)

    second_sums = near_sums(second_parts)
    ffn_terms = joined_products(
        [(normed_second, after(gate_up_grad, *second_sums)), (all_grads, hidden)]
    )
    ffn_rows = shard_sum(ffn_terms)
    normed_grad_second = after(direct_sums(second_sums), ffn_terms)
    ffn_gain_part = jnp.sum(normed_grad_second * unit_second, axis=0)
    unit_grad_second = normed_grad_second * full_ffn_gain
    middle_grad = own_grads.astype(jnp.float32) + inv_second * (
        unit_grad_second
        - unit_second * jnp.mean(unit_grad_second * unit_second, axis=1, keepdims=True)
    )
    grad_own = middle_grad.astype(bfloat)
    middle_pieces = gather_pieces(lambda offset: grad_own)
    down_partial = dot_right(after(hidden, grad_own), full_down)
    down_parts = scatter_parts(down_partial)
    down_sums = near_sums(down_parts)
    middle_grad_b, projected_grad, norm_gain_parts = whole_call(
        attend_back_kernel,
        [
            ((total_rows, model_width), bfloat),
            ((total_rows, qkv_width), bfloat),
            ((8, HEAD_SIZE), jnp.float32),
        ],
        [
            *middle_pieces[:-1],
            after(middle_pieces[-1], *down_sums),
            projected,
            attended,
            *tables,
            attn_weights,
            *small,
        ],
        [pltpu.VMEM((total_rows, query_width), bfloat)],
        flops=FLOPS_HINT,
    )
    block_sum = middle + direct_sums(down_sums)
    block_out = block_sum.astype(bfloat).reshape(sequence_batch, count_of_rows, model_width)

    def rows_for(rows):
        return lambda offset: lax.dynamic_slice_in_dim(
            rows, (ctx_place ^ (offset % ctx_size)) * own_rows, own_rows
        )

    projected_grad = after(projected_grad, ffn_rows)
    ffn_pieces = gather_pieces(rows_for(ffn_rows))
    attn_terms = joined_products([(first_normalized, projected_grad), (middle_grad_b, attended)])
    attn_rows = shard_sum(attn_terms)
    first_partial = dot_right(after(projected_grad, attn_terms), full_qkv)
    attn_gain_part = jnp.sum(first_partial * unit_first_all, axis=0)
    normed_grad_first = direct_sums(near_sums(scatter_parts(first_partial)))
    unit_grad_first = normed_grad_first * full_gain
    tokens_grad = middle_grad + inv_first * (
        unit_grad_first - unit_first * jnp.mean(unit_grad_first * unit_first, axis=1, keepdims=True)
    )
    gain_totals = everyone_sum(
        jnp.concatenate(
            [
                attn_gain_part.reshape(-1, HEAD_SIZE),
                ffn_gain_part.reshape(-1, HEAD_SIZE),
                norm_gain_parts,
            ],
            axis=0,
        )
    )
    gain_rows = model_width // HEAD_SIZE
    attn_gain_grad = lax.dynamic_slice_in_dim(
        gain_totals[:gain_rows].reshape(model_width), own_start, own_rows
    )
    ffn_gain_grad = lax.dynamic_slice_in_dim(
        gain_totals[gain_rows : 2 * gain_rows].reshape(model_width), own_start, own_rows
    )

    ffn_outs = spread_columns(ffn_pieces, member, [hidden_width] * 3)
    gate_weight_grad, up_weight_grad, down_weight_grad = ffn_outs
    attn_rows = after(attn_rows, *ffn_outs, tokens_grad, gain_totals, block_out)
    query_weight_grad, key_weight_grad, value_weight_grad, output_weight_grad = spread_columns(
        gather_pieces(rows_for(attn_rows)),
        member,
        [query_width, kv_width, kv_width, query_width],
    )
    return (
        block_out,
        tokens_grad.reshape(sequence_batch, count_of_rows, model_width),
        query_weight_grad,
        key_weight_grad,
        value_weight_grad,
        output_weight_grad,
        gate_weight_grad,
        up_weight_grad,
        down_weight_grad,
        attn_gain_grad,
        ffn_gain_grad,
        gain_totals[2 * gain_rows],
        gain_totals[2 * gain_rows + 1],
    )


def solution(mesh):
    in_specs = (
        P(("rep", "shard"), "ctx", None),
        P(("rep", "shard"), "ctx", None),
        P(("rep", "shard"), "ctx"),
        P(),
        P(("shard", "ctx")),
        P(),
        P(),
        P(("shard", "ctx"), None),
        P(("shard", "ctx"), None),
        P(("shard", "ctx"), None),
        P(("shard", "ctx"), None),
        P(("shard", "ctx")),
        P(("shard", "ctx"), None),
        P(("shard", "ctx"), None),
        P(("shard", "ctx"), None),
    )
    out_specs = (
        P(("rep", "shard"), "ctx", None),
        P(("rep", "shard"), "ctx", None),
        P(("shard", "ctx"), None),
        P(("shard", "ctx"), None),
        P(("shard", "ctx"), None),
        P(("shard", "ctx"), None),
        P(("shard", "ctx"), None),
        P(("shard", "ctx"), None),
        P(("shard", "ctx"), None),
        P(("shard", "ctx")),
        P(("shard", "ctx")),
        P(),
        P(),
    )

    return jax.shard_map(
        per_device, mesh=mesh, in_specs=in_specs, out_specs=out_specs, check_vma=False
    )
```

time: 322 us -> 283 us (0.88)
  local copies, waits for them, and re-layouts: 46.8 us -> 25.3 us
  blocking collectives: 20.8 us -> 0 us
  other arithmetic: 44.7 us -> 28.5 us
  matrix products: 32.8 us -> 19.1 us
  starting transfers between devices: 50.8 us -> 64 us
  waiting for transfers between devices: 79.2 us -> 91.9 us
  Pallas kernels: 29.8 us -> 38.2 us
    all_gather x1 -> x0, blocking collectives: 20.8 us -> none  [per_device(): lax.all_gather(jnp.stack([attn_gain, ffn_gain]), OWNERS, axis=1, tiled=True)]
    unnamed x120 -> x94, local copies, waits for them, and re-layouts: 27.6 us -> 10.8 us
    concatenate x23 -> x4, other arithmetic: 15.7 us -> 0.02 us  [gather_plain(): blocks = jnp.concatenate([blocks, swap(blocks, axes, offset)], axis=0)]
    ppermute x64 -> x75, starting transfers between devices: 50.6 us -> 63.7 us  [swap(): return lax.ppermute(value, axes, pairs)]
    dot_general x4 -> x1, matrix products: 13.2 us -> 0.19 us  [per_device(): jnp.einsum('jk,kgf->gjf', from_block.astype(jnp.bfloat16), gain_blocks, p...]
    ppermute x64 -> x75, waiting for transfers between devices: 79.1 us -> 91.8 us  [swap(): return lax.ppermute(value, axes, pairs)]
    pallas_call x4 -> x5, Pallas kernels: 29.8 us -> 38.2 us  [the longest x3 30.8 us: whole_call(): pl.pallas_call(kernel, in_specs=[pl.BlockSpec(memory_space=pltpu.VMEM)] *...]
    convert_element_type x0 -> x5, other arithmetic: none -> 5.19 us  [the longest x2 2.92 us: direct_sums(): part.astype(jnp.bfloat16)]
  transfers between devices with their start and end apart: 68 -> 79, of which waited for: 30 -> 31; matrix products, arithmetic and copies ran while one was open for 28% -> 19% of each run, Pallas kernels for 7% -> 9%
where the time goes in v3:
time: 283 us; the launch traced here: 282 us
  waiting for transfers between devices  91.9 us (32%)
  starting transfers between devices  64 us (23%)
  Pallas kernels  38.2 us (13%)
  other arithmetic  28.5 us (10%)
  local copies, waits for them, and re-layouts  25.3 us (9%)
  matrix products  19.1 us (7%)
  between operations  14.6 us (5%)
    ppermute x75, waiting for transfers between devices, swap(): return lax.ppermute(value, axes, pairs)  91.8 us
    ppermute x75, starting transfers between devices, swap(): return lax.ppermute(value, axes, pairs)  63.7 us
    pallas_call x3, Pallas kernels, whole_call(): pl.pallas_call(kernel, in_specs=[pl.BlockSpec(memory_space=pltpu.VMEM)] *...  30.8 us
    dot_general x4, matrix products, dot_left(): lax.dot_general(left_side, right_side, (((0,), (0,)), ((), ())), preferre...  11.5 us
    unnamed x94, local copies, waits for them, and re-layouts  10.8 us
    dot_general x2, matrix products, dot_right(): lax.dot_general(left_side, right_side, (((1,), (1,)), ((), ())), preferre...  7.43 us
    pallas_call x2, Pallas kernels, spread_columns(): pl.pallas_call(functools.partial(spread_kernel, widths=widths, offsets=of...  7.4 us
    another operation x4, other arithmetic  7.1 us
  transfers between devices with their start and end apart: 79, of which 31 were waited for; matrix products, arithmetic and copies ran while one was open for 19% of the time, Pallas kernels for 9%

profile of v3, /device:TPU:0, one launch (start us, length us, event | category | flops | bytes accessed | tf_op | source)
XLA Modules:
  0.0 281.7 jit_solution(13232261092690111451)
XLA Ops:
  31.7 4.0 %collective-permute-done.1 = bf16[128,1024]{1,0:T(8,128)(2,1)} collective-permute-done((bf16[128,1024]{1,0:T(8,128)(2,1)S(1)}, bf16[128,1024]{1,0:T(8,128)(2,1)}, u32[]{:S(2)}, u32[]{:S(2)}) %collective-permute-start.1) | collective-permute-done | bytes 262176 | tf_op jit(solution)/shard_map/ppermute | solution.py:48
  38.3 5.4 %collective-permute-done.12 = s32[1,1,128]{2,1,0:T(1,128)S(1)} collective-permute-done((s32[1,1,128]{2,1,0:T(1,128)S(1)}, s32[1,1,128]{2,1,0:T(1,128)S(1)}, u32[]{:S(2)}, u32[]{:S(2)}) %collective-permute-start.12) | collective-permute-done | bytes 544 | tf_op jit(solution)/shard_map/ppermute | solution.py:48
  58.7 10.1 %shard_map.246 = (f32[1024,512]{1,0:T(8,128)}, bf16[1024,256]{1,0:T(8,128)(2,1)}, f32[512,1024]{1,0:T(8,128)}, bf16[128,1024]{1,0:T(8,128)(2,1)}, bf16[384,1024]{1,0:T(8,128)(2,1)}) custom-call(bf16[1024,1024]{1,0:T(8,128)(2,1)} %fusion.2.normed_ref, f32[1024,128]{1,0:T(8,128)} %get-tuple-element.138.cosine_ref.refs_10_, ...), custom_call_target="tpu_custom_call" | custom-call | flops 8000000000 | bytes 10488832 | tf_op jit(solution)/shard_map/pallas_call | solution.py:342
  80.6 5.0 %collective-permute-done.17 = bf16[128,1024]{1,0:T(8,128)(2,1)S(1)} collective-permute-done((bf16[128,1024]{1,0:T(8,128)(2,1)S(1)}, bf16[128,1024]{1,0:T(8,128)(2,1)S(1)}, u32[]{:S(2)}, u32[]{:S(2)}) %collective-permute-start.17) | collective-permute-done | bytes 262176 | tf_op jit(solution)/shard_map/ppermute | solution.py:48
  85.6 5.1 %collective-permute-done.18 = bf16[128,1024]{1,0:T(8,128)(2,1)S(1)} collective-permute-done((bf16[128,1024]{1,0:T(8,128)(2,1)S(1)}, bf16[128,1024]{1,0:T(8,128)(2,1)S(1)}, u32[]{:S(2)}, u32[]{:S(2)}) %collective-permute-start.18) | collective-permute-done | bytes 262176 | tf_op jit(solution)/shard_map/ppermute | solution.py:48
  93.2 3.6 %collective-permute-done.29 = bf16[128,1024]{1,0:T(8,128)(2,1)S(1)} collective-permute-done((bf16[128,1024]{1,0:T(8,128)(2,1)S(1)}, bf16[128,1024]{1,0:T(8,128)(2,1)S(1)}, u32[]{:S(2)}, u32[]{:S(2)}) %collective-permute-start.29) | collective-permute-done | bytes 262176 | tf_op jit(solution)/shard_map/ppermute | solution.py:48
  102.6 6.3 %collective-permute-done.21.refs_2_ = bf16[128,1024]{1,0:T(8,128)(2,1)} collective-permute-done((bf16[128,1024]{1,0:T(8,128)(2,1)S(1)}, bf16[128,1024]{1,0:T(8,128)(2,1)}, u32[]{:S(2)}, u32[]{:S(2)}) %collective-permute-start.21) | collective-permute-done | bytes 262176 | tf_op jit(solution)/shard_map/ppermute | solution.py:48
  111.1 9.6 %shard_map.247 = (bf16[1024,1024]{1,0:T(8,128)(2,1)}, bf16[1024,768]{1,0:T(8,128)(2,1)}, bf16[1024,384]{1,0:T(8,128)(2,1)}, f32[512,1024]{1,0:T(8,128)}, bf16[12...) custom-call(bf16[128,1024]{1,0:T(8,128)(2,1)} %copy-done.14, bf16[128,1024]{1,0:T(8,128)(2,1)} %collective-permute-done.20.refs_1_, ...), custom_call_target="tpu_custom_call" | custom-call | flops 8000000000 | bytes 14155776 | tf_op jit(solution)/shard_map/pallas_call | solution.py:342
  121.2 3.2 %convolution_convert_fusion.2 = bf16[1024,384]{1,0:T(8,128)(2,1)S(1)} fusion(bf16[1024,1024]{1,0:T(8,128)(2,1)} %copy-done.23, bf16[1024,384]{1,0:T(8,128)(2,1)} %get-tuple-element.71), kind=kOutput, calls=%fused_computation.15 | convolution fusion | flops 805699584 | bytes 3670016 | tf_op jit(solution)/shard_map/dot_general | solution.py:35
  135.7 5.5 %collective-permute-done.36 = bf16[128,1024]{1,0:T(8,128)(2,1)S(1)} collective-permute-done((bf16[128,1024]{1,0:T(8,128)(2,1)S(1)}, bf16[128,1024]{1,0:T(8,128)(2,1)S(1)}, u32[]{:S(2)}, u32[]{:S(2)}) %collective-permute-start.36) | collective-permute-done | bytes 262176 | tf_op jit(solution)/shard_map/ppermute | solution.py:48
  141.2 4.7 %collective-permute-done.37 = bf16[128,1024]{1,0:T(8,128)(2,1)S(1)} collective-permute-done((bf16[128,1024]{1,0:T(8,128)(2,1)S(1)}, bf16[128,1024]{1,0:T(8,128)(2,1)S(1)}, u32[]{:S(2)}, u32[]{:S(2)}) %collective-permute-start.37) | collective-permute-done | bytes 262176 | tf_op jit(solution)/shard_map/ppermute | solution.py:48
  154.5 6.6 %collective-permute-done.46.refs_3_ = bf16[128,1024]{1,0:T(8,128)(2,1)S(1)} collective-permute-done((bf16[128,1024]{1,0:T(8,128)(2,1)S(1)}, bf16[128,1024]{1,0:T(8,128)(2,1)S(1)}, u32[]{:S(2)}, u32[]{:S(2)}) %collective-permute-start.46) | collective-permute-done | bytes 262176 | tf_op jit(solution)/shard_map/ppermute | solution.py:48
  161.1 4.7 %collective-permute-done.44.refs_1_ = bf16[128,1024]{1,0:T(8,128)(2,1)S(1)} collective-permute-done((bf16[128,1024]{1,0:T(8,128)(2,1)S(1)}, bf16[128,1024]{1,0:T(8,128)(2,1)S(1)}, u32[]{:S(2)}, u32[]{:S(2)}) %collective-permute-start.44) | collective-permute-done | bytes 262176 | tf_op jit(solution)/shard_map/ppermute | solution.py:48
  170.5 11.1 %shard_map.248 = (bf16[1024,1024]{1,0:T(8,128)(2,1)}, bf16[1024,512]{1,0:T(8,128)(2,1)}, f32[8,128]{1,0:T(8,128)}) custom-call(bf16[128,1024]{1,0:T(8,128)(2,1)} %copy-done.15, bf16[128,1024]{1,0:T(8,128)(2,1)} %copy-done.32, bf16[128,1024]{1,0:T(8,128)(2,1)} %copy-done.33, bf16[128,1024]{1,0:T(8,128)(2,1)} %copy-done.31, bf16[128,1024]{1,0:T(8,128)(2,1)} %copy-done.34, ...), custom_call_target="tpu_custom_call" | custom-call | flops 8000000000 | bytes 10492928 | tf_op jit(solution)/shard_map/pallas_call | solution.py:342
  181.6 3.2 %convolution_convert_fusion.3 = bf16[1024,256]{1,0:T(8,128)(2,1)} fusion(bf16[1024,1024]{1,0:T(8,128)(2,1)} %get-tuple-element.76, bf16[1024,256]{1,0:T(8,128)(2,1)} %get-tuple-element.58.refs_9_), kind=kOutput, calls=%fused_computation.16 | convolution fusion | flops 537133056 | bytes 3145728 | tf_op jit(solution)/shard_map/dot_general | solution.py:35
  184.8 3.2 %convolution_convert_fusion.1 = bf16[1024,512]{1,0:T(8,128)(2,1)S(1)} fusion(bf16[1024,1024]{1,0:T(8,128)(2,1)} %fusion.2.normed_ref, bf16[1024,512]{1,0:T(8,128)(2,1)} %get-tuple-element.77), kind=kOutput, calls=%fused_computation.14 | convolution fusion | flops 1074266112 | bytes 4194304 | tf_op jit(solution)/shard_map/dot_general | solution.py:35
  189.4 4.9 %fusion.3 = (f32[1024]{0:T(1024)S(1)}, bf16[1024,1024]{1,0:T(8,128)(2,1)S(1)}, f32[1024,1024]{1,0:T(8,128)}) fusion(bf16[1024,1024]{1,0:T(8,128)(2,1)S(1)} %constant_dynamic-update-slice_fusion, f32[1024]{0:T(1024)S(1)} %add_rsqrt_fusion, bf16[1024,512]{1,0:T(8,128)(2,1)} %get-tuple-element.77, ...), kind=kOutput, calls=%fused_computation.5 | convolution fusion | flops 1078983680 | bytes 10493952 | tf_op jit(solution)/shard_map/dot_general | solution.py:29
  212.2 3.8 %collective-permute-done.56.refs_1_ = bf16[128,1152]{1,0:T(8,128)(2,1)S(1)} collective-permute-done((bf16[128,1152]{1,0:T(8,128)(2,1)S(1)}, bf16[128,1152]{1,0:T(8,128)(2,1)S(1)}, u32[]{:S(2)}, u32[]{:S(2)}) %collective-permute-start.56) | collective-permute-done | bytes 294944 | tf_op jit(solution)/shard_map/ppermute | solution.py:48
  234.1 4.0 %shard_map.249 = (f32[128,3072]{1,0:T(8,128)}, f32[128,3072]{1,0:T(8,128)}, f32[128,3072]{1,0:T(8,128)}) custom-call(s32[1]{0:T(128)} %bitcast.19.member_ref, bf16[128,1152]{1,0:T(8,128)(2,1)} %copy-done.6, bf16[128,1152]{1,0:T(8,128)(2,1)} %copy-done.11, bf16[128,1152]{1,0:T(8,128)(2,1)} %collective-permute-done.57.refs_2_, ...), custom_call_target="tpu_custom_call" | custom-call | tf_op jit(solution)/shard_map/pallas_call | solution.py:375
  242.7 4.4 %collective-permute-done.41 = bf16[128,1024]{1,0:T(8,128)(2,1)} collective-permute-done((bf16[128,1024]{1,0:T(8,128)(2,1)}, bf16[128,1024]{1,0:T(8,128)(2,1)}, u32[]{:S(2)}, u32[]{:S(2)}) %collective-permute-start.41) | collective-permute-done | bytes 262176 | tf_op jit(solution)/shard_map/ppermute | solution.py:48
  247.1 4.6 %collective-permute-done.42 = bf16[128,1024]{1,0:T(8,128)(2,1)} collective-permute-done((bf16[128,1024]{1,0:T(8,128)(2,1)}, bf16[128,1024]{1,0:T(8,128)(2,1)}, u32[]{:S(2)}, u32[]{:S(2)}) %collective-permute-start.42) | collective-permute-done | bytes 262176 | tf_op jit(solution)/shard_map/ppermute | solution.py:48
  260.2 3.1 %collective-permute-done.68.refs_1_ = bf16[128,768]{1,0:T(8,128)(2,1)S(1)} collective-permute-done((bf16[128,768]{1,0:T(8,128)(2,1)S(1)}, bf16[128,768]{1,0:T(8,128)(2,1)S(1)}, u32[]{:S(2)}, u32[]{:S(2)}) %collective-permute-start.68) | collective-permute-done | bytes 196640 | tf_op jit(solution)/shard_map/ppermute | solution.py:48
  263.3 5.7 %collective-permute-done.69.refs_2_ = bf16[128,768]{1,0:T(8,128)(2,1)S(1)} collective-permute-done((bf16[128,768]{1,0:T(8,128)(2,1)S(1)}, bf16[128,768]{1,0:T(8,128)(2,1)S(1)}, u32[]{:S(2)}, u32[]{:S(2)}) %collective-permute-start.69) | collective-permute-done | bytes 196640 | tf_op jit(solution)/shard_map/ppermute | solution.py:48
  271.8 3.4 %shard_map.250 = (f32[128,2048]{1,0:T(8,128)}, f32[128,1024]{1,0:T(8,128)}, f32[128,1024]{1,0:T(8,128)}, f32[128,2048]{1,0:T(8,128)}) custom-call(s32[1]{0:T(128)} %bitcast.19.member_ref, bf16[128,768]{1,0:T(8,128)(2,1)} %copy-done.8, bf16[128,768]{1,0:T(8,128)(2,1)} %copy-done.16, bf16[128,768]{1,0:T(8,128)(2,1)} %copy-done.18, ...), custom_call_target="tpu_custom_call" | custom-call | tf_op jit(solution)/shard_map/pallas_call | solution.py:375
  (316 shorter events, 141.8 us)
Async XLA Ops:
  7.2 51.4 %all-gather.3.cloned.1.call-start = ((), (), s32[]{:S(2)}) async-start(), calls=%async_computation.2 | async-start | bytes 1966080 | tf_op jit(solution)/shard_map/all_gather | solution.py:451
  18.0 92.8 %all-gather.5.cloned.1.call-start = ((), (), s32[]{:S(2)}) async-start(), calls=%async_computation.3 | async-start | bytes 2949120 | tf_op jit(solution)/shard_map/all_gather | solution.py:451
  29.7 14.0 %collective-permute-start.3 = (bf16[128,1024]{1,0:T(8,128)(2,1)S(1)}, bf16[128,1024]{1,0:T(8,128)(2,1)S(1)}, u32[]{:S(2)}, u32[]{:S(2)}) collective-permute-start(bf16[128,1024]{1,0:T(8,128)(2,1)S(1)} %bitcast.60), channel_id=1, source_target_pairs={{0,17},{1,16},{8,25},{9,24},{16,1},{17,0},{24,9},{25,8},{2,19},{3,... | collective-permute-start | bytes 786440 | tf_op jit(solution)/shard_map/ppermute | solution.py:48
  29.9 17.4 %collective-permute-start.4 = (bf16[128,1024]{1,0:T(8,128)(2,1)S(1)}, bf16[128,1024]{1,0:T(8,128)(2,1)S(1)}, u32[]{:S(2)}, u32[]{:S(2)}) collective-permute-start(bf16[128,1024]{1,0:T(8,128)(2,1)S(1)} %bitcast.61), channel_id=1, source_target_pairs={{0,8},{1,9},{8,0},{9,1},{16,24},{17,25},{24,16},{25,17},{2,10},{3,... | collective-permute-start | bytes 786440 | tf_op jit(solution)/shard_map/ppermute | solution.py:48
  29.9 22.1 %collective-permute-start.11 = (bf16[128,1152]{1,0:T(8,128)(2,1)S(1)}, bf16[128,1152]{1,0:T(8,128)(2,1)S(1)}, u32[]{:S(2)}, u32[]{:S(2)}) collective-permute-start(bf16[128,1152]{1,0:T(8,128)(2,1)S(1)} %pad_maximum_fusion.2), channel_id=1, source_target_pairs={{0,1},{1,0},{2,3},{3,2},{4,5},{5,4},{6,7},{7,6},{8,9},{9,8},{10,11... | collective-permute-start | bytes 884744 | tf_op jit(solution)/shard_map/ppermute | solution.py:48
  38.2 15.1 %collective-permute-start.5 = (bf16[128,1024]{1,0:T(8,128)(2,1)}, bf16[128,1024]{1,0:T(8,128)(2,1)}, u32[]{:S(2)}, u32[]{:S(2)}) collective-permute-start(bf16[128,1024]{1,0:T(8,128)(2,1)} %collective-permute-done.1), channel_id=1, source_target_pairs={{0,8},{1,9},{8,0},{9,1},{16,24},{17,25},{24,16},{25,17},{2,10},{3,... | collective-permute-start | bytes 786440 | tf_op jit(solution)/shard_map/ppermute | solution.py:48
  53.0 131.8 %reduce-scatter.3.cloned.1.call-start = ((), (), s32[]{:S(2)}) async-start(), calls=%async_computation.4 | async-start | bytes 2949120 | tf_op jit(solution)/shard_map/reduce_scatter | solution.py:564
  77.0 13.7 %collective-permute-start.18 = (bf16[128,1024]{1,0:T(8,128)(2,1)S(1)}, bf16[128,1024]{1,0:T(8,128)(2,1)S(1)}, u32[]{:S(2)}, u32[]{:S(2)}) collective-permute-start(bf16[128,1024]{1,0:T(8,128)(2,1)S(1)} %get-tuple-element.109), channel_id=1, source_target_pairs={{0,16},{1,17},{8,24},{9,25},{16,0},{17,1},{24,8},{25,9},{2,18},{3,... | collective-permute-start | bytes 786440 | tf_op jit(solution)/shard_map/ppermute | solution.py:48
  77.6 13.6 %collective-permute-start.19 = (bf16[128,1024]{1,0:T(8,128)(2,1)S(1)}, bf16[128,1024]{1,0:T(8,128)(2,1)S(1)}, u32[]{:S(2)}, u32[]{:S(2)}) collective-permute-start(bf16[128,1024]{1,0:T(8,128)(2,1)S(1)} %get-tuple-element.110), channel_id=1, source_target_pairs={{0,1},{1,0},{8,9},{9,8},{16,17},{17,16},{24,25},{25,24},{2,3},{3,2... | collective-permute-start | bytes 786440 | tf_op jit(solution)/shard_map/ppermute | solution.py:48
  78.7 18.1 %collective-permute-start.29 = (bf16[128,1024]{1,0:T(8,128)(2,1)S(1)}, bf16[128,1024]{1,0:T(8,128)(2,1)S(1)}, u32[]{:S(2)}, u32[]{:S(2)}) collective-permute-start(bf16[128,1024]{1,0:T(8,128)(2,1)S(1)} %bitcast.65), channel_id=1, source_target_pairs={{0,17},{1,16},{8,25},{9,24},{16,1},{17,0},{24,9},{25,8},{2,19},{3,... | collective-permute-start | bytes 786440 | tf_op jit(solution)/shard_map/ppermute | solution.py:48
  80.5 17.8 %collective-permute-start.30 = (bf16[128,1024]{1,0:T(8,128)(2,1)S(1)}, bf16[128,1024]{1,0:T(8,128)(2,1)S(1)}, u32[]{:S(2)}, u32[]{:S(2)}) collective-permute-start(bf16[128,1024]{1,0:T(8,128)(2,1)S(1)} %bitcast.66), channel_id=1, source_target_pairs={{0,8},{1,9},{8,0},{9,1},{16,24},{17,25},{24,16},{25,17},{2,10},{3,... | collective-permute-start | bytes 786440 | tf_op jit(solution)/shard_map/ppermute | solution.py:48
  85.6 14.2 %collective-permute-start.31 = (bf16[128,1024]{1,0:T(8,128)(2,1)S(1)}, bf16[128,1024]{1,0:T(8,128)(2,1)S(1)}, u32[]{:S(2)}, u32[]{:S(2)}) collective-permute-start(bf16[128,1024]{1,0:T(8,128)(2,1)S(1)} %collective-permute-done.27), channel_id=1, source_target_pairs={{0,8},{1,9},{8,0},{9,1},{16,24},{17,25},{24,16},{25,17},{2,10},{3,... | collective-permute-start | bytes 786440 | tf_op jit(solution)/shard_map/ppermute | solution.py:48
  131.0 123.4 %reduce-scatter.5.cloned.1.call-start = ((), (), s32[]{:S(2)}) async-start(), calls=%async_computation.5 | async-start | bytes 1966080 | tf_op jit(solution)/shard_map/reduce_scatter | solution.py:564
  150.3 16.8 %collective-permute-start.39 = (bf16[384,1024]{1,0:T(8,128)(2,1)S(1)}, bf16[384,1024]{1,0:T(8,128)(2,1)S(1)}, u32[]{:S(2)}, u32[]{:S(2)}) collective-permute-start(bf16[384,1024]{1,0:T(8,128)(2,1)S(1)} %slice.167), channel_id=1, source_target_pairs={{0,8},{1,9},{8,0},{9,1},{16,24},{17,25},{24,16},{25,17},{2,10},{3,... | collective-permute-start | bytes 2359304 | tf_op jit(solution)/shard_map/ppermute | solution.py:48
  153.3 12.5 %collective-permute-start.44 = (bf16[128,1024]{1,0:T(8,128)(2,1)S(1)}, bf16[128,1024]{1,0:T(8,128)(2,1)S(1)}, u32[]{:S(2)}, u32[]{:S(2)}) collective-permute-start(bf16[128,1024]{1,0:T(8,128)(2,1)S(1)} %fusion.41.refs_0_), channel_id=1, source_target_pairs={{0,1},{1,0},{8,9},{9,8},{16,17},{17,16},{24,25},{25,24},{2,3},{3,2... | collective-permute-start | bytes 786440 | tf_op jit(solution)/shard_map/ppermute | solution.py:48
  154.5 14.4 %collective-permute-start.47 = (bf16[128,1024]{1,0:T(8,128)(2,1)S(1)}, bf16[128,1024]{1,0:T(8,128)(2,1)S(1)}, u32[]{:S(2)}, u32[]{:S(2)}) collective-permute-start(bf16[128,1024]{1,0:T(8,128)(2,1)S(1)} %fusion.41.refs_0_), channel_id=1, source_target_pairs={{0,8},{1,9},{8,0},{9,1},{16,24},{17,25},{24,16},{25,17},{2,10},{3,... | collective-permute-start | bytes 786440 | tf_op jit(solution)/shard_map/ppermute | solution.py:48
  195.7 25.6 %collective-permute-start.51 = (bf16[384,1024]{1,0:T(8,128)(2,1)S(1)}, bf16[384,1024]{1,0:T(8,128)(2,1)S(1)}, u32[]{:S(2)}, u32[]{:S(2)}) collective-permute-start(bf16[384,1024]{1,0:T(8,128)(2,1)S(1)} %slice.175), channel_id=1, source_target_pairs={{0,8},{1,9},{8,0},{9,1},{16,24},{17,25},{24,16},{25,17},{2,10},{3,... | collective-permute-start | bytes 2359304 | tf_op jit(solution)/shard_map/ppermute | solution.py:48
  210.4 16.8 %collective-permute-start.59 = (bf16[128,1152]{1,0:T(8,128)(2,1)S(1)}, bf16[128,1152]{1,0:T(8,128)(2,1)S(1)}, u32[]{:S(2)}, u32[]{:S(2)}) collective-permute-start(bf16[128,1152]{1,0:T(8,128)(2,1)S(1)} %get-tuple-element.118.refs_0_), channel_id=1, source_target_pairs={{0,8},{1,9},{8,0},{9,1},{16,24},{17,25},{24,16},{25,17},{2,10},{3,... | collective-permute-start | bytes 884744 | tf_op jit(solution)/shard_map/ppermute | solution.py:48
  225.4 12.7 %collective-permute-start.53 = (bf16[128,1024]{1,0:T(8,128)(2,1)}, bf16[128,1024]{1,0:T(8,128)(2,1)}, u32[]{:S(2)}, u32[]{:S(2)}) collective-permute-start(bf16[128,1024]{1,0:T(8,128)(2,1)} %fusion.16), channel_id=1, source_target_pairs={{0,17},{1,16},{8,25},{9,24},{16,1},{17,0},{24,9},{25,8},{2,19},{3,... | collective-permute-start | bytes 786440 | tf_op jit(solution)/shard_map/ppermute | solution.py:48
  227.2 14.2 %collective-permute-start.54 = (bf16[128,1024]{1,0:T(8,128)(2,1)}, bf16[128,1024]{1,0:T(8,128)(2,1)S(1)}, u32[]{:S(2)}, u32[]{:S(2)}) collective-permute-start(bf16[128,1024]{1,0:T(8,128)(2,1)} %get-tuple-element.103), channel_id=1, source_target_pairs={{0,16},{1,17},{8,24},{9,25},{16,0},{17,1},{24,8},{25,9},{2,18},{3,... | collective-permute-start | bytes 786440 | tf_op jit(solution)/shard_map/ppermute | solution.py:48
  228.7 12.7 %collective-permute-start.55 = (bf16[128,1024]{1,0:T(8,128)(2,1)}, bf16[128,1024]{1,0:T(8,128)(2,1)}, u32[]{:S(2)}, u32[]{:S(2)}) collective-permute-start(bf16[128,1024]{1,0:T(8,128)(2,1)} %get-tuple-element.104), channel_id=1, source_target_pairs={{0,1},{1,0},{8,9},{9,8},{16,17},{17,16},{24,25},{25,24},{2,3},{3,2... | collective-permute-start | bytes 786440 | tf_op jit(solution)/shard_map/ppermute | solution.py:48
  231.6 15.5 %collective-permute-start.41 = (bf16[128,1024]{1,0:T(8,128)(2,1)}, bf16[128,1024]{1,0:T(8,128)(2,1)}, u32[]{:S(2)}, u32[]{:S(2)}) collective-permute-start(bf16[128,1024]{1,0:T(8,128)(2,1)} %slice_add_fusion.4), channel_id=1, source_target_pairs={{0,17},{1,16},{8,25},{9,24},{16,1},{17,0},{24,9},{25,8},{2,19},{3,... | collective-permute-start | bytes 786440 | tf_op jit(solution)/shard_map/ppermute | solution.py:48
  233.4 18.3 %collective-permute-start.42 = (bf16[128,1024]{1,0:T(8,128)(2,1)}, bf16[128,1024]{1,0:T(8,128)(2,1)}, u32[]{:S(2)}, u32[]{:S(2)}) collective-permute-start(bf16[128,1024]{1,0:T(8,128)(2,1)} %get-tuple-element.105), channel_id=1, source_target_pairs={{0,16},{1,17},{8,24},{9,25},{16,0},{17,1},{24,8},{25,9},{2,18},{3,... | collective-permute-start | bytes 786440 | tf_op jit(solution)/shard_map/ppermute | solution.py:48
  238.2 13.6 %collective-permute-start.43 = (bf16[128,1024]{1,0:T(8,128)(2,1)}, bf16[128,1024]{1,0:T(8,128)(2,1)S(1)}, u32[]{:S(2)}, u32[]{:S(2)}) collective-permute-start(bf16[128,1024]{1,0:T(8,128)(2,1)} %get-tuple-element.106), channel_id=1, source_target_pairs={{0,1},{1,0},{8,9},{9,8},{16,17},{17,16},{24,25},{25,24},{2,3},{3,2... | collective-permute-start | bytes 786440 | tf_op jit(solution)/shard_map/ppermute | solution.py:48
  (95 other events, 704.0 us)
Sparse Core Ops, SparseCore 0:
  18.1 38.5 all-gather.2
  58.8 48.8 all-gather.4
  131.1 48.8 reduce-scatter.2
  189.5 36.7 reduce-scatter.4

commit v4 on v3

--- a/solution.py
+++ b/solution.py
@@ -88,15 +88,14 @@
     )
 
 
-def direct_sums(sums):
-    rest, last = sums
+def direct_sums(sums, sent=None):
+    rest, last = sent or [part.astype(jnp.bfloat16) for part in sums]
     _, direct, _ = team_layout()
     rows = last.shape[0]
     bands = [rest[place * rows : (place + 1) * rows] for place in range(len(direct) - 1)] + [last]
-    total = bands[0]
+    total = sums[0][:rows]
     moved = [
-        swap(part.astype(jnp.bfloat16), TEAM, offset)
-        for offset, part in list(zip(direct, bands))[:0:-1]
+        swap(part, TEAM, offset) for offset, part in list(zip(direct, bands))[:0:-1]
     ]
     for part in moved:
         total = total + part.astype(jnp.float32)
@@ -111,9 +110,14 @@
 
 
 def everyone_sum(value):
-    for axis_name in ("rep", "ctx", "shard"):
-        for bit in axis_bits(axis_name):
-            value = value + swap(value, axis_name, bit)
+    for axis_name in ("shard", "rep", "ctx"):
+        size = lax.axis_size(axis_name)
+        if size <= 4:
+            moved = [swap(value, axis_name, offset) for offset in range(1, size)]
+            value = sum(moved, value)
+        else:
+            for bit in axis_bits(axis_name):
+                value = value + swap(value, axis_name, bit)
     return value
 
 
@@ -210,7 +214,7 @@
 
 
 def feed_kernel(*refs):
-    pieces = refs[:-8]
+    pieces = refs[:-11]
     (
         grads_ref,
         weights_ref,
@@ -220,7 +224,10 @@
         keep_ref,
         last_ref,
         rest_ref,
-    ) = refs[-8:]
+        down_keep_ref,
+        down_last_ref,
+        down_rest_ref,
+    ) = refs[-11:]
     hidden_width = hidden_ref.shape[1]
     height = pieces[0].shape[0]
     for place, piece in enumerate(pieces):
@@ -245,6 +252,13 @@
             keep_ref,
             last_ref,
             rest_ref,
+        )
+        put_partial(
+            dot_right(hidden_ref[rows, :], weights_ref[:, 2 * hidden_width :]),
+            first,
+            down_keep_ref,
+            down_last_ref,
+            down_rest_ref,
         )
 
 
@@ -458,7 +472,6 @@
     ffn_weights = all_rows(ffn_part)
     qkv_width = query_width + 2 * kv_width
     full_qkv = attn_weights[:, :qkv_width]
-    full_down = ffn_weights[:, 2 * hidden_width :]
     owners = lax.axis_size(OWNERS)
     gain_blocks = gather_plain(
         jnp.stack([attn_gain, ffn_gain]),
@@ -543,14 +556,14 @@
     unit_second = middle * inv_second
     normed_own = (unit_second * full_ffn_gain).astype(bfloat)
     normed_pieces = gather_pieces(lambda offset: normed_own)
-    normed_second, gate_up_grad, hidden, *second_parts = whole_call(
+    normed_second, gate_up_grad, hidden, *feed_parts = whole_call(
         feed_kernel,
         [
             ((total_rows, model_width), bfloat),
             ((total_rows, 2 * hidden_width), bfloat),
             ((total_rows, hidden_width), bfloat),
         ]
-        + partial_shapes(total_rows, model_width, team),
+        + partial_shapes(total_rows, model_width, team) * 2,
         [*normed_pieces, all_grads, ffn_weights],
         flops=FLOPS_HINT,
     )
@@ -563,7 +576,8 @@
     def shard_sum(rows):
         return lax.psum_scatter(rows, "shard", scatter_dimension=0, tiled=True)
 
-    second_sums = near_sums(second_parts)
+    second_sums = near_sums(feed_parts[:3])
+    down_sums = near_sums([after(part, *second_sums) for part in feed_parts[3:]])
     ffn_terms = joined_products(
         [(normed_second, after(gate_up_grad, *second_sums)), (all_grads, hidden)]
     )
@@ -576,10 +590,9 @@
         - unit_second * jnp.mean(unit_grad_second * unit_second, axis=1, keepdims=True)
     )
     grad_own = middle_grad.astype(bfloat)
-    middle_pieces = gather_pieces(lambda offset: grad_own)
-    down_partial = dot_right(after(hidden, grad_own), full_down)
-    down_parts = scatter_parts(down_partial)
-    down_sums = near_sums(down_parts)
+    down_sums = [after(part, grad_own) for part in down_sums]
+    down_sent = [part.astype(bfloat) for part in down_sums]
+    middle_pieces = gather_pieces(lambda offset: grad_own, *down_sent)
     middle_grad_b, projected_grad, norm_gain_parts = whole_call(
         attend_back_kernel,
         [
@@ -589,7 +602,7 @@
         ],
         [
             *middle_pieces[:-1],
-            after(middle_pieces[-1], *down_sums),
+            middle_pieces[-1],
             projected,
             attended,
             *tables,
@@ -599,7 +612,7 @@
         [pltpu.VMEM((total_rows, query_width), bfloat)],
         flops=FLOPS_HINT,
     )
-    block_sum = middle + direct_sums(down_sums)
+    block_sum = middle + direct_sums(down_sums, down_sent)
     block_out = block_sum.astype(bfloat).reshape(sequence_batch, count_of_rows, model_width)
 
     def rows_for(rows):
@@ -607,17 +620,19 @@
             rows, (ctx_place ^ (offset % ctx_size)) * own_rows, own_rows
         )
 
-    projected_grad = after(projected_grad, ffn_rows)
-    ffn_pieces = gather_pieces(rows_for(ffn_rows))
     attn_terms = joined_products([(first_normalized, projected_grad), (middle_grad_b, attended)])
     attn_rows = shard_sum(attn_terms)
+    ffn_pieces = gather_pieces(rows_for(after(ffn_rows, attn_terms)))
     first_partial = dot_right(after(projected_grad, attn_terms), full_qkv)
     attn_gain_part = jnp.sum(first_partial * unit_first_all, axis=0)
-    normed_grad_first = direct_sums(near_sums(scatter_parts(first_partial)))
+    first_parts = scatter_parts(after(first_partial, *ffn_pieces[1 : team // 2]))
+    normed_grad_first = direct_sums(near_sums(first_parts))
     unit_grad_first = normed_grad_first * full_gain
     tokens_grad = middle_grad + inv_first * (
-        unit_grad_first - unit_first * jnp.mean(unit_grad_first * unit_first, axis=1, keepdims=True)
-    )
+        unit_grad_first
+        - unit_first * jnp.mean(unit_grad_first * unit_first, axis=1, keepdims=True)
+    )
+    tokens_grad = tokens_grad.reshape(sequence_batch, count_of_rows, model_width)
     gain_totals = everyone_sum(
         jnp.concatenate(
             [
@@ -638,7 +653,7 @@
 
     ffn_outs = spread_columns(ffn_pieces, member, [hidden_width] * 3)
     gate_weight_grad, up_weight_grad, down_weight_grad = ffn_outs
-    attn_rows = after(attn_rows, *ffn_outs, tokens_grad, gain_totals, block_out)
+    attn_rows = after(attn_rows, *ffn_pieces, gain_totals)
     query_weight_grad, key_weight_grad, value_weight_grad, output_weight_grad = spread_columns(
         gather_pieces(rows_for(attn_rows)),
         member,
@@ -646,7 +661,7 @@
     )
     return (
         block_out,
-        tokens_grad.reshape(sequence_batch, count_of_rows, model_width),
+        tokens_grad,
         query_weight_grad,
         key_weight_grad,
         value_weight_grad,

time: 283 us -> 277 us (0.979)
  waiting for transfers between devices: 91.9 us -> 83.2 us
  matrix products: 19.1 us -> 14 us
  starting transfers between devices: 64 us -> 67.9 us
    ppermute x75 -> x77, waiting for transfers between devices: 91.8 us -> 82.2 us  [swap(): return lax.ppermute(value, axes, pairs)]
    convert_element_type x2 -> x6, other arithmetic: 2.92 us -> 9.26 us  [the longest x5 8.27 us: direct_sums(): rest, last = sent or [part.astype(jnp.bfloat16) for part in sums]]
    another operation x4 -> x1, other arithmetic: 7.1 us -> 2.79 us
    ppermute x75 -> x77, starting transfers between devices: 63.7 us -> 67.6 us  [swap(): return lax.ppermute(value, axes, pairs)]
    dot_general x2 -> x1, matrix products: 7.43 us -> 4.85 us  [dot_right(): lax.dot_general(left_side, right_side, (((1,), (1,)), ((), ())), preferre...]
    unnamed x94 -> x78, local copies, waits for them, and re-layouts: 10.8 us -> 10.2 us
  transfers between devices with their start and end apart: 79 -> 81, of which waited for: 31 -> 28; matrix products, arithmetic and copies ran while one was open for 19% -> 20% of each run, Pallas kernels for 9% -> 10%
where the time goes in v4:
time: 277 us; the launch traced here: 276 us
  waiting for transfers between devices  83.2 us (30%)
  starting transfers between devices  67.9 us (25%)
  Pallas kernels  39.6 us (14%)
  other arithmetic  30.7 us (11%)
  local copies, waits for them, and re-layouts  26 us (9%)
  between operations  14.6 us (5%)
  matrix products  14 us (5%)
    ppermute x77, waiting for transfers between devices, swap(): return lax.ppermute(value, axes, pairs)  82.2 us
    ppermute x77, starting transfers between devices, swap(): return lax.ppermute(value, axes, pairs)  67.6 us
    pallas_call x3, Pallas kernels, whole_call(): pl.pallas_call(kernel, in_specs=[pl.BlockSpec(memory_space=pltpu.VMEM)] *...  32.2 us
    unnamed x78, local copies, waits for them, and re-layouts  10.2 us
    dot_general x4, matrix products, dot_left(): lax.dot_general(left_side, right_side, (((0,), (0,)), ((), ())), preferre...  8.97 us
    convert_element_type x5, other arithmetic, direct_sums(): rest, last = sent or [part.astype(jnp.bfloat16) for part in sums]  8.27 us
    pallas_call x2, Pallas kernels, spread_columns(): pl.pallas_call(functools.partial(spread_kernel, widths=widths, offsets=of...  7.4 us
  transfers between devices with their start and end apart: 81, of which 28 were waited for; matrix products, arithmetic and copies ran while one was open for 20% of the time, Pallas kernels for 10%

profile of v4, /device:TPU:0, one launch (start us, length us, event | category | flops | bytes accessed | tf_op | source)
XLA Modules:
  0.0 275.9 jit_solution(11741405302172911401)
XLA Ops:
  9.2 3.0 %collective-permute-start = (bf16[128,768]{1,0:T(8,128)(2,1)S(1)}, bf16[128,768]{1,0:T(8,128)(2,1)S(1)}, u32[]{:S(2)}, u32[]{:S(2)}) collective-permute-start(bf16[128,768]{1,0:T(8,128)(2,1)S(1)} %pad_maximum_fusion.3), channel_id=1, source_target_pairs={{0,1},{1,0},{2,3},{3,2},{4,5},{5,4},{6,7},{7,6},{8,9},{9,8},{10,11... | collective-permute-start | bytes 589832 | tf_op jit(solution)/shard_map/ppermute | solution.py:48
  21.7 2.9 %collective-permute-start.10 = (bf16[4,2,128]{2,0,1:T(4,128)(2,1)S(1)}, bf16[4,2,128]{2,0,1:T(4,128)(2,1)S(1)}, u32[]{:S(2)}, u32[]{:S(2)}) collective-permute-start(bf16[4,2,128]{2,0,1:T(4,128)(2,1)S(1)} %pad_maximum_fusion.5), channel_id=1, source_target_pairs={{0,4},{1,5},{2,6},{3,7},{4,0},{5,1},{6,2},{7,3},{8,12},{9,13},{10,... | collective-permute-start | bytes 6152 | tf_op jit(solution)/shard_map/ppermute | solution.py:48
  31.7 4.0 %collective-permute-done.1 = bf16[128,1024]{1,0:T(8,128)(2,1)} collective-permute-done((bf16[128,1024]{1,0:T(8,128)(2,1)S(1)}, bf16[128,1024]{1,0:T(8,128)(2,1)}, u32[]{:S(2)}, u32[]{:S(2)}) %collective-permute-start.1) | collective-permute-done | bytes 262176 | tf_op jit(solution)/shard_map/ppermute | solution.py:48
  38.2 5.4 %collective-permute-done.12 = s32[1,1,128]{2,1,0:T(1,128)S(1)} collective-permute-done((s32[1,1,128]{2,1,0:T(1,128)S(1)}, s32[1,1,128]{2,1,0:T(1,128)S(1)}, u32[]{:S(2)}, u32[]{:S(2)}) %collective-permute-start.12) | collective-permute-done | bytes 544 | tf_op jit(solution)/shard_map/ppermute | solution.py:48
  49.2 3.0 %fusion.14 = (f32[1024,128]{1,0:T(8,128)}, f32[1024,128]{1,0:T(8,128)}) fusion(f32[128]{0:T(128)S(1)} %get-tuple-element.169, f32[128]{0:T(128)S(1)} %get-tuple-element.170, f32[1024]{0:T(1024)S(1)} %bitcast.70), kind=kLoop, calls=%fused_computation.32 | loop fusion | flops 262144 | bytes 1053696 | tf_op jit(solution)/shard_map/mul | solution.py:513
  58.8 10.1 %shard_map.246 = (f32[1024,512]{1,0:T(8,128)}, bf16[1024,256]{1,0:T(8,128)(2,1)}, f32[512,1024]{1,0:T(8,128)}, bf16[128,1024]{1,0:T(8,128)(2,1)}, bf16[384,1024]{1,0:T(8,128)(2,1)}) custom-call(bf16[1024,1024]{1,0:T(8,128)(2,1)} %fusion.2.normed_ref, f32[1024,128]{1,0:T(8,128)} %get-tuple-element.156.cosine_ref.refs_10_, ...), custom_call_target="tpu_custom_call" | custom-call | flops 8000000000 | bytes 10488832 | tf_op jit(solution)/shard_map/pallas_call | solution.py:356
  80.7 5.0 %collective-permute-done.17 = bf16[128,1024]{1,0:T(8,128)(2,1)S(1)} collective-permute-done((bf16[128,1024]{1,0:T(8,128)(2,1)S(1)}, bf16[128,1024]{1,0:T(8,128)(2,1)S(1)}, u32[]{:S(2)}, u32[]{:S(2)}) %collective-permute-start.17) | collective-permute-done | bytes 262176 | tf_op jit(solution)/shard_map/ppermute | solution.py:48
  85.8 5.1 %collective-permute-done.18 = bf16[128,1024]{1,0:T(8,128)(2,1)S(1)} collective-permute-done((bf16[128,1024]{1,0:T(8,128)(2,1)S(1)}, bf16[128,1024]{1,0:T(8,128)(2,1)S(1)}, u32[]{:S(2)}, u32[]{:S(2)}) %collective-permute-start.18) | collective-permute-done | bytes 262176 | tf_op jit(solution)/shard_map/ppermute | solution.py:48
  93.4 3.6 %collective-permute-done.29 = bf16[128,1024]{1,0:T(8,128)(2,1)S(1)} collective-permute-done((bf16[128,1024]{1,0:T(8,128)(2,1)S(1)}, bf16[128,1024]{1,0:T(8,128)(2,1)S(1)}, u32[]{:S(2)}, u32[]{:S(2)}) %collective-permute-start.29) | collective-permute-done | bytes 262176 | tf_op jit(solution)/shard_map/ppermute | solution.py:48
  102.7 6.3 %collective-permute-done.21.refs_2_ = bf16[128,1024]{1,0:T(8,128)(2,1)} collective-permute-done((bf16[128,1024]{1,0:T(8,128)(2,1)S(1)}, bf16[128,1024]{1,0:T(8,128)(2,1)}, u32[]{:S(2)}, u32[]{:S(2)}) %collective-permute-start.21) | collective-permute-done | bytes 262176 | tf_op jit(solution)/shard_map/ppermute | solution.py:48
  111.3 11.0 %shard_map.247 = (bf16[1024,1024]{1,0:T(8,128)(2,1)}, bf16[1024,768]{1,0:T(8,128)(2,1)}, bf16[1024,384]{1,0:T(8,128)(2,1)}, f32[512,1024]{1,0:T(8,128)}, bf16[12...) custom-call(bf16[128,1024]{1,0:T(8,128)(2,1)} %copy-done.9, ...), custom_call_target="tpu_custom_call" | custom-call | flops 8000000000 | bytes 17301504 | tf_op jit(solution)/shard_map/pallas_call | solution.py:356
  122.7 3.2 %convolution_convert_fusion.2 = bf16[1024,384]{1,0:T(8,128)(2,1)S(1)} fusion(bf16[1024,1024]{1,0:T(8,128)(2,1)} %copy-done.14, bf16[1024,384]{1,0:T(8,128)(2,1)} %get-tuple-element.84), kind=kOutput, calls=%fused_computation.15 | convolution fusion | flops 805699584 | bytes 3670016 | tf_op jit(solution)/shard_map/dot_general | solution.py:35
  137.7 5.0 %collective-permute-done.37 = bf16[128,1024]{1,0:T(8,128)(2,1)S(1)} collective-permute-done((bf16[128,1024]{1,0:T(8,128)(2,1)S(1)}, bf16[128,1024]{1,0:T(8,128)(2,1)S(1)}, u32[]{:S(2)}, u32[]{:S(2)}) %collective-permute-start.37) | collective-permute-done | bytes 262176 | tf_op jit(solution)/shard_map/ppermute | solution.py:48
  142.7 4.7 %collective-permute-done.38 = bf16[128,1024]{1,0:T(8,128)(2,1)S(1)} collective-permute-done((bf16[128,1024]{1,0:T(8,128)(2,1)S(1)}, bf16[128,1024]{1,0:T(8,128)(2,1)S(1)}, u32[]{:S(2)}, u32[]{:S(2)}) %collective-permute-start.38) | collective-permute-done | bytes 262176 | tf_op jit(solution)/shard_map/ppermute | solution.py:48
  156.0 3.4 %collective-permute-done.46.refs_3_ = bf16[128,1024]{1,0:T(8,128)(2,1)S(1)} collective-permute-done((bf16[128,1024]{1,0:T(8,128)(2,1)S(1)}, bf16[128,1024]{1,0:T(8,128)(2,1)S(1)}, u32[]{:S(2)}, u32[]{:S(2)}) %collective-permute-start.46) | collective-permute-done | bytes 262176 | tf_op jit(solution)/shard_map/ppermute | solution.py:48
  159.4 4.7 %collective-permute-done.45.refs_2_ = bf16[128,1024]{1,0:T(8,128)(2,1)S(1)} collective-permute-done((bf16[128,1024]{1,0:T(8,128)(2,1)S(1)}, bf16[128,1024]{1,0:T(8,128)(2,1)S(1)}, u32[]{:S(2)}, u32[]{:S(2)}) %collective-permute-start.45) | collective-permute-done | bytes 262176 | tf_op jit(solution)/shard_map/ppermute | solution.py:48
  167.4 11.1 %shard_map.248 = (bf16[1024,1024]{1,0:T(8,128)(2,1)}, bf16[1024,512]{1,0:T(8,128)(2,1)}, f32[8,128]{1,0:T(8,128)}) custom-call(bf16[128,1024]{1,0:T(8,128)(2,1)} %copy-done.10, bf16[128,1024]{1,0:T(8,128)(2,1)} %copy-done.24, bf16[128,1024]{1,0:T(8,128)(2,1)} %copy-done.23, bf16[128,1024]{1,0:T(8,128)(2,1)} %copy-done.22, bf16[128,1024]{1,0:T(8,128)(2,1)} %copy-done.28, ...), custom_call_target="tpu_custom_call" | custom-call | flops 8000000000 | bytes 10492928 | tf_op jit(solution)/shard_map/pallas_call | solution.py:356
  183.7 4.9 %fusion.3 = (f32[1024]{0:T(1024)S(1)}, f32[1024,1024]{1,0:T(8,128)}) fusion(bf16[1024,1024]{1,0:T(8,128)(2,1)S(1)} %constant_dynamic-update-slice_fusion, f32[1024]{0:T(1024)S(1)} %add_rsqrt_fusion, bf16[1024,512]{1,0:T(8,128)(2,1)} %get-tuple-element.97, bf16[1024,768]{1,0:T(8,128)(2,1)} %all-gather.3.cloned.1.call-done.weights_ref.refs_12_), kind=kOutput, calls=%fused_computation.5 | convolution fusion | flops 1077935104 | bytes 8396800 | tf_op jit(solution)/shard_map/dot_general | solution.py:29
  198.0 3.6 %collective-permute-start.65 = (f32[24,128]{1,0:T(8,128)S(1)}, f32[24,128]{1,0:T(8,128)S(1)}, u32[]{:S(2)}, u32[]{:S(2)}) collective-permute-start(f32[24,128]{1,0:T(8,128)S(1)} %pad_maximum_fusion.4), channel_id=1, source_target_pairs={{0,6},{2,4},{4,2},{6,0},{1,7},{3,5},{5,3},{7,1},{8,14},{10,12},{12... | collective-permute-start | bytes 36872 | tf_op jit(solution)/shard_map/ppermute | solution.py:48
  208.5 2.8 %convert.5 = bf16[1024,1024]{1,0:T(8,128)(2,1)S(1)} convert(f32[1024,1024]{1,0:T(8,128)} %get-tuple-element.99) | non-fusion elementwise | flops 1048576 | bytes 6291456 | tf_op jit(solution)/shard_map/convert.2
  232.7 9.9 %collective-permute-done.71.refs_2_ = bf16[128,768]{1,0:T(8,128)(2,1)} collective-permute-done((bf16[128,768]{1,0:T(8,128)(2,1)S(1)}, bf16[128,768]{1,0:T(8,128)(2,1)}, u32[]{:S(2)}, u32[]{:S(2)}) %collective-permute-start.71) | collective-permute-done | bytes 196640 | tf_op jit(solution)/shard_map/ppermute | solution.py:48
  247.7 4.0 %shard_map.250 = (f32[128,3072]{1,0:T(8,128)}, f32[128,3072]{1,0:T(8,128)}, f32[128,3072]{1,0:T(8,128)}) custom-call(s32[1]{0:T(128)} %bitcast.19.member_ref, bf16[128,1152]{1,0:T(8,128)(2,1)} %get-tuple-element.135.refs_0_, bf16[128,1152]{1,0:T(8,128)(2,1)} %collective-permute-done.51.refs_1_, bf16[128,1152]{1,0:T(8,128)(2,1)} %collective-permute-done.52.refs_2_, ...), custom_call_target="tpu_custom_call" | custom-call | tf_op jit(solution)/shard_map/pallas_call | solution.py:389
  254.2 3.4 %shard_map.249 = (f32[128,2048]{1,0:T(8,128)}, f32[128,1024]{1,0:T(8,128)}, f32[128,1024]{1,0:T(8,128)}, f32[128,2048]{1,0:T(8,128)}) custom-call(s32[1]{0:T(128)} %bitcast.19.member_ref, bf16[128,768]{1,0:T(8,128)(2,1)} %copy-done.8, bf16[128,768]{1,0:T(8,128)(2,1)} %copy-done.11, bf16[128,768]{1,0:T(8,128)(2,1)} %collective-permute-done.71.refs_2_, ...), custom_call_target="tpu_custom_call" | custom-call | tf_op jit(solution)/shard_map/pallas_call | solution.py:389
  262.0 4.7 %collective-permute-done.42 = bf16[128,1024]{1,0:T(8,128)(2,1)} collective-permute-done((bf16[128,1024]{1,0:T(8,128)(2,1)}, bf16[128,1024]{1,0:T(8,128)(2,1)}, u32[]{:S(2)}, u32[]{:S(2)}) %collective-permute-start.42) | collective-permute-done | bytes 262176 | tf_op jit(solution)/shard_map/ppermute | solution.py:48
  (301 shorter events, 136.5 us)
Async XLA Ops:
  7.2 51.6 %all-gather.3.cloned.1.call-start = ((), (), s32[]{:S(2)}) async-start(), calls=%async_computation.2 | async-start | bytes 1966080 | tf_op jit(solution)/shard_map/all_gather | solution.py:465
  18.0 93.0 %all-gather.5.cloned.1.call-start = ((), (), s32[]{:S(2)}) async-start(), calls=%async_computation.3 | async-start | bytes 2949120 | tf_op jit(solution)/shard_map/all_gather | solution.py:465
  29.7 14.0 %collective-permute-start.3 = (bf16[128,1024]{1,0:T(8,128)(2,1)S(1)}, bf16[128,1024]{1,0:T(8,128)(2,1)}, u32[]{:S(2)}, u32[]{:S(2)}) collective-permute-start(bf16[128,1024]{1,0:T(8,128)(2,1)S(1)} %bitcast.60), channel_id=1, source_target_pairs={{0,17},{1,16},{8,25},{9,24},{16,1},{17,0},{24,9},{25,8},{2,19},{3,... | collective-permute-start | bytes 786440 | tf_op jit(solution)/shard_map/ppermute | solution.py:48
  29.9 17.4 %collective-permute-start.4 = (bf16[128,1024]{1,0:T(8,128)(2,1)S(1)}, bf16[128,1024]{1,0:T(8,128)(2,1)S(1)}, u32[]{:S(2)}, u32[]{:S(2)}) collective-permute-start(bf16[128,1024]{1,0:T(8,128)(2,1)S(1)} %bitcast.61), channel_id=1, source_target_pairs={{0,8},{1,9},{8,0},{9,1},{16,24},{17,25},{24,16},{25,17},{2,10},{3,... | collective-permute-start | bytes 786440 | tf_op jit(solution)/shard_map/ppermute | solution.py:48
  29.9 22.3 %collective-permute-start.11 = (bf16[128,1152]{1,0:T(8,128)(2,1)S(1)}, bf16[128,1152]{1,0:T(8,128)(2,1)S(1)}, u32[]{:S(2)}, u32[]{:S(2)}) collective-permute-start(bf16[128,1152]{1,0:T(8,128)(2,1)S(1)} %pad_maximum_fusion.2), channel_id=1, source_target_pairs={{0,1},{1,0},{2,3},{3,2},{4,5},{5,4},{6,7},{7,6},{8,9},{9,8},{10,11... | collective-permute-start | bytes 884744 | tf_op jit(solution)/shard_map/ppermute | solution.py:48
  38.1 15.3 %collective-permute-start.5 = (bf16[128,1024]{1,0:T(8,128)(2,1)}, bf16[128,1024]{1,0:T(8,128)(2,1)}, u32[]{:S(2)}, u32[]{:S(2)}) collective-permute-start(bf16[128,1024]{1,0:T(8,128)(2,1)} %collective-permute-done.1), channel_id=1, source_target_pairs={{0,8},{1,9},{8,0},{9,1},{16,24},{17,25},{24,16},{25,17},{2,10},{3,... | collective-permute-start | bytes 786440 | tf_op jit(solution)/shard_map/ppermute | solution.py:48
  53.2 135.3 %reduce-scatter.3.cloned.1.call-start = ((), (), s32[]{:S(2)}) async-start(), calls=%async_computation.4 | async-start | bytes 2949120 | tf_op jit(solution)/shard_map/reduce_scatter | solution.py:577
  78.9 18.1 %collective-permute-start.29 = (bf16[128,1024]{1,0:T(8,128)(2,1)S(1)}, bf16[128,1024]{1,0:T(8,128)(2,1)S(1)}, u32[]{:S(2)}, u32[]{:S(2)}) collective-permute-start(bf16[128,1024]{1,0:T(8,128)(2,1)S(1)} %bitcast.65), channel_id=1, source_target_pairs={{0,17},{1,16},{8,25},{9,24},{16,1},{17,0},{24,9},{25,8},{2,19},{3,... | collective-permute-start | bytes 786440 | tf_op jit(solution)/shard_map/ppermute | solution.py:48
  80.7 17.8 %collective-permute-start.30 = (bf16[128,1024]{1,0:T(8,128)(2,1)S(1)}, bf16[128,1024]{1,0:T(8,128)(2,1)S(1)}, u32[]{:S(2)}, u32[]{:S(2)}) collective-permute-start(bf16[128,1024]{1,0:T(8,128)(2,1)S(1)} %bitcast.66), channel_id=1, source_target_pairs={{0,8},{1,9},{8,0},{9,1},{16,24},{17,25},{24,16},{25,17},{2,10},{3,... | collective-permute-start | bytes 786440 | tf_op jit(solution)/shard_map/ppermute | solution.py:48
  85.8 14.2 %collective-permute-start.31 = (bf16[128,1024]{1,0:T(8,128)(2,1)S(1)}, bf16[128,1024]{1,0:T(8,128)(2,1)S(1)}, u32[]{:S(2)}, u32[]{:S(2)}) collective-permute-start(bf16[128,1024]{1,0:T(8,128)(2,1)S(1)} %collective-permute-done.27), channel_id=1, source_target_pairs={{0,8},{1,9},{8,0},{9,1},{16,24},{17,25},{24,16},{25,17},{2,10},{3,... | collective-permute-start | bytes 786440 | tf_op jit(solution)/shard_map/ppermute | solution.py:48
  132.5 88.1 %reduce-scatter.5.cloned.1.call-start = ((), (), s32[]{:S(2)}) async-start(), calls=%async_computation.5 | async-start | bytes 1966080 | tf_op jit(solution)/shard_map/reduce_scatter | solution.py:577
  137.2 15.5 %collective-permute-start.40 = (bf16[128,1024]{1,0:T(8,128)(2,1)}, bf16[128,1024]{1,0:T(8,128)(2,1)S(1)}, u32[]{:S(2)}, u32[]{:S(2)}) collective-permute-start(bf16[128,1024]{1,0:T(8,128)(2,1)} %get-tuple-element.88), channel_id=1, source_target_pairs={{0,8},{1,9},{8,0},{9,1},{16,24},{17,25},{24,16},{25,17},{2,10},{3,... | collective-permute-start | bytes 786440 | tf_op jit(solution)/shard_map/ppermute | solution.py:48
  137.2 16.3 %collective-permute-start.36 = (bf16[384,1024]{1,0:T(8,128)(2,1)}, bf16[384,1024]{1,0:T(8,128)(2,1)S(1)}, u32[]{:S(2)}, u32[]{:S(2)}) collective-permute-start(bf16[384,1024]{1,0:T(8,128)(2,1)} %get-tuple-element.80), channel_id=1, source_target_pairs={{0,8},{1,9},{8,0},{9,1},{16,24},{17,25},{24,16},{25,17},{2,10},{3,... | collective-permute-start | bytes 2359304 | tf_op jit(solution)/shard_map/ppermute | solution.py:48
  190.3 15.2 %collective-permute-start.51 = (bf16[128,1152]{1,0:T(8,128)(2,1)S(1)}, bf16[128,1152]{1,0:T(8,128)(2,1)}, u32[]{:S(2)}, u32[]{:S(2)}) collective-permute-start(bf16[128,1152]{1,0:T(8,128)(2,1)S(1)} %get-tuple-element.136), channel_id=1, source_target_pairs={{0,1},{1,0},{8,9},{9,8},{16,17},{17,16},{24,25},{25,24},{2,3},{3,2... | collective-permute-start | bytes 884744 | tf_op jit(solution)/shard_map/ppermute | solution.py:48
  191.8 16.8 %collective-permute-start.53 = (bf16[128,1152]{1,0:T(8,128)(2,1)S(1)}, bf16[128,1152]{1,0:T(8,128)(2,1)}, u32[]{:S(2)}, u32[]{:S(2)}) collective-permute-start(bf16[128,1152]{1,0:T(8,128)(2,1)S(1)} %get-tuple-element.136), channel_id=1, source_target_pairs={{0,17},{1,16},{8,25},{9,24},{16,1},{17,0},{24,9},{25,8},{2,19},{3,... | collective-permute-start | bytes 884744 | tf_op jit(solution)/shard_map/ppermute | solution.py:48
  193.3 15.3 %collective-permute-start.52 = (bf16[128,1152]{1,0:T(8,128)(2,1)}, bf16[128,1152]{1,0:T(8,128)(2,1)}, u32[]{:S(2)}, u32[]{:S(2)}) collective-permute-start(bf16[128,1152]{1,0:T(8,128)(2,1)} %get-tuple-element.135.refs_0_), channel_id=1, source_target_pairs={{0,16},{1,17},{8,24},{9,25},{16,0},{17,1},{24,8},{25,9},{2,18},{3,... | collective-permute-start | bytes 884744 | tf_op jit(solution)/shard_map/ppermute | solution.py:48
  212.3 17.2 %collective-permute-start.54 = (bf16[384,1024]{1,0:T(8,128)(2,1)}, bf16[384,1024]{1,0:T(8,128)(2,1)}, u32[]{:S(2)}, u32[]{:S(2)}) collective-permute-start(bf16[384,1024]{1,0:T(8,128)(2,1)} %slice.141), channel_id=1, source_target_pairs={{0,8},{1,9},{8,0},{9,1},{16,24},{17,25},{24,16},{25,17},{2,10},{3,... | collective-permute-start | bytes 2359304 | tf_op jit(solution)/shard_map/ppermute | solution.py:48
  225.0 32.6 %collective-permute-start.56 = (bf16[128,1024]{1,0:T(8,128)(2,1)}, bf16[128,1024]{1,0:T(8,128)(2,1)S(1)}, u32[]{:S(2)}, u32[]{:S(2)}) collective-permute-start(bf16[128,1024]{1,0:T(8,128)(2,1)} %add_convert_fusion), channel_id=1, source_target_pairs={{0,17},{1,16},{8,25},{9,24},{16,1},{17,0},{24,9},{25,8},{2,19},{3,... | collective-permute-start | bytes 786440 | tf_op jit(solution)/shard_map/ppermute | solution.py:48
  226.5 17.1 %collective-permute-start.72 = (bf16[128,768]{1,0:T(8,128)(2,1)S(1)}, bf16[128,768]{1,0:T(8,128)(2,1)}, u32[]{:S(2)}, u32[]{:S(2)}) collective-permute-start(bf16[128,768]{1,0:T(8,128)(2,1)S(1)} %get-tuple-element.143), channel_id=1, source_target_pairs={{0,17},{1,16},{8,25},{9,24},{16,1},{17,0},{24,9},{25,8},{2,19},{3,... | collective-permute-start | bytes 589832 | tf_op jit(solution)/shard_map/ppermute | solution.py:48
  228.0 14.7 %collective-permute-start.71 = (bf16[128,768]{1,0:T(8,128)(2,1)S(1)}, bf16[128,768]{1,0:T(8,128)(2,1)}, u32[]{:S(2)}, u32[]{:S(2)}) collective-permute-start(bf16[128,768]{1,0:T(8,128)(2,1)S(1)} %get-tuple-element.144.refs_0_), channel_id=1, source_target_pairs={{0,16},{1,17},{8,24},{9,25},{16,0},{17,1},{24,8},{25,9},{2,18},{3,... | collective-permute-start | bytes 589832 | tf_op jit(solution)/shard_map/ppermute | solution.py:48
  229.4 16.4 %collective-permute-start.73 = (bf16[128,768]{1,0:T(8,128)(2,1)S(1)}, bf16[128,768]{1,0:T(8,128)(2,1)S(1)}, u32[]{:S(2)}, u32[]{:S(2)}) collective-permute-start(bf16[128,768]{1,0:T(8,128)(2,1)S(1)} %get-tuple-element.144.refs_0_), channel_id=1, source_target_pairs={{0,8},{1,9},{8,0},{9,1},{16,24},{17,25},{24,16},{25,17},{2,10},{3,... | collective-permute-start | bytes 589832 | tf_op jit(solution)/shard_map/ppermute | solution.py:48
  229.4 16.4 %collective-permute-start.74 = (bf16[128,768]{1,0:T(8,128)(2,1)S(1)}, bf16[128,768]{1,0:T(8,128)(2,1)S(1)}, u32[]{:S(2)}, u32[]{:S(2)}) collective-permute-start(bf16[128,768]{1,0:T(8,128)(2,1)S(1)} %collective-permute-done.70.refs_1_), channel_id=1, source_target_pairs={{0,8},{1,9},{8,0},{9,1},{16,24},{17,25},{24,16},{25,17},{2,10},{3,... | collective-permute-start | bytes 589832 | tf_op jit(solution)/shard_map/ppermute | solution.py:48
  242.6 16.1 %collective-permute-start.57 = (bf16[128,1024]{1,0:T(8,128)(2,1)}, bf16[128,1024]{1,0:T(8,128)(2,1)}, u32[]{:S(2)}, u32[]{:S(2)}) collective-permute-start(bf16[128,1024]{1,0:T(8,128)(2,1)} %get-tuple-element.121), channel_id=1, source_target_pairs={{0,16},{1,17},{8,24},{9,25},{16,0},{17,1},{24,8},{25,9},{2,18},{3,... | collective-permute-start | bytes 786440 | tf_op jit(solution)/shard_map/ppermute | solution.py:48
  243.6 15.1 %collective-permute-start.58 = (bf16[128,1024]{1,0:T(8,128)(2,1)}, bf16[128,1024]{1,0:T(8,128)(2,1)}, u32[]{:S(2)}, u32[]{:S(2)}) collective-permute-start(bf16[128,1024]{1,0:T(8,128)(2,1)} %get-tuple-element.122), channel_id=1, source_target_pairs={{0,1},{1,0},{8,9},{9,8},{16,17},{17,16},{24,25},{25,24},{2,3},{3,2... | collective-permute-start | bytes 786440 | tf_op jit(solution)/shard_map/ppermute | solution.py:48
  (89 other events, 686.1 us)
Sparse Core Ops, SparseCore 0:
  18.1 38.5 all-gather.2
  58.8 48.8 all-gather.4
  132.6 48.8 reduce-scatter.2
  184.2 36.3 reduce-scatter.4

commit v5 on v4

--- a/solution.py
+++ b/solution.py
@@ -578,9 +578,9 @@
 
     second_sums = near_sums(feed_parts[:3])
     down_sums = near_sums([after(part, *second_sums) for part in feed_parts[3:]])
-    ffn_terms = joined_products(
-        [(normed_second, after(gate_up_grad, *second_sums)), (all_grads, hidden)]
-    )
+    down_terms = dot_left(all_grads, hidden).astype(bfloat)
+    gate_up_terms = dot_left(normed_second, after(gate_up_grad, *second_sums)).astype(bfloat)
+    ffn_terms = jnp.concatenate([gate_up_terms, down_terms], axis=1)
     ffn_rows = shard_sum(ffn_terms)
     normed_grad_second = after(direct_sums(second_sums), ffn_terms)
     ffn_gain_part = jnp.sum(normed_grad_second * unit_second, axis=0)
@@ -622,17 +622,12 @@
 
     attn_terms = joined_products([(first_normalized, projected_grad), (middle_grad_b, attended)])
     attn_rows = shard_sum(attn_terms)
-    ffn_pieces = gather_pieces(rows_for(after(ffn_rows, attn_terms)))
-    first_partial = dot_right(after(projected_grad, attn_terms), full_qkv)
+    ffn_sent = {
+        offset: rows_for(after(ffn_rows, attn_terms))(offset) for offset in team_layout()[1]
+    }
+    ffn_pieces = gather_pieces(lambda offset: ffn_sent[offset])
+    first_partial = dot_right(after(projected_grad, attn_terms, *ffn_sent.values()), full_qkv)
     attn_gain_part = jnp.sum(first_partial * unit_first_all, axis=0)
-    first_parts = scatter_parts(after(first_partial, *ffn_pieces[1 : team // 2]))
-    normed_grad_first = direct_sums(near_sums(first_parts))
-    unit_grad_first = normed_grad_first * full_gain
-    tokens_grad = middle_grad + inv_first * (
-        unit_grad_first
-        - unit_first * jnp.mean(unit_grad_first * unit_first, axis=1, keepdims=True)
-    )
-    tokens_grad = tokens_grad.reshape(sequence_batch, count_of_rows, model_width)
     gain_totals = everyone_sum(
         jnp.concatenate(
             [
@@ -643,6 +638,14 @@
             axis=0,
         )
     )
+    first_parts = scatter_parts(after(first_partial, *ffn_pieces[1 : team // 2]))
+    normed_grad_first = direct_sums(near_sums(first_parts))
+    unit_grad_first = normed_grad_first * full_gain
+    tokens_grad = middle_grad + inv_first * (
+        unit_grad_first
+        - unit_first * jnp.mean(unit_grad_first * unit_first, axis=1, keepdims=True)
+    )
+    tokens_grad = tokens_grad.reshape(sequence_batch, count_of_rows, model_width)
     gain_rows = model_width // HEAD_SIZE
     attn_gain_grad = lax.dynamic_slice_in_dim(
         gain_totals[:gain_rows].reshape(model_width), own_start, own_rows
@@ -653,7 +656,7 @@
 
     ffn_outs = spread_columns(ffn_pieces, member, [hidden_width] * 3)
     gate_weight_grad, up_weight_grad, down_weight_grad = ffn_outs
-    attn_rows = after(attn_rows, *ffn_pieces, gain_totals)
+    attn_rows = after(attn_rows, *ffn_pieces)
     query_weight_grad, key_weight_grad, value_weight_grad, output_weight_grad = spread_columns(
         gather_pieces(rows_for(attn_rows)),
         member,

time: 277 us -> 277 us (level)
  waiting for transfers between devices: 83.2 us -> 87.4 us
    reduce_scatter x2, waiting for transfers between devices: 0.89 us -> 6.95 us  [shard_sum(): return lax.psum_scatter(rows, 'shard', scatter_dimension=0, tiled=True)]
    unnamed x78 -> x80, local copies, waits for them, and re-layouts: 10.2 us -> 10.2 us
  transfers between devices with their start and end apart: 81 -> 81, of which waited for: 28 -> 29; matrix products, arithmetic and copies ran while one was open for 20% -> 18% of each run, Pallas kernels for 10% -> 10%
where the time goes in v5:
time: 277 us; the launch traced here: 276 us
  waiting for transfers between devices  87.4 us (32%)
  starting transfers between devices  67.8 us (24%)
  Pallas kernels  39.6 us (14%)
  other arithmetic  28.4 us (10%)
  local copies, waits for them, and re-layouts  26 us (9%)
  between operations  14.6 us (5%)
  matrix products  12.1 us (4%)
    ppermute x77, waiting for transfers between devices, swap(): return lax.ppermute(value, axes, pairs)  80.4 us
    ppermute x77, starting transfers between devices, swap(): return lax.ppermute(value, axes, pairs)  67.5 us
    pallas_call x3, Pallas kernels, whole_call(): pl.pallas_call(kernel, in_specs=[pl.BlockSpec(memory_space=pltpu.VMEM)] *...  32.2 us
    unnamed x80, local copies, waits for them, and re-layouts  10.2 us
    dot_general x4, matrix products, dot_left(): lax.dot_general(left_side, right_side, (((0,), (0,)), ((), ())), preferre...  8.97 us
    convert_element_type x5, other arithmetic, direct_sums(): rest, last = sent or [part.astype(jnp.bfloat16) for part in sums]  8.27 us
    pallas_call x2, Pallas kernels, spread_columns(): pl.pallas_call(functools.partial(spread_kernel, widths=widths, offsets=of...  7.4 us
    reduce_scatter x2, waiting for transfers between devices, shard_sum(): return lax.psum_scatter(rows, 'shard', scatter_dimension=0, tiled=True)  6.95 us
  transfers between devices with their start and end apart: 81, of which 29 were waited for; matrix products, arithmetic and copies ran while one was open for 18% of the time, Pallas kernels for 10%

profile of v5, /device:TPU:0, one launch (start us, length us, event | category | flops | bytes accessed | tf_op | source)
XLA Modules:
  0.0 275.9 jit_solution(9057886150817747416)
XLA Ops:
  9.2 3.0 %collective-permute-start = (bf16[128,768]{1,0:T(8,128)(2,1)S(1)}, bf16[128,768]{1,0:T(8,128)(2,1)S(1)}, u32[]{:S(2)}, u32[]{:S(2)}) collective-permute-start(bf16[128,768]{1,0:T(8,128)(2,1)S(1)} %pad_maximum_fusion.3), channel_id=1, source_target_pairs={{0,1},{1,0},{2,3},{3,2},{4,5},{5,4},{6,7},{7,6},{8,9},{9,8},{10,11... | collective-permute-start | bytes 589832 | tf_op jit(solution)/shard_map/ppermute | solution.py:48
  21.7 2.9 %collective-permute-start.10 = (bf16[4,2,128]{2,0,1:T(4,128)(2,1)S(1)}, bf16[4,2,128]{2,0,1:T(4,128)(2,1)S(1)}, u32[]{:S(2)}, u32[]{:S(2)}) collective-permute-start(bf16[4,2,128]{2,0,1:T(4,128)(2,1)S(1)} %pad_maximum_fusion.5), channel_id=1, source_target_pairs={{0,4},{1,5},{2,6},{3,7},{4,0},{5,1},{6,2},{7,3},{8,12},{9,13},{10,... | collective-permute-start | bytes 6152 | tf_op jit(solution)/shard_map/ppermute | solution.py:48
  31.7 4.0 %collective-permute-done.1 = bf16[128,1024]{1,0:T(8,128)(2,1)} collective-permute-done((bf16[128,1024]{1,0:T(8,128)(2,1)S(1)}, bf16[128,1024]{1,0:T(8,128)(2,1)}, u32[]{:S(2)}, u32[]{:S(2)}) %collective-permute-start.1) | collective-permute-done | bytes 262176 | tf_op jit(solution)/shard_map/ppermute | solution.py:48
  38.2 5.4 %collective-permute-done.12 = s32[1,1,128]{2,1,0:T(1,128)S(1)} collective-permute-done((s32[1,1,128]{2,1,0:T(1,128)S(1)}, s32[1,1,128]{2,1,0:T(1,128)S(1)}, u32[]{:S(2)}, u32[]{:S(2)}) %collective-permute-start.12) | collective-permute-done | bytes 544 | tf_op jit(solution)/shard_map/ppermute | solution.py:48
  49.2 3.0 %fusion.14 = (f32[1024,128]{1,0:T(8,128)}, f32[1024,128]{1,0:T(8,128)}) fusion(f32[128]{0:T(128)S(1)} %get-tuple-element.169, f32[128]{0:T(128)S(1)} %get-tuple-element.170, f32[1024]{0:T(1024)S(1)} %bitcast.70), kind=kLoop, calls=%fused_computation.32 | loop fusion | flops 262144 | bytes 1053696 | tf_op jit(solution)/shard_map/mul | solution.py:513
  58.8 10.1 %shard_map.246 = (f32[1024,512]{1,0:T(8,128)}, bf16[1024,256]{1,0:T(8,128)(2,1)}, f32[512,1024]{1,0:T(8,128)}, bf16[128,1024]{1,0:T(8,128)(2,1)}, bf16[384,1024]{1,0:T(8,128)(2,1)}) custom-call(bf16[1024,1024]{1,0:T(8,128)(2,1)} %fusion.2.normed_ref, f32[1024,128]{1,0:T(8,128)} %get-tuple-element.156.cosine_ref.refs_10_, ...), custom_call_target="tpu_custom_call" | custom-call | flops 8000000000 | bytes 10488832 | tf_op jit(solution)/shard_map/pallas_call | solution.py:356
  80.7 5.0 %collective-permute-done.17 = bf16[128,1024]{1,0:T(8,128)(2,1)S(1)} collective-permute-done((bf16[128,1024]{1,0:T(8,128)(2,1)S(1)}, bf16[128,1024]{1,0:T(8,128)(2,1)S(1)}, u32[]{:S(2)}, u32[]{:S(2)}) %collective-permute-start.17) | collective-permute-done | bytes 262176 | tf_op jit(solution)/shard_map/ppermute | solution.py:48
  85.7 5.1 %collective-permute-done.18 = bf16[128,1024]{1,0:T(8,128)(2,1)S(1)} collective-permute-done((bf16[128,1024]{1,0:T(8,128)(2,1)S(1)}, bf16[128,1024]{1,0:T(8,128)(2,1)S(1)}, u32[]{:S(2)}, u32[]{:S(2)}) %collective-permute-start.18) | collective-permute-done | bytes 262176 | tf_op jit(solution)/shard_map/ppermute | solution.py:48
  93.3 3.6 %collective-permute-done.29 = bf16[128,1024]{1,0:T(8,128)(2,1)S(1)} collective-permute-done((bf16[128,1024]{1,0:T(8,128)(2,1)S(1)}, bf16[128,1024]{1,0:T(8,128)(2,1)S(1)}, u32[]{:S(2)}, u32[]{:S(2)}) %collective-permute-start.29) | collective-permute-done | bytes 262176 | tf_op jit(solution)/shard_map/ppermute | solution.py:48
  102.7 6.3 %collective-permute-done.21.refs_2_ = bf16[128,1024]{1,0:T(8,128)(2,1)} collective-permute-done((bf16[128,1024]{1,0:T(8,128)(2,1)S(1)}, bf16[128,1024]{1,0:T(8,128)(2,1)}, u32[]{:S(2)}, u32[]{:S(2)}) %collective-permute-start.21) | collective-permute-done | bytes 262176 | tf_op jit(solution)/shard_map/ppermute | solution.py:48
  111.2 11.0 %shard_map.247 = (bf16[1024,1024]{1,0:T(8,128)(2,1)}, bf16[1024,768]{1,0:T(8,128)(2,1)}, bf16[1024,384]{1,0:T(8,128)(2,1)}, f32[512,1024]{1,0:T(8,128)}, bf16[12...) custom-call(bf16[128,1024]{1,0:T(8,128)(2,1)} %copy-done.10, ...), custom_call_target="tpu_custom_call" | custom-call | flops 8000000000 | bytes 17301504 | tf_op jit(solution)/shard_map/pallas_call | solution.py:356
  122.7 3.2 %convolution_convert_fusion.2 = bf16[1024,384]{1,0:T(8,128)(2,1)S(1)} fusion(bf16[1024,1024]{1,0:T(8,128)(2,1)} %copy-done.15, bf16[1024,384]{1,0:T(8,128)(2,1)} %get-tuple-element.84), kind=kOutput, calls=%fused_computation.15 | convolution fusion | flops 805699584 | bytes 3670016 | tf_op jit(solution)/shard_map/dot_general | solution.py:35
  137.7 5.0 %collective-permute-done.37 = bf16[128,1024]{1,0:T(8,128)(2,1)S(1)} collective-permute-done((bf16[128,1024]{1,0:T(8,128)(2,1)S(1)}, bf16[128,1024]{1,0:T(8,128)(2,1)S(1)}, u32[]{:S(2)}, u32[]{:S(2)}) %collective-permute-start.37) | collective-permute-done | bytes 262176 | tf_op jit(solution)/shard_map/ppermute | solution.py:48
  142.7 4.7 %collective-permute-done.38 = bf16[128,1024]{1,0:T(8,128)(2,1)S(1)} collective-permute-done((bf16[128,1024]{1,0:T(8,128)(2,1)S(1)}, bf16[128,1024]{1,0:T(8,128)(2,1)S(1)}, u32[]{:S(2)}, u32[]{:S(2)}) %collective-permute-start.38) | collective-permute-done | bytes 262176 | tf_op jit(solution)/shard_map/ppermute | solution.py:48
  155.9 3.4 %collective-permute-done.46.refs_3_ = bf16[128,1024]{1,0:T(8,128)(2,1)S(1)} collective-permute-done((bf16[128,1024]{1,0:T(8,128)(2,1)S(1)}, bf16[128,1024]{1,0:T(8,128)(2,1)S(1)}, u32[]{:S(2)}, u32[]{:S(2)}) %collective-permute-start.46) | collective-permute-done | bytes 262176 | tf_op jit(solution)/shard_map/ppermute | solution.py:48
  159.3 4.7 %collective-permute-done.45.refs_2_ = bf16[128,1024]{1,0:T(8,128)(2,1)S(1)} collective-permute-done((bf16[128,1024]{1,0:T(8,128)(2,1)S(1)}, bf16[128,1024]{1,0:T(8,128)(2,1)S(1)}, u32[]{:S(2)}, u32[]{:S(2)}) %collective-permute-start.45) | collective-permute-done | bytes 262176 | tf_op jit(solution)/shard_map/ppermute | solution.py:48
  167.3 11.1 %shard_map.248 = (bf16[1024,1024]{1,0:T(8,128)(2,1)}, bf16[1024,512]{1,0:T(8,128)(2,1)}, f32[8,128]{1,0:T(8,128)}) custom-call(bf16[128,1024]{1,0:T(8,128)(2,1)} %copy-done.11, bf16[128,1024]{1,0:T(8,128)(2,1)} %copy-done.25, bf16[128,1024]{1,0:T(8,128)(2,1)} %copy-done.24, bf16[128,1024]{1,0:T(8,128)(2,1)} %copy-done.23, bf16[128,1024]{1,0:T(8,128)(2,1)} %copy-done.29, ...), custom_call_target="tpu_custom_call" | custom-call | flops 8000000000 | bytes 10492928 | tf_op jit(solution)/shard_map/pallas_call | solution.py:356
  189.0 3.0 %fusion.3 = (f32[1024]{0:T(1024)S(1)}, f32[1024,1024]{1,0:T(8,128)S(1)}) fusion(bf16[1024,1024]{1,0:T(8,128)(2,1)S(1)} %constant_dynamic-update-slice_fusion, f32[1024]{0:T(1024)S(1)} %add_rsqrt_fusion, bf16[1024,512]{1,0:T(8,128)(2,1)} %get-tuple-element.98, bf16[1024,768]{1,0:T(8,128)(2,1)} %all-gather.3.cloned.1.call-done.weights_ref.refs_12_), kind=kOutput, calls=%fused_computation.5 | convolution fusion | flops 1077935104 | bytes 8396800 | tf_op jit(solution)/shard_map/dot_general | solution.py:29
  196.3 3.4 %collective-permute-start.72 = (f32[24,128]{1,0:T(8,128)S(1)}, f32[24,128]{1,0:T(8,128)S(1)}, u32[]{:S(2)}, u32[]{:S(2)}) collective-permute-start(f32[24,128]{1,0:T(8,128)S(1)} %pad_maximum_fusion.4), channel_id=1, source_target_pairs={{0,6},{2,4},{4,2},{6,0},{1,7},{3,5},{5,3},{7,1},{8,14},{10,12},{12... | collective-permute-start | bytes 36872 | tf_op jit(solution)/shard_map/ppermute | solution.py:48
  213.6 6.9 %reduce-scatter.5.cloned.1.call-done = bf16[256,768]{1,0:T(8,128)(2,1)} async-done(((bf16[1024,768]{1,0:T(8,128)(2,1)}), bf16[256,768]{1,0:T(8,128)(2,1)}) %reduce-scatter.5.cloned.1.call-update) | async-done | bytes 393232 | tf_op jit(solution)/shard_map/reduce_scatter | solution.py:577
  232.7 9.9 %collective-permute-done.64.refs_2_ = bf16[128,768]{1,0:T(8,128)(2,1)} collective-permute-done((bf16[128,768]{1,0:T(8,128)(2,1)S(1)}, bf16[128,768]{1,0:T(8,128)(2,1)}, u32[]{:S(2)}, u32[]{:S(2)}) %collective-permute-start.64) | collective-permute-done | bytes 196640 | tf_op jit(solution)/shard_map/ppermute | solution.py:48
  247.7 4.0 %shard_map.250 = (f32[128,3072]{1,0:T(8,128)}, f32[128,3072]{1,0:T(8,128)}, f32[128,3072]{1,0:T(8,128)}) custom-call(s32[1]{0:T(128)} %bitcast.19.member_ref, bf16[128,1152]{1,0:T(8,128)(2,1)} %get-tuple-element.136.refs_0_, bf16[128,1152]{1,0:T(8,128)(2,1)} %collective-permute-done.51.refs_1_, bf16[128,1152]{1,0:T(8,128)(2,1)} %collective-permute-done.52.refs_2_, ...), custom_call_target="tpu_custom_call" | custom-call | tf_op jit(solution)/shard_map/pallas_call | solution.py:389
  254.2 3.4 %shard_map.249 = (f32[128,2048]{1,0:T(8,128)}, f32[128,1024]{1,0:T(8,128)}, f32[128,1024]{1,0:T(8,128)}, f32[128,2048]{1,0:T(8,128)}) custom-call(s32[1]{0:T(128)} %bitcast.19.member_ref, bf16[128,768]{1,0:T(8,128)(2,1)} %copy-done.9, bf16[128,768]{1,0:T(8,128)(2,1)} %copy-done.12, bf16[128,768]{1,0:T(8,128)(2,1)} %collective-permute-done.64.refs_2_, ...), custom_call_target="tpu_custom_call" | custom-call | tf_op jit(solution)/shard_map/pallas_call | solution.py:389
  262.0 4.7 %collective-permute-done.42 = bf16[128,1024]{1,0:T(8,128)(2,1)} collective-permute-done((bf16[128,1024]{1,0:T(8,128)(2,1)}, bf16[128,1024]{1,0:T(8,128)(2,1)}, u32[]{:S(2)}, u32[]{:S(2)}) %collective-permute-start.42) | collective-permute-done | bytes 262176 | tf_op jit(solution)/shard_map/ppermute | solution.py:48
  (303 shorter events, 134.3 us)
Async XLA Ops:
  7.2 51.6 %all-gather.3.cloned.1.call-start = ((), (), s32[]{:S(2)}) async-start(), calls=%async_computation.2 | async-start | bytes 1966080 | tf_op jit(solution)/shard_map/all_gather | solution.py:465
  18.0 92.9 %all-gather.5.cloned.1.call-start = ((), (), s32[]{:S(2)}) async-start(), calls=%async_computation.3 | async-start | bytes 2949120 | tf_op jit(solution)/shard_map/all_gather | solution.py:465
  29.7 14.0 %collective-permute-start.3 = (bf16[128,1024]{1,0:T(8,128)(2,1)S(1)}, bf16[128,1024]{1,0:T(8,128)(2,1)}, u32[]{:S(2)}, u32[]{:S(2)}) collective-permute-start(bf16[128,1024]{1,0:T(8,128)(2,1)S(1)} %bitcast.60), channel_id=1, source_target_pairs={{0,17},{1,16},{8,25},{9,24},{16,1},{17,0},{24,9},{25,8},{2,19},{3,... | collective-permute-start | bytes 786440 | tf_op jit(solution)/shard_map/ppermute | solution.py:48
  29.9 17.4 %collective-permute-start.4 = (bf16[128,1024]{1,0:T(8,128)(2,1)S(1)}, bf16[128,1024]{1,0:T(8,128)(2,1)S(1)}, u32[]{:S(2)}, u32[]{:S(2)}) collective-permute-start(bf16[128,1024]{1,0:T(8,128)(2,1)S(1)} %bitcast.61), channel_id=1, source_target_pairs={{0,8},{1,9},{8,0},{9,1},{16,24},{17,25},{24,16},{25,17},{2,10},{3,... | collective-permute-start | bytes 786440 | tf_op jit(solution)/shard_map/ppermute | solution.py:48
  29.9 22.3 %collective-permute-start.11 = (bf16[128,1152]{1,0:T(8,128)(2,1)S(1)}, bf16[128,1152]{1,0:T(8,128)(2,1)S(1)}, u32[]{:S(2)}, u32[]{:S(2)}) collective-permute-start(bf16[128,1152]{1,0:T(8,128)(2,1)S(1)} %pad_maximum_fusion.2), channel_id=1, source_target_pairs={{0,1},{1,0},{2,3},{3,2},{4,5},{5,4},{6,7},{7,6},{8,9},{9,8},{10,11... | collective-permute-start | bytes 884744 | tf_op jit(solution)/shard_map/ppermute | solution.py:48
  38.1 15.3 %collective-permute-start.5 = (bf16[128,1024]{1,0:T(8,128)(2,1)}, bf16[128,1024]{1,0:T(8,128)(2,1)}, u32[]{:S(2)}, u32[]{:S(2)}) collective-permute-start(bf16[128,1024]{1,0:T(8,128)(2,1)} %collective-permute-done.1), channel_id=1, source_target_pairs={{0,8},{1,9},{8,0},{9,1},{16,24},{17,25},{24,16},{25,17},{2,10},{3,... | collective-permute-start | bytes 786440 | tf_op jit(solution)/shard_map/ppermute | solution.py:48
  53.2 130.4 %reduce-scatter.3.cloned.1.call-start = ((), (), s32[]{:S(2)}) async-start(), calls=%async_computation.4 | async-start | bytes 2949120 | tf_op jit(solution)/shard_map/reduce_scatter | solution.py:577
  78.9 18.1 %collective-permute-start.29 = (bf16[128,1024]{1,0:T(8,128)(2,1)S(1)}, bf16[128,1024]{1,0:T(8,128)(2,1)S(1)}, u32[]{:S(2)}, u32[]{:S(2)}) collective-permute-start(bf16[128,1024]{1,0:T(8,128)(2,1)S(1)} %bitcast.65), channel_id=1, source_target_pairs={{0,17},{1,16},{8,25},{9,24},{16,1},{17,0},{24,9},{25,8},{2,19},{3,... | collective-permute-start | bytes 786440 | tf_op jit(solution)/shard_map/ppermute | solution.py:48
  80.6 17.8 %collective-permute-start.30 = (bf16[128,1024]{1,0:T(8,128)(2,1)S(1)}, bf16[128,1024]{1,0:T(8,128)(2,1)S(1)}, u32[]{:S(2)}, u32[]{:S(2)}) collective-permute-start(bf16[128,1024]{1,0:T(8,128)(2,1)S(1)} %bitcast.66), channel_id=1, source_target_pairs={{0,8},{1,9},{8,0},{9,1},{16,24},{17,25},{24,16},{25,17},{2,10},{3,... | collective-permute-start | bytes 786440 | tf_op jit(solution)/shard_map/ppermute | solution.py:48
  85.7 14.2 %collective-permute-start.31 = (bf16[128,1024]{1,0:T(8,128)(2,1)S(1)}, bf16[128,1024]{1,0:T(8,128)(2,1)S(1)}, u32[]{:S(2)}, u32[]{:S(2)}) collective-permute-start(bf16[128,1024]{1,0:T(8,128)(2,1)S(1)} %collective-permute-done.27), channel_id=1, source_target_pairs={{0,8},{1,9},{8,0},{9,1},{16,24},{17,25},{24,16},{25,17},{2,10},{3,... | collective-permute-start | bytes 786440 | tf_op jit(solution)/shard_map/ppermute | solution.py:48
  132.4 88.2 %reduce-scatter.5.cloned.1.call-start = ((), (), s32[]{:S(2)}) async-start(), calls=%async_computation.5 | async-start | bytes 1966080 | tf_op jit(solution)/shard_map/reduce_scatter | solution.py:577
  137.2 15.5 %collective-permute-start.40 = (bf16[128,1024]{1,0:T(8,128)(2,1)}, bf16[128,1024]{1,0:T(8,128)(2,1)S(1)}, u32[]{:S(2)}, u32[]{:S(2)}) collective-permute-start(bf16[128,1024]{1,0:T(8,128)(2,1)} %get-tuple-element.88), channel_id=1, source_target_pairs={{0,8},{1,9},{8,0},{9,1},{16,24},{17,25},{24,16},{25,17},{2,10},{3,... | collective-permute-start | bytes 786440 | tf_op jit(solution)/shard_map/ppermute | solution.py:48
  137.2 16.3 %collective-permute-start.36 = (bf16[384,1024]{1,0:T(8,128)(2,1)}, bf16[384,1024]{1,0:T(8,128)(2,1)S(1)}, u32[]{:S(2)}, u32[]{:S(2)}) collective-permute-start(bf16[384,1024]{1,0:T(8,128)(2,1)} %get-tuple-element.80), channel_id=1, source_target_pairs={{0,8},{1,9},{8,0},{9,1},{16,24},{17,25},{24,16},{25,17},{2,10},{3,... | collective-permute-start | bytes 2359304 | tf_op jit(solution)/shard_map/ppermute | solution.py:48
  185.5 18.2 %collective-permute-start.51 = (bf16[128,1152]{1,0:T(8,128)(2,1)S(1)}, bf16[128,1152]{1,0:T(8,128)(2,1)}, u32[]{:S(2)}, u32[]{:S(2)}) collective-permute-start(bf16[128,1152]{1,0:T(8,128)(2,1)S(1)} %get-tuple-element.135), channel_id=1, source_target_pairs={{0,1},{1,0},{8,9},{9,8},{16,17},{17,16},{24,25},{25,24},{2,3},{3,2... | collective-permute-start | bytes 884744 | tf_op jit(solution)/shard_map/ppermute | solution.py:48
  186.9 17.2 %collective-permute-start.52 = (bf16[128,1152]{1,0:T(8,128)(2,1)}, bf16[128,1152]{1,0:T(8,128)(2,1)}, u32[]{:S(2)}, u32[]{:S(2)}) collective-permute-start(bf16[128,1152]{1,0:T(8,128)(2,1)} %get-tuple-element.136.refs_0_), channel_id=1, source_target_pairs={{0,16},{1,17},{8,24},{9,25},{16,0},{17,1},{24,8},{25,9},{2,18},{3,... | collective-permute-start | bytes 884744 | tf_op jit(solution)/shard_map/ppermute | solution.py:48
  187.8 16.6 %collective-permute-start.53 = (bf16[128,1152]{1,0:T(8,128)(2,1)S(1)}, bf16[128,1152]{1,0:T(8,128)(2,1)}, u32[]{:S(2)}, u32[]{:S(2)}) collective-permute-start(bf16[128,1152]{1,0:T(8,128)(2,1)S(1)} %get-tuple-element.135), channel_id=1, source_target_pairs={{0,17},{1,16},{8,25},{9,24},{16,1},{17,0},{24,9},{25,8},{2,19},{3,... | collective-permute-start | bytes 884744 | tf_op jit(solution)/shard_map/ppermute | solution.py:48
  206.0 23.4 %collective-permute-start.54 = (bf16[384,1024]{1,0:T(8,128)(2,1)}, bf16[384,1024]{1,0:T(8,128)(2,1)}, u32[]{:S(2)}, u32[]{:S(2)}) collective-permute-start(bf16[384,1024]{1,0:T(8,128)(2,1)} %slice.141), channel_id=1, source_target_pairs={{0,8},{1,9},{8,0},{9,1},{16,24},{17,25},{24,16},{25,17},{2,10},{3,... | collective-permute-start | bytes 2359304 | tf_op jit(solution)/shard_map/ppermute | solution.py:48
  225.0 32.6 %collective-permute-start.56 = (bf16[128,1024]{1,0:T(8,128)(2,1)}, bf16[128,1024]{1,0:T(8,128)(2,1)S(1)}, u32[]{:S(2)}, u32[]{:S(2)}) collective-permute-start(bf16[128,1024]{1,0:T(8,128)(2,1)} %add_convert_fusion), channel_id=1, source_target_pairs={{0,17},{1,16},{8,25},{9,24},{16,1},{17,0},{24,9},{25,8},{2,19},{3,... | collective-permute-start | bytes 786440 | tf_op jit(solution)/shard_map/ppermute | solution.py:48
  226.5 17.1 %collective-permute-start.65 = (bf16[128,768]{1,0:T(8,128)(2,1)S(1)}, bf16[128,768]{1,0:T(8,128)(2,1)}, u32[]{:S(2)}, u32[]{:S(2)}) collective-permute-start(bf16[128,768]{1,0:T(8,128)(2,1)S(1)} %get-tuple-element.143), channel_id=1, source_target_pairs={{0,17},{1,16},{8,25},{9,24},{16,1},{17,0},{24,9},{25,8},{2,19},{3,... | collective-permute-start | bytes 589832 | tf_op jit(solution)/shard_map/ppermute | solution.py:48
  227.9 14.7 %collective-permute-start.64 = (bf16[128,768]{1,0:T(8,128)(2,1)S(1)}, bf16[128,768]{1,0:T(8,128)(2,1)}, u32[]{:S(2)}, u32[]{:S(2)}) collective-permute-start(bf16[128,768]{1,0:T(8,128)(2,1)S(1)} %get-tuple-element.144.refs_0_), channel_id=1, source_target_pairs={{0,16},{1,17},{8,24},{9,25},{16,0},{17,1},{24,8},{25,9},{2,18},{3,... | collective-permute-start | bytes 589832 | tf_op jit(solution)/shard_map/ppermute | solution.py:48
  229.4 16.4 %collective-permute-start.66 = (bf16[128,768]{1,0:T(8,128)(2,1)S(1)}, bf16[128,768]{1,0:T(8,128)(2,1)S(1)}, u32[]{:S(2)}, u32[]{:S(2)}) collective-permute-start(bf16[128,768]{1,0:T(8,128)(2,1)S(1)} %get-tuple-element.144.refs_0_), channel_id=1, source_target_pairs={{0,8},{1,9},{8,0},{9,1},{16,24},{17,25},{24,16},{25,17},{2,10},{3,... | collective-permute-start | bytes 589832 | tf_op jit(solution)/shard_map/ppermute | solution.py:48
  229.4 16.4 %collective-permute-start.67 = (bf16[128,768]{1,0:T(8,128)(2,1)S(1)}, bf16[128,768]{1,0:T(8,128)(2,1)S(1)}, u32[]{:S(2)}, u32[]{:S(2)}) collective-permute-start(bf16[128,768]{1,0:T(8,128)(2,1)S(1)} %collective-permute-done.63.refs_1_), channel_id=1, source_target_pairs={{0,8},{1,9},{8,0},{9,1},{16,24},{17,25},{24,16},{25,17},{2,10},{3,... | collective-permute-start | bytes 589832 | tf_op jit(solution)/shard_map/ppermute | solution.py:48
  242.6 16.1 %collective-permute-start.57 = (bf16[128,1024]{1,0:T(8,128)(2,1)}, bf16[128,1024]{1,0:T(8,128)(2,1)}, u32[]{:S(2)}, u32[]{:S(2)}) collective-permute-start(bf16[128,1024]{1,0:T(8,128)(2,1)} %get-tuple-element.121), channel_id=1, source_target_pairs={{0,16},{1,17},{8,24},{9,25},{16,0},{17,1},{24,8},{25,9},{2,18},{3,... | collective-permute-start | bytes 786440 | tf_op jit(solution)/shard_map/ppermute | solution.py:48
  243.6 15.1 %collective-permute-start.58 = (bf16[128,1024]{1,0:T(8,128)(2,1)}, bf16[128,1024]{1,0:T(8,128)(2,1)}, u32[]{:S(2)}, u32[]{:S(2)}) collective-permute-start(bf16[128,1024]{1,0:T(8,128)(2,1)} %get-tuple-element.122), channel_id=1, source_target_pairs={{0,1},{1,0},{8,9},{9,8},{16,17},{17,16},{24,25},{25,24},{2,3},{3,2... | collective-permute-start | bytes 786440 | tf_op jit(solution)/shard_map/ppermute | solution.py:48
  (90 other events, 701.9 us)
Sparse Core Ops, SparseCore 0:
  18.1 38.5 all-gather.2
  58.8 48.8 all-gather.4
  132.5 48.8 reduce-scatter.2
  184.2 36.3 reduce-scatter.4
